TPU v7x, 32 devices: a whole 2x2x4 slice. The times are simulated.
32 devices in a mesh: ctx: 16 (over z, y, core), tp: 2 (over x).
Axes of the slice: x: 2, y: 2, z: 4, core: 2. Of those that a mesh axis runs over, the one named last changes fastest.
Arguments:
- student_rows: bfloat16 [4096, 8192], P('ctx', 'tp'), may hold values from -3 to 3
- queries: bfloat16 [4096, 4096], P('ctx', 'tp'), may hold values from -5 to 5
- keys_values: bfloat16 [2, 4096, 512], P(None, 'ctx'), may hold values from -5 to 5
- out_weight: bfloat16 [4096, 8192], P(None, 'tp'), may hold values from -0.09375 to 0.09375
- teacher_rows: bfloat16 [6144, 8192], P('ctx', 'tp'), may hold values from -6 to 6
- span_start: int32 [4096], P('ctx'), may hold values from 0 to 6143, as said below
- span_len: int32 [4096], P('ctx'), may hold values from 1 to 4, as said below
Outputs:
- student_out: bfloat16 [4096, 8192], P('ctx', 'tp')
- teacher_grad: bfloat16 [6144, 8192], P('ctx', 'tp')
Inputs may be any that keep to these rules, and one draw needn't show every extreme that they name: Student token s of shard c = s // 256 pools teacher tokens span_start[s] to span_start[s] + span_len[s] - 1, all within 8 tokens of shard c's block of teacher tokens c * 384 to (c + 1) * 384 - 1. The first student token of every shard but the first starts exactly 8 tokens before that block. `span_len`: the last student token of every shard but the last ends exactly 8 tokens after its shard's block.
All inputs are finite; a program needn't handle non-finite values.
Results may differ from a plain program's by a relative error of at most 0.012.
Values may be sent and summed in bfloat16 or wider, within the bound.
No kernel may reach another device: no remote copies, remote signals or barrier semaphores. Data moves between devices by JAX's collectives and lax.ppermute only.
A program may use at most 192 MiB of HBM per device.

v0:
```python
import math

import jax
import jax.numpy as jnp
from jax import lax
from jax.sharding import PartitionSpec as P

HEADS = 32
KVH = 4
HD = 128
HALO = 8


floor_score = -1e30


def with_halo(array, sides, width):
    for axis, dim in sides:
        peers, length = (lax.axis_size(axis), array.shape[dim])
        up = [(i, (i + 1) % peers) for i in range(peers - 1)]
        down = [(j, i) for i, j in up]
        last = lax.slice_in_dim(array, length - width, length, axis=dim)
        leading = lax.slice_in_dim(array, 0, width, axis=dim)
        before = lax.ppermute(last, axis, up)
        after = lax.ppermute(leading, axis, down)
        array = jnp.concatenate([before, array, after], axis=dim)
    return array


def shifted(value, axis, steps):
    count = lax.axis_size(axis)
    leading, last = (max(0, -steps), min(count, count - steps))
    return lax.ppermute(value, axis, [(source, source + steps) for source in range(leading, last)])


def fresh_state(row_count, kv_count, per_kv, head_size):
    return (
        jnp.full((kv_count, per_kv, row_count), floor_score, jnp.float32),
        jnp.zeros((kv_count, per_kv, row_count), jnp.float32),
        jnp.zeros((kv_count, per_kv, row_count, head_size), jnp.float32),
    )


def attend(state, query_block, query_pos, key_rows, value_rows, key_pos):
    kv_count = query_block.shape[1]
    head_size = query_block.shape[3]
    score_scale = 1.0 / math.sqrt(head_size)
    key_heads = key_rows.reshape(key_rows.shape[0], kv_count, head_size)
    value_heads = value_rows.reshape(value_rows.shape[0], kv_count, head_size)

    def update(current):
        peak, total, accum = current
        scores = (
            jnp.einsum("rkgd,pkd->kgrp", query_block, key_heads, preferred_element_type=jnp.float32)
            * score_scale
        )
        visible = key_pos[None, :] <= query_pos[:, None]
        scores = jnp.where(visible, scores, floor_score)
        new_peak = jnp.maximum(peak, jnp.max(scores, axis=-1))
        weights = jnp.where(visible, jnp.exp(scores - new_peak[..., None]), 0.0)
        total = jnp.sum(weights, axis=-1)
        accum = jnp.einsum(
            "kgrp,pkd->kgrd",
            weights.astype(jnp.bfloat16),
            value_heads,
            preferred_element_type=jnp.float32,
        )
        return (new_peak, total, accum)

    def unchanged(current):
        return current

    return lax.cond(jnp.min(key_pos) > jnp.max(query_pos), unchanged, update, state)


def finish(state):
    peak, total, accum = state
    result = accum / total[..., None]
    return result.transpose(2, 0, 1, 3).reshape(result.shape[2], -1).astype(jnp.bfloat16)


def body(student_rows, queries, keys_values, out_weight, teacher_rows, span_start, span_len):
    ctx_rank = lax.axis_index("ctx")
    tp_lane = lax.axis_index("tp")
    rows_dev = student_rows.shape[0]
    teach_dev = teacher_rows.shape[0]
    heads_dev = queries.shape[1] // HD
    group_size = HEADS // KVH
    kv_dev = max(1, heads_dev // group_size)
    per_own = heads_dev // kv_dev
    extended = with_halo(teacher_rows, (("ctx", 0),), HALO)
    window = teach_dev + 2 * HALO
    columns = ctx_rank * teach_dev - HALO + jnp.arange(window)
    span_end = span_start + span_len
    member = (
        (columns[None, :] >= span_start[:, None]) & (columns[None, :] < span_end[:, None])
    ).astype(jnp.bfloat16)
    span_counts = span_len.astype(jnp.float32)[:, None]
    target = jnp.dot(member, extended, preferred_element_type=jnp.float32) / span_counts
    kv_first = tp_lane * heads_dev // group_size
    kv_own = lax.dynamic_slice_in_dim(keys_values, kv_first * HD, kv_dev * HD, 2)
    own_pos = ctx_rank * rows_dev + jnp.arange(rows_dev)
    block = queries.reshape(rows_dev, kv_dev, per_own, HD)
    initial = fresh_state(rows_dev, kv_dev, per_own, HD)
    piece = lax.all_gather(kv_own, "ctx", axis=1, tiled=True)
    key_pos = jnp.arange(piece.shape[1])
    state = attend(initial, block, own_pos, piece[0], piece[1], key_pos)
    attended = finish(state)
    projected = jnp.dot(
        lax.all_gather(attended, "tp", axis=1, tiled=True),
        out_weight,
        preferred_element_type=jnp.float32,
    )
    student32 = student_rows.astype(jnp.float32) + projected
    resid = student32 - target
    weighted = (resid / span_counts).astype(jnp.bfloat16)
    spread = lax.dot_general(
        member, weighted, (((0,), (0,)), ((), ())), preferred_element_type=jnp.float32
    )
    from_above = shifted(spread[:HALO].astype(jnp.bfloat16), "ctx", -1).astype(jnp.float32)
    from_below = shifted(spread[teach_dev + HALO :].astype(jnp.bfloat16), "ctx", 1).astype(
        jnp.float32
    )
    core = spread[HALO : HALO + teach_dev]
    core = core.at[teach_dev - HALO :].add(from_above)
    core = core.at[:HALO].add(from_below)
    return (student32.astype(jnp.bfloat16), core.astype(jnp.bfloat16))


def solution(mesh):
    return jax.shard_map(
        body,
        mesh=mesh,
        in_specs=(
            P("ctx", "tp"),
            P("ctx", "tp"),
            P(None, "ctx", None),
            P(None, "tp"),
            P("ctx", "tp"),
            P("ctx"),
            P("ctx"),
        ),
        out_specs=(P("ctx", "tp"), P("ctx", "tp")),
        check_vma=False,
    )
```

profile of v0, /device:TPU:8, one launch (start us, length us, event | category | flops | bytes accessed | tf_op | source)
XLA Modules:
  0.0 230.7 jit_solution(16554722170010180326)
XLA Ops:
  7.2 1.0 copy-done
  8.2 0.8 copy.27
  10.5 52.2 %all-gather.3.cloned.1.call-done = bf16[2,4096,256]{1,2,0:T(8,128)(2,1)} async-done(((bf16[2,256,256]{1,2,0:T(8,128)(2,1)}), bf16[2,4096,256]{1,2,0:T(8,128)(2,1)}) %all-gather.3.cloned.1.call-update) | async-done | bytes 4194320 | tf_op jit(solution)/shard_map/all_gather | solution.py:105
  62.7 83.2 %conditional.1 = (f32[2,8,256]{2,1,0:T(8,128)S(1)}, f32[2,8,256,128]{2,3,1,0:T(8,128)}) conditional(s32[]{:T(128)} %convert_element_type.40, (s32[4096]{0:T(1024)S(1)}, s32[256]{0:T(256)S(1)}, bf16[2,4096,256]{1,2,0:T(8,128)(2,1)}, bf16[256,2048]{1,0:T(8,128)(2,1)}) %tuple.24, () %tuple.25), branch_computations={%region_1.0_spmd, %region_4.5_spmd} | conditional | flops 8809082880 | bytes 227656752 | solution.py:73
  62.7 1.9 broadcast_compare_fusion
  64.6 4.8 %fusion.33 = (bf16[1,4096,256]{1,2,0:T(8,128)(2,1)}, bf16[1,4096,256]{1,2,0:T(8,128)(2,1)}) fusion(bf16[2,4096,256]{1,2,0:T(8,128)(2,1)} %get-tuple-element.40), kind=kLoop, calls=%fused_computation.39 | loop fusion | bytes 8388608 | tf_op jit(solution)/shard_map/slice | solution.py:107
  69.4 1.2 copy.28
  70.6 26.7 %fusion = (f32[2,8,256]{2,1,0:T(8,128)S(1)}, f32[2,4096,256,8]{2,1,3,0:T(8,128)}) fusion(pred[256,4096]{0,1:T(8,128)(4,1)S(1)} %broadcast_compare_fusion, bf16[4096,2,128,1]{0,2,3,1:T(8,128)(2,1)} %bitcast.33, bf16[256,2,8,128]{3,2,1,0:T(8,128)(2,1)} %bitcast.35), kind=kOutput, calls=%fused_computation.2 | convolution fusion | flops 4345294848 | bytes 71319552 | tf_op jit(solution)/shard_map/cond/branch_0_fun/rkgd,pkd->kgrp/dot_general | solution.py:54
  97.3 26.9 %fusion.3 = f32[2,8,256,128]{2,3,1,0:T(8,128)} fusion(bf16[4096,2,128,1]{0,2,3,1:T(8,128)(2,1)} %bitcast.32, f32[2,4096,256,8]{2,1,3,0:T(8,128)} %get-tuple-element.54, f32[2,8,256]{2,1,0:T(8,128)S(1)} %broadcast_maximum_fusion, pred[256,4096]{0,1:T(8,128)(4,1)S(1)} %broadcast_compare_fusion), kind=kOutput, calls=%fused_computation.5 | convolution fusion | flops 4378853376 | bytes 72368128 | tf_op jit(solution)/shard_map/cond | solution.py:73
  124.1 21.7 %fusion.2 = f32[2,8,256]{2,1,0:T(8,128)S(1)} fusion(f32[2,4096,256,8]{2,1,3,0:T(8,128)} %get-tuple-element.54, f32[2,8,256]{2,1,0:T(8,128)S(1)} %broadcast_maximum_fusion, pred[256,4096]{0,1:T(8,128)(4,1)S(1)} %broadcast_compare_fusion), kind=kLoop, calls=%fused_computation.4 | loop fusion | flops 83881984 | bytes 68190208 | tf_op jit(solution)/shard_map/cond/branch_0_fun/reduce_sum | solution.py:61
  145.9 2.9 %divide_convert_fusion = bf16[2,8,256,128]{2,3,1,0:T(8,128)(2,1)} fusion(f32[2,8,256,128]{2,3,1,0:T(8,128)} %get-tuple-element.50, f32[2,8,256]{2,1,0:T(8,128)S(1)} %get-tuple-element.47), kind=kLoop, calls=%fused_computation.24 | loop fusion | flops 1048576 | bytes 3162112 | tf_op jit(solution)/shard_map/convert_element_type | solution.py:79
  148.8 0.9 fusion.35
  149.7 2.2 collective-permute-start
  151.9 4.8 %collective-permute-start.1 = (bf16[8,4096]{1,0:T(8,128)(2,1)S(1)}, bf16[8,4096]{1,0:T(8,128)(2,1)S(1)}, u32[]{:S(2)}, u32[]{:S(2)}) collective-permute-start(bf16[8,4096]{1,0:T(8,128)(2,1)S(1)} %get-tuple-element.58), channel_id=1, source_target_pairs={{2,0},{4,2},{6,4},{8,6},{10,8},{12,10},{14,12},{16,14},{18,16},{20... | collective-permute-start | bytes 196616 | tf_op jit(solution)/shard_map/ppermute | solution.py:25
  156.8 25.2 %all-gather.5.cloned.1.call-done = bf16[256,4096]{0,1:T(8,128)(2,1)} async-done(((bf16[256,2048]{0,1:T(8,128)(2,1)}), bf16[256,4096]{0,1:T(8,128)(2,1)}) %all-gather.5.cloned.1.call-update) | async-done | bytes 2097168 | tf_op jit(solution)/shard_map/all_gather | solution.py:110
  182.0 17.3 %fusion.37 = (bf16[256,4096]{1,0:T(8,128)(2,1)}, f32[256,4096]{1,0:T(8,128)}) fusion(bf16[256,4096]{0,1:T(8,128)(2,1)} %all-gather.5.cloned.1.call-done, bf16[4096,4096]{1,0:T(8,128)(2,1)} %param.16, bf16[256,4096]{1,0:T(8,128)(2,1)S(1)} %copy-done.2), kind=kOutput, calls=%fused_computation.43 | convolution fusion | flops 8593080320 | bytes 44040192 | tf_op jit(solution)/shard_map/dot_general | solution.py:109
  199.3 9.3 %fusion.38 = (bf16[400,4096]{1,0:T(8,128)(2,1)}, f32[400,4096]{1,0:T(8,128)}) fusion(f32[256,4096]{1,0:T(8,128)} %get-tuple-element.62, bf16[8,4096]{1,0:T(8,128)(2,1)S(1)} %collective-permute-done.1, bf16[384,4096]{1,0:T(8,128)(2,1)} %param.17, bf16[8,4096]{1,0:T(8,128)(2,1)S(1)} %collective-permute-done, f32[256]{0:T(256)S(1)} %get-tuple-element.60, ...), kind=kOutput, calls=%fused_computation.44 | convolution fusion | flops 1693999104 | bytes 17306176 | tf_op jit(solution)/shard_map/dot_general | solution.py:117
  208.6 0.9 fusion.34
  209.5 2.6 %collective-permute-start.2 = (bf16[8,4096]{1,0:T(8,128)(2,1)S(1)}, bf16[8,4096]{1,0:T(8,128)(2,1)S(1)}, u32[]{:S(2)}, u32[]{:S(2)}) collective-permute-start(bf16[8,4096]{1,0:T(8,128)(2,1)S(1)} %get-tuple-element.56), channel_id=1, source_target_pairs={{2,0},{4,2},{6,4},{8,6},{10,8},{12,10},{14,12},{16,14},{18,16},{20... | collective-permute-start | bytes 196616 | tf_op jit(solution)/shard_map/ppermute | solution.py:33
  212.1 3.2 %slice.71 = f32[384,4096]{1,0:T(8,128)S(1)} slice(f32[400,4096]{1,0:T(8,128)} %get-tuple-element.64), slice={[8:392], [0:4096]} | slice | bytes 12582912 | tf_op jit(solution)/shard_map/slice | solution.py:124
  215.3 1.9 collective-permute-start.3
  217.2 0.9 fusion.29
  218.2 3.6 %collective-permute-done.3 = bf16[8,4096]{1,0:T(8,128)(2,1)S(1)} collective-permute-done((bf16[8,4096]{1,0:T(8,128)(2,1)S(1)}, bf16[8,4096]{1,0:T(8,128)(2,1)S(1)}, u32[]{:S(2)}, u32[]{:S(2)}) %collective-permute-start.3) | collective-permute-done | bytes 65568 | tf_op jit(solution)/shard_map/ppermute | solution.py:33
  221.8 2.1 convert_element_type.49
  (26 shorter events, 0.9 us)
Async XLA Ops:
  7.2 1.1 copy-start
  7.2 55.5 %all-gather.3.cloned.1.call-start = ((), (), s32[]{:S(2)}) async-start(), calls=%async_computation | async-start | bytes 4456448 | tf_op jit(solution)/shard_map/all_gather | solution.py:105
  9.1 172.9 %all-gather.5.cloned.1.call-start = ((), (), s32[]{:S(2)}) async-start(), calls=%async_computation.1 | async-start | bytes 3145728 | tf_op jit(solution)/shard_map/all_gather | solution.py:110
  64.5 4.8 %copy-start.3 = (bf16[256,2048]{1,0:T(8,128)(2,1)S(1)}, bf16[256,2048]{1,0:T(8,128)(2,1)}, u32[]{:S(2)}) copy-start(bf16[256,2048]{1,0:T(8,128)(2,1)} %get-tuple-element.49) | copy-start | bytes 3145732 | tf_op jit(solution)/shard_map/cond
  145.8 10.9 %copy-start.4 = (s32[256]{0:T(256)S(1)}, s32[256]{0:T(256)}, u32[]{:S(2)}) copy-start(s32[256]{0:T(256)} %param.19) | copy-start | bytes 3076
  145.9 10.9 %copy-start.5 = (s32[256]{0:T(256)S(1)}, s32[256]{0:T(256)}, u32[]{:S(2)}) copy-start(s32[256]{0:T(256)} %param.18) | copy-start | bytes 3076
  145.9 36.1 %copy-start.2 = (bf16[256,4096]{1,0:T(8,128)(2,1)S(1)}, bf16[256,4096]{1,0:T(8,128)(2,1)}, u32[]{:S(2)}) copy-start(bf16[256,4096]{1,0:T(8,128)(2,1)} %param.13) | copy-start | bytes 6291460
  149.7 49.6 %collective-permute-start = (bf16[8,4096]{1,0:T(8,128)(2,1)S(1)}, bf16[8,4096]{1,0:T(8,128)(2,1)S(1)}, u32[]{:S(2)}, u32[]{:S(2)}) collective-permute-start(bf16[8,4096]{1,0:T(8,128)(2,1)S(1)} %get-tuple-element.57), channel_id=1, source_target_pairs={{0,2},{2,4},{4,6},{6,8},{8,10},{10,12},{12,14},{14,16},{16,18},{18... | collective-permute-start | bytes 196616 | tf_op jit(solution)/shard_map/ppermute | solution.py:24
  151.9 47.4 %collective-permute-start.1 = (bf16[8,4096]{1,0:T(8,128)(2,1)S(1)}, bf16[8,4096]{1,0:T(8,128)(2,1)S(1)}, u32[]{:S(2)}, u32[]{:S(2)}) collective-permute-start(bf16[8,4096]{1,0:T(8,128)(2,1)S(1)} %get-tuple-element.58), channel_id=1, source_target_pairs={{2,0},{4,2},{6,4},{8,6},{10,8},{12,10},{14,12},{16,14},{18,16},{20... | collective-permute-start | bytes 196616 | tf_op jit(solution)/shard_map/ppermute | solution.py:25
  209.5 7.8 %collective-permute-start.2 = (bf16[8,4096]{1,0:T(8,128)(2,1)S(1)}, bf16[8,4096]{1,0:T(8,128)(2,1)S(1)}, u32[]{:S(2)}, u32[]{:S(2)}) collective-permute-start(bf16[8,4096]{1,0:T(8,128)(2,1)S(1)} %get-tuple-element.56), channel_id=1, source_target_pairs={{2,0},{4,2},{6,4},{8,6},{10,8},{12,10},{14,12},{16,14},{18,16},{20... | collective-permute-start | bytes 196616 | tf_op jit(solution)/shard_map/ppermute | solution.py:33
  215.3 6.5 %collective-permute-start.3 = (bf16[8,4096]{1,0:T(8,128)(2,1)S(1)}, bf16[8,4096]{1,0:T(8,128)(2,1)S(1)}, u32[]{:S(2)}, u32[]{:S(2)}) collective-permute-start(bf16[8,4096]{1,0:T(8,128)(2,1)S(1)} %get-tuple-element.55), channel_id=1, source_target_pairs={{0,2},{2,4},{4,6},{6,8},{8,10},{10,12},{12,14},{14,16},{16,18},{18... | collective-permute-start | bytes 196616 | tf_op jit(solution)/shard_map/ppermute | solution.py:33
  221.8 2.1 copy-start.1
Sparse Core Ops, SparseCore 0:
  10.7 51.9 all-gather.2
  148.9 32.9 all-gather.4
where the time goes:
time: 231 us
  waiting for transfers between devices  81.1 us (35%)
  matrix products  80.2 us (35%)
  other arithmetic  30.1 us (13%)
  between operations  14.9 us (6%)
  local copies, waits for them, and re-layouts  12.8 us (6%)
  starting transfers between devices  11.6 us (5%)
    all_gather x1, waiting for transfers between devices, body(): piece = lax.all_gather(kv_own, 'ctx', axis=1, tiled=True)  52.2 us
    cond x1, matrix products, attend(): lax.cond(jnp.min(key_pos) > jnp.max(query_pos), unchanged, update, state)  26.9 us
    dot_general x1, matrix products, update(): jnp.einsum('rkgd,pkd->kgrp', query_block, key_heads, preferred_element_ty...  26.7 us
    all_gather x1, waiting for transfers between devices, body(): lax.all_gather(attended, 'tp', axis=1, tiled=True)  25.2 us
    reduce_sum x1, other arithmetic, update(): total = jnp.sum(weights, axis=-1)  21.7 us
    dot_general x1, matrix products, body(): jnp.dot(lax.all_gather(attended, 'tp', axis=1, tiled=True), out_weight, p...  17.3 us
    dot_general x1, matrix products, body(): lax.dot_general(member, weighted, (((0,), (0,)), ((), ())), preferred_ele...  9.29 us
    ppermute x1, starting transfers between devices, with_halo(): after = lax.ppermute(leading, axis, down)  4.84 us
  transfers between devices with their start and end apart: 6, of which 3 were waited for; matrix products, arithmetic and copies ran while one was open for 10% of the time, Pallas kernels for 0%

commit v1 on v0

v1 whole, which is shorter than its diff:
```python
import functools
import math

import jax
import jax.numpy as jnp
from jax import lax
from jax.experimental import pallas as pl
from jax.experimental.pallas import tpu as pltpu
from jax.sharding import PartitionSpec as P


HEADS = 32
KVH = 4
HD = 128
HALO = 8
GROUP = 4

F32 = jnp.float32
BF16 = jnp.bfloat16
floor_score = -1e30
exp2_scale = math.log2(math.e) / math.sqrt(HD)

SPLIT = True
ATTN_VMEM = 8 * 1024 * 1024
PROJECT_VMEM = 20 * 1024 * 1024
FINISH_VMEM = 8 * 1024 * 1024


def shifted(value, axis, steps):
    count = lax.axis_size(axis)
    leading, last = (max(0, -steps), min(count, count - steps))
    return lax.ppermute(value, axis, [(source, source + steps) for source in range(leading, last)])


def swapped(value, axis, bit):
    count = lax.axis_size(axis)
    return lax.ppermute(value, axis, [(source, source ^ bit) for source in range(count)])


def attention_step(
    query_ref, heads, keys, values, state, hidden, diagonal, peak_ref, accum_ref
):
    rows = keys[0].shape[0]
    ones = jnp.ones((rows, HD), BF16)
    padded = [jnp.concatenate([block, ones], axis=1) for block in values]

    def product(head):
        query = query_ref[:, head * HD : (head + 1) * HD]
        return [
            lax.dot_general(query, block, (((1,), (1,)), ((), ())), preferred_element_type=F32)
            for block in keys
        ]

    scores = product(0)
    for head in range(heads):
        following = product(head + 1) if head + 1 < heads else None
        if diagonal is not None:
            scores[0] = jnp.where(diagonal, scores[0], floor_score)
        if hidden is None:
            top = functools.reduce(jnp.maximum, scores)
            top = jnp.max(top, axis=1, keepdims=True) * exp2_scale
        else:
            tops = [
                jnp.max(block, axis=1, keepdims=True) * exp2_scale - off
                for block, off in zip(scores, hidden)
            ]
            top = functools.reduce(jnp.maximum, tops)
        peak = top if state is None else jnp.maximum(state[head][0], top)
        accum = None if state is None else state[head][1][...] * jnp.exp2(state[head][0] - peak)
        for index, (block, value) in enumerate(zip(scores, padded)):
            shift = peak if hidden is None else peak + hidden[index]
            weights = jnp.exp2(block * exp2_scale - shift).astype(BF16)
            added = jnp.dot(weights, value, preferred_element_type=F32)
            accum = added if accum is None else accum + added
        peak_ref[:, head : head + 1] = peak
        accum_ref[head] = accum
        scores = following


def own_kernel(heads, query_ref, own_ref, side_ref, other_ref, peak_ref, accum_ref):
    rows = query_ref.shape[0]
    place = lax.rem(lax.axis_index("ctx"), GROUP)
    pieces = [own_ref, side_ref, other_ref.at[0], other_ref.at[1]]
    hidden = [0.0] + [
        jnp.where((place ^ flip) < place, 0.0, -floor_score).astype(F32) for flip in (2, 1, 3)
    ]
    diagonal = lax.broadcasted_iota(jnp.int32, (rows, rows), 1) <= lax.broadcasted_iota(
        jnp.int32, (rows, rows), 0
    )
    attention_step(
        query_ref,
        heads,
        [p[0] for p in pieces],
        [p[1] for p in pieces],
        None,
        hidden,
        diagonal,
        peak_ref,
        accum_ref,
    )


def more_kernel(heads, stages, last, query_ref, near_ref, far_ref, *refs):
    peak_in, accum_in = refs[:2]
    peak_ref, accum_ref = refs[-2:]
    out_ref = refs[2]
    for head in range(heads):
        accum_ref[head] = accum_in[head]
    peak_ref[...] = peak_in[...]
    group = lax.div(lax.axis_index("ctx"), GROUP)
    count = len(stages)

    def step(index, carry):
        @pl.when((group ^ (index + stages[0])) < group)
        def _():
            pieces = [ref.at[at] for ref in (near_ref, far_ref) for at in (index, index + count)]
            state = [(peak_ref[:, head : head + 1], accum_ref.at[head]) for head in range(heads)]
            attention_step(
                query_ref,
                heads,
                [p[0] for p in pieces],
                [p[1] for p in pieces],
                state,
                None,
                None,
                peak_ref,
                accum_ref,
            )

        return carry

    lax.fori_loop(0, count, step, 0)
    if last:
        for head in range(heads):
            accum = accum_ref[head]
            out_ref[:, head * HD : (head + 1) * HD] = (accum[:, :HD] / accum[:, HD:]).astype(BF16)


VMEM_SPEC = pl.BlockSpec(memory_space=pltpu.VMEM)
HBM_SPEC = pl.BlockSpec(memory_space=pltpu.HBM)
MIB = 1024 * 1024


def attention_cost(rows, heads, keys):
    return pl.CostEstimate(
        flops=4 * rows * heads * keys * HD * 2,
        transcendentals=rows * heads * keys,
        bytes_accessed=2 * MIB,
    )


def state_shapes(rows, heads):
    return [((rows, HD), F32), ((heads, rows, 2 * HD), F32)]


def query_spec(rows, heads, kv):
    return pl.BlockSpec((rows, heads * HD), lambda i: (0, kv))


def attend_own(queries, kv, heads, own, side, other):
    rows = queries.shape[0]
    return pl.pallas_call(
        functools.partial(own_kernel, heads),
        grid=(1,),
        in_specs=[query_spec(rows, heads, kv)] + [VMEM_SPEC] * 3,
        out_specs=[VMEM_SPEC] * 2,
        out_shape=[jax.ShapeDtypeStruct(*shape) for shape in state_shapes(rows, heads)],
        compiler_params=pltpu.CompilerParams(vmem_limit_bytes=ATTN_VMEM),
        cost_estimate=attention_cost(rows, heads, GROUP * rows),
        name="attend_own",
    )(queries, own, side, other)


def attend_more(queries, kv, heads, stages, last, near, far, state):
    rows = queries.shape[0]
    states = state_shapes(rows, heads)
    result = [((rows, heads * HD), BF16)] if last else states
    return pl.pallas_call(
        functools.partial(more_kernel, heads, stages, last),
        grid=(1,),
        in_specs=[query_spec(rows, heads, kv)] + [VMEM_SPEC] * 4,
        out_specs=[VMEM_SPEC] * len(result),
        out_shape=[jax.ShapeDtypeStruct(*shape) for shape in result],
        scratch_shapes=[pltpu.VMEM(*shape) for shape in states] if last else [],
        compiler_params=pltpu.CompilerParams(vmem_limit_bytes=ATTN_VMEM),
        cost_estimate=attention_cost(rows, heads, 2 * near.shape[0] * rows),
        name="attend_last" if last else "attend_more",
    )(queries, near, far, *state)


def upright(row):
    count = row.shape[1]
    same = iota((count, count), 0) == iota((count, count), 1)
    return jnp.sum(jnp.where(same, row, 0), axis=1, keepdims=True)


def member_of(starts, lens, columns):
    return ((columns >= starts) & (columns < starts + lens)).astype(F32).astype(BF16)


def iota(shape, axis):
    return lax.broadcasted_iota(jnp.int32, shape, axis)


def rim_rows(index, teach):
    return jnp.where(index < HALO, index - HALO, index - HALO + teach)


def base_kernel(count, cols, slots, tp_count, start_ref, len_ref, student_ref, teacher_ref, halo_ref, *refs):
    piece_refs = refs[:count]
    weight_hbm, base_ref, target_ref, last_ref, buf, sems, last_sem = refs[count:]
    rows, width = student_ref.shape
    teach = teacher_ref.shape[0]
    depth = piece_refs[0].shape[1]
    steps = width // cols

    own = (count + 1) // tp_count

    def block(index):
        lane = lax.rem(lax.axis_index("tp") + tp_count - index // own, tp_count)
        return pl.ds(pl.multiple_of((lane * own + index % own) * depth, depth), depth)

    def loads(step):
        slot = step % slots
        return [
            pltpu.make_async_copy(
                weight_hbm.at[block(index), pl.ds(step * cols, cols)],
                buf.at[slot, index],
                sems.at[slot, index],
            )
            for index in range(count)
        ]

    tail = pltpu.make_async_copy(weight_hbm.at[block(count), :], last_ref, last_sem)
    for step in range(min(slots, steps)):
        for load in loads(step):
            load.start()
    if steps <= slots:
        tail.start()
    starts = upright(start_ref[...]) - lax.axis_index("ctx") * teach
    lens = upright(len_ref[...])
    inner = member_of(starts, lens, iota((rows, teach), 1))
    outer = member_of(starts, lens, rim_rows(iota((rows, 2 * HALO), 1), teach))
    counts = lens.astype(F32)
    for step in range(steps):
        span = slice(step * cols, (step + 1) * cols)
        target = jnp.dot(inner, teacher_ref[:, span], preferred_element_type=F32)
        target += jnp.dot(outer, halo_ref[:, span], preferred_element_type=F32)
        target_ref[:, span] = target / counts
        for load in loads(step):
            load.wait()
        total = student_ref[:, span].astype(F32)
        for index in range(count):
            total += jnp.dot(
                piece_refs[index][...], buf[step % slots, index], preferred_element_type=F32
            )
        base_ref[:, span] = total
        if step + slots < steps:
            for load in loads(step + slots):
                load.start()
            if step + slots == steps - 1:
                tail.start()
    tail.wait()


def project_base(tp_count, starts, lens, student, teacher, halo, pieces, out_weight):
    rows, width = student.shape
    count, depth = len(pieces), pieces[0].shape[1]
    cols, slots = min(512, width), 4
    return pl.pallas_call(
        functools.partial(base_kernel, count, cols, slots, tp_count),
        in_specs=[VMEM_SPEC] * (count + 5) + [HBM_SPEC],
        out_specs=[VMEM_SPEC] * 3,
        out_shape=[jax.ShapeDtypeStruct((rows, width), F32)] * 2
        + [pltpu.VMEM((depth, width), BF16)],
        scratch_shapes=[
            pltpu.VMEM((slots, count, depth, cols), BF16),
            pltpu.SemaphoreType.DMA((slots, count)),
            pltpu.SemaphoreType.DMA,
        ],
        compiler_params=pltpu.CompilerParams(vmem_limit_bytes=PROJECT_VMEM),
        cost_estimate=pl.CostEstimate(
            flops=2 * rows * width * (depth * count + teacher.shape[0]),
            transcendentals=0,
            bytes_accessed=2 * depth * count * width + 10 * rows * width,
        ),
        name="project_base",
    )(starts[None, :], lens[None, :], student, teacher, halo, *pieces, out_weight)


def final_kernel(count, cols, start_ref, len_ref, base_ref, target_ref, *refs):
    piece_refs, weight_refs = refs[:count], refs[count : 2 * count]
    student_out, core_out, edge_ref, rim_ref, student_buf, core_buf, sems = refs[2 * count :]
    rows, width = base_ref.shape
    teach = core_buf.shape[0]
    starts, lens = start_ref[...] - lax.axis_index("ctx") * teach, len_ref[...]
    inner_t = member_of(starts, lens, iota((teach, rows), 0))
    outer_t = member_of(starts, lens, rim_rows(iota((2 * HALO, rows), 0), teach))
    counts = upright(lens).astype(F32)
    copies = []
    for index, start in enumerate(range(0, width, cols)):
        span = slice(start, start + cols)
        total = base_ref[:, span]
        for piece in range(count):
            total += jnp.dot(
                piece_refs[piece][...], weight_refs[piece][:, span], preferred_element_type=F32
            )
        student_buf[:, span] = total.astype(BF16)
        weighted = ((total - target_ref[:, span]) / counts).astype(BF16)
        edge = jnp.dot(outer_t, weighted, preferred_element_type=F32)
        edge_ref[:, span] = edge.astype(BF16)
        core = jnp.dot(inner_t, weighted, preferred_element_type=F32)
        core_buf[:, span] = core.astype(BF16)
        rim_ref[:HALO, span] = core[:HALO]
        rim_ref[HALO:, span] = core[teach - HALO :]
        for slot, (source, result) in enumerate(((student_buf, student_out), (core_buf, core_out))):
            copy = pltpu.make_async_copy(
                source.at[:, span], result.at[:, span], sems.at[slot, index]
            )
            copy.start()
            copies.append(copy)
    for copy in copies:
        copy.wait()


def finish(starts, lens, base, target, teach, pieces, weights):
    rows, width = base.shape
    count, depth = len(pieces), pieces[0].shape[1]
    cols = min(512, width)
    return pl.pallas_call(
        functools.partial(final_kernel, count, cols),
        in_specs=[VMEM_SPEC] * (4 + 2 * count),
        out_specs=[HBM_SPEC, HBM_SPEC, VMEM_SPEC, VMEM_SPEC],
        scratch_shapes=[
            pltpu.VMEM((rows, width), BF16),
            pltpu.VMEM((teach, width), BF16),
            pltpu.SemaphoreType.DMA((2, width // cols)),
        ],
        out_shape=[
            jax.ShapeDtypeStruct((rows, width), BF16),
            jax.ShapeDtypeStruct((teach, width), BF16),
            jax.ShapeDtypeStruct((2 * HALO, width), BF16),
            jax.ShapeDtypeStruct((2 * HALO, width), F32),
        ],
        compiler_params=pltpu.CompilerParams(vmem_limit_bytes=FINISH_VMEM),
        cost_estimate=pl.CostEstimate(
            flops=2 * rows * width * (depth * count + teach),
            transcendentals=0,
            bytes_accessed=2 * depth * count * width + 10 * rows * width + 2 * teach * width,
        ),
        name="finish",
    )(starts[None, :], lens[None, :], base, target, *pieces, *weights)


def rim_kernel(core_ref, rim_ref, below_ref, above_ref, out_ref):
    block = core_ref[...].astype(F32)

    @pl.when(pl.program_id(0) == 0)
    def _():
        first = rim_ref[:HALO] + below_ref[...].astype(F32)
        out_ref[...] = jnp.concatenate([first, block[HALO:]], axis=0).astype(BF16)

    @pl.when(pl.program_id(0) == 1)
    def _():
        last = rim_ref[HALO:] + above_ref[...].astype(F32)
        out_ref[...] = jnp.concatenate([block[:HALO], last], axis=0).astype(BF16)


def add_rim(core, rim, below, above):
    teach, width = core.shape
    end = teach // (2 * HALO) - 1
    place = pl.BlockSpec((2 * HALO, width), lambda i: (i * end, 0))
    return pl.pallas_call(
        rim_kernel,
        grid=(2,),
        in_specs=[place] + [pl.BlockSpec((n, width), lambda i: (0, 0)) for n in (2 * HALO, HALO, HALO)],
        out_specs=place,
        out_shape=jax.ShapeDtypeStruct(core.shape, core.dtype),
        input_output_aliases={0: 0},
        compiler_params=pltpu.CompilerParams(vmem_limit_bytes=4 * MIB),
        name="add_rim",
    )(core, rim, below, above)


def body(student_rows, queries, keys_values, out_weight, teacher_rows, span_start, span_len):
    ctx_count = lax.axis_size("ctx")
    tp_lane = lax.axis_index("tp")
    tp_count = lax.axis_size("tp")
    teach_dev = teacher_rows.shape[0]
    heads_dev = queries.shape[1] // HD
    group_size = HEADS // KVH
    kv_dev = max(1, heads_dev // group_size)
    per_own = heads_dev // kv_dev
    groups = ctx_count // GROUP
    kv_first = tp_lane * heads_dev // group_size

    owns = [
        lax.dynamic_slice_in_dim(keys_values, (kv_first + kv) * HD, HD, 2) for kv in range(kv_dev)
    ]
    both = jnp.stack(owns)
    side_all = swapped(both, "ctx", 2)
    other_all = swapped(jnp.stack([both, side_all], axis=1), "ctx", 1)
    before = shifted(teacher_rows[teach_dev - HALO :], "ctx", 1)
    after = shifted(teacher_rows[:HALO], "ctx", -1)
    halo = jnp.concatenate([before, after], axis=0)

    plan = [list(range(1, groups - 1)), [groups - 1]] if SPLIT else [list(range(1, groups))]
    out_weight = pltpu.with_memory_space_constraint(out_weight, pltpu.HBM)
    attended = []
    for kv in range(kv_dev):
        lifts = []
        for step in range(1, groups):
            lifts.append(swapped(owns[kv], "ctx", GROUP * step))
        state = attend_own(queries, kv, per_own, owns[kv], side_all[kv], other_all[kv])
        for turn, stages in enumerate(plan):
            straight = jnp.stack([lifts[step - 1] for step in stages])
            crossed = swapped(straight, "ctx", 2)
            near = jnp.concatenate([straight, crossed])
            far = swapped(near, "ctx", 1)
            last = turn == len(plan) - 1
            state = attend_more(queries, kv, per_own, stages, last, near, far, state)
        attended.append(state[0])

    pieces = list(attended)
    for step in range(1, tp_count):
        ring = [(i, (i + step) % tp_count) for i in range(tp_count)]
        for kv in range(kv_dev):
            pieces.append(lax.ppermute(attended[kv], "tp", ring))
    base, target, weight = project_base(
        tp_count, span_start, span_len, student_rows, teacher_rows, halo, pieces[:-1], out_weight
    )
    student_out, core, edge, rim = finish(
        span_start, span_len, base, target, teach_dev, pieces[-1:], [weight]
    )
    above = shifted(edge[:HALO], "ctx", -1)
    below = shifted(edge[HALO:], "ctx", 1)
    return (student_out, add_rim(core, rim, below, above))


def solution(mesh):
    return jax.shard_map(
        body,
        mesh=mesh,
        in_specs=(
            P("ctx", "tp"),
            P("ctx", "tp"),
            P(None, "ctx", None),
            P(None, "tp"),
            P("ctx", "tp"),
            P("ctx"),
            P("ctx"),
        ),
        out_specs=(P("ctx", "tp"), P("ctx", "tp")),
        check_vma=False,
    )
```

time: 231 us -> 105 us (0.45)
  the two profiles are of different devices: /device:TPU:8 before, /device:TPU:24 now
where the time goes in v1:
time: 105 us
  Pallas kernels  45.5 us (43%)
  starting transfers between devices  31.9 us (30%)
  waiting for transfers between devices  24.2 us (23%)
  local copies, waits for them, and re-layouts  1.97 us (2%)
    pallas_call x4, Pallas kernels, attend_more(): pl.pallas_call(functools.partial(more_kernel, heads, stages, last), grid=...  21.5 us
    ppermute x16, starting transfers between devices, swapped(): lax.ppermute(value, axis, [(source, source ^ bit) for source in range(cou...  19 us
    ppermute x16, waiting for transfers between devices, swapped(): lax.ppermute(value, axis, [(source, source ^ bit) for source in range(cou...  16.6 us
    pallas_call x1, Pallas kernels, project_base(): pl.pallas_call(functools.partial(base_kernel, count, cols, slots, tp_coun...  11.3 us
    ppermute x4, starting transfers between devices, shifted(): lax.ppermute(value, axis, [(source, source + steps) for source in range(l...  10.8 us
    ppermute x4, waiting for transfers between devices, shifted(): lax.ppermute(value, axis, [(source, source + steps) for source in range(l...  5.86 us
    pallas_call x1, Pallas kernels, finish(): pl.pallas_call(functools.partial(final_kernel, count, cols), in_specs=[VM...  5.54 us
    pallas_call x2, Pallas kernels, attend_own(): pl.pallas_call(functools.partial(own_kernel, heads), grid=(1,), in_specs=...  5.51 us
  transfers between devices with their start and end apart: 22, of which 8 were waited for; matrix products, arithmetic and copies ran while one was open for 1% of the time, Pallas kernels for 37%

profile of v1, /device:TPU:24, one launch (start us, length us, event | category | flops | bytes accessed | tf_op | source)
XLA Modules:
  0.0 104.9 jit_solution(3240349415127107065)
XLA Ops:
  2.2 3.9 %collective-permute-start.11 = (bf16[2,256,128]{2,1,0:T(8,128)(2,1)S(1)}, bf16[2,256,128]{2,1,0:T(8,128)(2,1)S(1)}, u32[]{:S(2)}, u32[]{:S(2)}) collective-permute-start(bf16[2,256,128]{2,1,0:T(8,128)(2,1)S(1)} %get-tuple-element.36.own_ref), channel_id=1, source_target_pairs={{0,24},{2,26},{4,28},{6,30},{8,16},{10,18},{12,20},{14,22},{16,8},... | collective-permute-start | bytes 393224 | tf_op jit(solution)/shard_map/ppermute | solution.py:37
  7.0 1.9 %collective-permute-start = (bf16[8,4096]{1,0:T(8,128)(2,1)S(1)}, bf16[8,4096]{1,0:T(8,128)(2,1)S(1)}, u32[]{:S(2)}, u32[]{:S(2)}) collective-permute-start(bf16[8,4096]{1,0:T(8,128)(2,1)S(1)} %get-tuple-element.32), channel_id=1, source_target_pairs={{0,2},{2,4},{4,6},{6,8},{8,10},{10,12},{12,14},{14,16},{16,18},{18... | collective-permute-start | bytes 196616 | tf_op jit(solution)/shard_map/ppermute | solution.py:32
  8.9 4.5 %collective-permute-start.1 = (bf16[8,4096]{1,0:T(8,128)(2,1)S(1)}, bf16[8,4096]{1,0:T(8,128)(2,1)S(1)}, u32[]{:S(2)}, u32[]{:S(2)}) collective-permute-start(bf16[8,4096]{1,0:T(8,128)(2,1)S(1)} %get-tuple-element.33), channel_id=1, source_target_pairs={{2,0},{4,2},{6,4},{8,6},{10,8},{12,10},{14,12},{16,14},{18,16},{20... | collective-permute-start | bytes 196616 | tf_op jit(solution)/shard_map/ppermute | solution.py:32
  13.5 1.6 %collective-permute-done = bf16[8,4096]{1,0:T(8,128)(2,1)S(1)} collective-permute-done((bf16[8,4096]{1,0:T(8,128)(2,1)S(1)}, bf16[8,4096]{1,0:T(8,128)(2,1)S(1)}, u32[]{:S(2)}, u32[]{:S(2)}) %collective-permute-start) | collective-permute-done | bytes 65568 | tf_op jit(solution)/shard_map/ppermute | solution.py:32
  15.4 6.5 %collective-permute-start.5 = (bf16[2,256,128]{2,1,0:T(8,128)(2,1)S(1)}, bf16[2,256,128]{2,1,0:T(8,128)(2,1)S(1)}, u32[]{:S(2)}, u32[]{:S(2)}) collective-permute-start(bf16[2,256,128]{2,1,0:T(8,128)(2,1)S(1)} %get-tuple-element.37.own_ref), channel_id=1, source_target_pairs={{0,8},{2,10},{4,12},{6,14},{8,0},{10,2},{12,4},{14,6},{16,24},{18,... | collective-permute-start | bytes 393224 | tf_op jit(solution)/shard_map/ppermute | solution.py:37
  21.8 2.4 %collective-permute-start.2 = (bf16[2,256,128]{2,1,0:T(8,128)(2,1)S(1)}, bf16[2,256,128]{2,1,0:T(8,128)(2,1)S(1)}, u32[]{:S(2)}, u32[]{:S(2)}) collective-permute-start(bf16[2,256,128]{2,1,0:T(8,128)(2,1)S(1)} %get-tuple-element.37.own_ref), channel_id=1, source_target_pairs={{0,24},{2,26},{4,28},{6,30},{8,16},{10,18},{12,20},{14,22},{16,8},... | collective-permute-start | bytes 393224 | tf_op jit(solution)/shard_map/ppermute | solution.py:37
  24.4 2.0 %collective-permute-start.12 = (bf16[1,2,256,128]{3,2,1,0:T(8,128)(2,1)S(1)}, bf16[1,2,256,128]{3,2,1,0:T(8,128)(2,1)S(1)}, u32[]{:S(2)}, u32[]{:S(2)}) collective-permute-start(bf16[1,2,256,128]{3,2,1,0:T(8,128)(2,1)S(1)} %bitcast.38), channel_id=1, source_target_pairs={{0,4},{2,6},{4,0},{6,2},{8,12},{10,14},{12,8},{14,10},{16,20},{18,... | collective-permute-start | bytes 393224 | tf_op jit(solution)/shard_map/ppermute | solution.py:37
  26.4 3.6 %collective-permute-done.2 = bf16[2,256,128]{2,1,0:T(8,128)(2,1)S(1)} collective-permute-done((bf16[2,256,128]{2,1,0:T(8,128)(2,1)S(1)}, bf16[2,256,128]{2,1,0:T(8,128)(2,1)S(1)}, u32[]{:S(2)}, u32[]{:S(2)}) %collective-permute-start.2) | collective-permute-done | bytes 131104 | tf_op jit(solution)/shard_map/ppermute | solution.py:37
  30.0 2.1 %collective-permute-start.16 = (bf16[2,2,256,128]{3,2,1,0:T(8,128)(2,1)S(1)}, bf16[2,2,256,128]{3,2,1,0:T(8,128)(2,1)S(1)}, u32[]{:S(2)}, u32[]{:S(2)}) collective-permute-start(bf16[2,2,256,128]{3,2,1,0:T(8,128)(2,1)S(1)} %pad_maximum_fusion.7), channel_id=1, source_target_pairs={{0,4},{2,6},{4,0},{6,2},{8,12},{10,14},{12,8},{14,10},{16,20},{18,... | collective-permute-start | bytes 786440 | tf_op jit(solution)/shard_map/ppermute | solution.py:37
  32.2 6.9 %collective-permute-done.3 = bf16[1,2,256,128]{3,2,1,0:T(8,128)(2,1)S(1)} collective-permute-done((bf16[1,2,256,128]{3,2,1,0:T(8,128)(2,1)S(1)}, bf16[1,2,256,128]{3,2,1,0:T(8,128)(2,1)S(1)}, u32[]{:S(2)}, u32[]{:S(2)}) %collective-permute-start.3) | collective-permute-done | bytes 131104 | tf_op jit(solution)/shard_map/ppermute | solution.py:37
  40.0 6.1 %collective-permute-done.7 = bf16[2,2,256,128]{3,2,1,0:T(8,128)(2,1)S(1)} collective-permute-done((bf16[2,2,256,128]{3,2,1,0:T(8,128)(2,1)S(1)}, bf16[2,2,256,128]{3,2,1,0:T(8,128)(2,1)S(1)}, u32[]{:S(2)}, u32[]{:S(2)}) %collective-permute-start.7) | collective-permute-done | bytes 262176 | tf_op jit(solution)/shard_map/ppermute | solution.py:37
  46.9 2.8 %attend_own.3 = (f32[256,128]{1,0:T(8,128)S(1)}, f32[8,256,256]{2,1,0:T(8,128)S(1)}) custom-call(bf16[256,2048]{1,0:T(8,128)(2,1)S(1)} %copy-done.4, bf16[2,256,128]{2,1,0:T(8,128)(2,1)S(1)} %get-tuple-element.36.own_ref, bf16[2,256,128]{2,1,0:T(8,128)(2,1)S(1)} %get-tuple-element.38.side_ref, bf16[2,2,256,128]{3,2,1,0:T(8,128)(2,1)S(1)} %get-tuple-element.34.other_ref), custom_call_target="tpu_custom_call" | custom-call | flops 2147483648 | bytes 2097152 | tf_op jit(solution)/shard_map/attend_own/pallas_call | solution.py:162
  49.7 2.8 %attend_own.2 = (f32[256,128]{1,0:T(8,128)S(1)}, f32[8,256,256]{2,1,0:T(8,128)S(1)}) custom-call(bf16[256,2048]{1,0:T(8,128)(2,1)S(1)} %copy-done.4, bf16[2,256,128]{2,1,0:T(8,128)(2,1)S(1)} %get-tuple-element.37.own_ref, bf16[2,256,128]{2,1,0:T(8,128)(2,1)S(1)} %get-tuple-element.39.side_ref, bf16[2,2,256,128]{3,2,1,0:T(8,128)(2,1)S(1)} %get-tuple-element.35.other_ref), custom_call_target="tpu_custom_call" | custom-call | flops 2147483648 | bytes 2097152 | tf_op jit(solution)/shard_map/attend_own/pallas_call | solution.py:162
  52.4 6.9 %attend_more.2 = (f32[256,128]{1,0:T(8,128)S(1)}, f32[8,256,256]{2,1,0:T(8,128)S(1)}) custom-call(bf16[256,2048]{1,0:T(8,128)(2,1)S(1)} %copy-done.4, bf16[4,2,256,128]{3,2,1,0:T(8,128)(2,1)S(1)} %pad_maximum_fusion.near_ref, bf16[4,2,256,128]{3,2,1,0:T(8,128)(2,1)S(1)} %collective-permute-done.8.far_ref, f32[256,128]{1,0:T(8,128)S(1)} %get-tuple-element.17.refs_0_, ...), custom_call_target="tpu_custom_call" | custom-call | flops 4294967296 | bytes 2097152 | tf_op jit(solution)/shard_map/attend_more/pallas_call | solution.py:178
  59.3 3.8 %attend_last.2.refs_0_ = bf16[256,1024]{1,0:T(8,128)(2,1)S(1)} custom-call(bf16[256,2048]{1,0:T(8,128)(2,1)S(1)} %copy-done.4, bf16[2,2,256,128]{3,2,1,0:T(8,128)(2,1)S(1)} %pad_maximum_fusion.3.near_ref, bf16[2,2,256,128]{3,2,1,0:T(8,128)(2,1)S(1)} %collective-permute-done.4.far_ref, f32[256,128]{1,0:T(8,128)S(1)} %get-tuple-element.19.refs_0_, ...), custom_call_target="tpu_custom_call" | custom-call | flops 2147483648 | bytes 2097152 | tf_op jit(solution)/shard_map/attend_last/pallas_call | solution.py:178
  63.2 1.6 %collective-permute-start.18 = (bf16[256,1024]{1,0:T(8,128)(2,1)S(1)}, bf16[256,1024]{1,0:T(8,128)(2,1)S(1)}, u32[]{:S(2)}, u32[]{:S(2)}) collective-permute-start(bf16[256,1024]{1,0:T(8,128)(2,1)S(1)} %attend_last.2.refs_0_), channel_id=1, source_target_pairs={{0,1},{1,0},{2,3},{3,2},{4,5},{5,4},{6,7},{7,6},{8,9},{9,8},{10,11... | collective-permute-start | bytes 1572872 | tf_op jit(solution)/shard_map/ppermute | solution.py:428
  64.7 6.9 %attend_more.3 = (f32[256,128]{1,0:T(8,128)S(1)}, f32[8,256,256]{2,1,0:T(8,128)S(1)}) custom-call(bf16[256,2048]{1,0:T(8,128)(2,1)S(1)} %copy-done.4, bf16[4,2,256,128]{3,2,1,0:T(8,128)(2,1)S(1)} %pad_maximum_fusion.2.near_ref, bf16[4,2,256,128]{3,2,1,0:T(8,128)(2,1)S(1)} %collective-permute-done.17.far_ref, f32[256,128]{1,0:T(8,128)S(1)} %get-tuple-element.21.refs_0_, ...), custom_call_target="tpu_custom_call" | custom-call | flops 4294967296 | bytes 2097152 | tf_op jit(solution)/shard_map/attend_more/pallas_call | solution.py:178
  71.7 3.9 %attend_last.3.refs_1_ = bf16[256,1024]{1,0:T(8,128)(2,1)S(1)} custom-call(bf16[256,2048]{1,0:T(8,128)(2,1)S(1)} %copy-done.4, bf16[2,2,256,128]{3,2,1,0:T(8,128)(2,1)S(1)} %pad_maximum_fusion.6.near_ref, bf16[2,2,256,128]{3,2,1,0:T(8,128)(2,1)S(1)} %collective-permute-done.13.far_ref, f32[256,128]{1,0:T(8,128)S(1)} %get-tuple-element.23.refs_0_, ...), custom_call_target="tpu_custom_call" | custom-call | flops 2147483648 | bytes 2097152 | tf_op jit(solution)/shard_map/attend_last/pallas_call | solution.py:178
  77.1 11.3 %project_base.1 = (f32[256,4096]{1,0:T(8,128)S(1)}, f32[256,4096]{1,0:T(8,128)S(1)}, bf16[1024,4096]{1,0:T(8,128)(2,1)S(1)}) custom-call(s32[1,256]{1,0:T(1,128)S(1)} %bitcast.25, s32[1,256]{1,0:T(1,128)S(1)} %bitcast.27, bf16[256,4096]{1,0:T(8,128)(2,1)S(1)} %copy-done.1, bf16[384,4096]{1,0:T(8,128)(2,1)S(1)} %copy-done, ...), custom_call_target="tpu_custom_call" | custom-call | flops 7247757312 | bytes 35651584 | tf_op jit(solution)/shard_map/project_base/pallas_call | solution.py:270
  89.2 5.5 %finish.1 = (bf16[256,4096]{1,0:T(8,128)(2,1)}, bf16[384,4096]{1,0:T(8,128)(2,1)}, bf16[16,4096]{1,0:T(8,128)(2,1)S(1)}, f32[16,4096]{1,0:T(8,128)S(1)}) custom-call(s32[1,256]{1,0:T(1,128)S(1)} %bitcast.26, s32[1,256]{1,0:T(1,128)S(1)} %bitcast.28, f32[256,4096]{1,0:T(8,128)S(1)} %get-tuple-element.25.base_ref, ...), custom_call_target="tpu_custom_call" | custom-call | flops 2952790016 | bytes 22020096 | tf_op jit(solution)/shard_map/finish/pallas_call | solution.py:330
  94.8 1.9 %collective-permute-start.21 = (bf16[8,4096]{1,0:T(8,128)(2,1)S(1)}, bf16[8,4096]{1,0:T(8,128)(2,1)S(1)}, u32[]{:S(2)}, u32[]{:S(2)}) collective-permute-start(bf16[8,4096]{1,0:T(8,128)(2,1)S(1)} %get-tuple-element.42), channel_id=1, source_target_pairs={{2,0},{4,2},{6,4},{8,6},{10,8},{12,10},{14,12},{16,14},{18,16},{20... | collective-permute-start | bytes 196616 | tf_op jit(solution)/shard_map/ppermute | solution.py:32
  96.7 2.4 %collective-permute-start.20 = (bf16[8,4096]{1,0:T(8,128)(2,1)S(1)}, bf16[8,4096]{1,0:T(8,128)(2,1)S(1)}, u32[]{:S(2)}, u32[]{:S(2)}) collective-permute-start(bf16[8,4096]{1,0:T(8,128)(2,1)S(1)} %get-tuple-element.43), channel_id=1, source_target_pairs={{0,2},{2,4},{4,6},{6,8},{8,10},{10,12},{12,14},{14,16},{16,18},{18... | collective-permute-start | bytes 196616 | tf_op jit(solution)/shard_map/ppermute | solution.py:32
  99.2 4.1 %collective-permute-done.20.below_ref = bf16[8,4096]{1,0:T(8,128)(2,1)S(1)} collective-permute-done((bf16[8,4096]{1,0:T(8,128)(2,1)S(1)}, bf16[8,4096]{1,0:T(8,128)(2,1)S(1)}, u32[]{:S(2)}, u32[]{:S(2)}) %collective-permute-start.20) | collective-permute-done | bytes 65568 | tf_op jit(solution)/shard_map/ppermute | solution.py:32
  103.2 1.6 %add_rim.1 = bf16[384,4096]{1,0:T(8,128)(2,1)} custom-call(bf16[384,4096]{1,0:T(8,128)(2,1)} %get-tuple-element.29.core_ref, f32[16,4096]{1,0:T(8,128)S(1)} %get-tuple-element.30.rim_ref, bf16[8,4096]{1,0:T(8,128)(2,1)S(1)} %collective-permute-done.20.below_ref, bf16[8,4096]{1,0:T(8,128)(2,1)S(1)} %collective-permute-done.21.above_ref), custom_call_target="tpu_custom_call", output_to_operand_aliasing={{}: (0, {})} | custom-call | tf_op jit(solution)/shard_map/add_rim/pallas_call | solution.py:373
  (53 shorter events, 6.9 us)
Async XLA Ops:
  1.7 20.2 %collective-permute-start.15 = (bf16[2,256,128]{2,1,0:T(8,128)(2,1)S(1)}, bf16[2,256,128]{2,1,0:T(8,128)(2,1)S(1)}, u32[]{:S(2)}, u32[]{:S(2)}) collective-permute-start(bf16[2,256,128]{2,1,0:T(8,128)(2,1)S(1)} %get-tuple-element.36.own_ref), channel_id=1, source_target_pairs={{0,16},{2,18},{4,20},{6,22},{8,24},{10,26},{12,28},{14,30},{16,0},... | collective-permute-start | bytes 393224 | tf_op jit(solution)/shard_map/ppermute | solution.py:37
  2.1 22.2 %collective-permute-start.14 = (bf16[2,256,128]{2,1,0:T(8,128)(2,1)S(1)}, bf16[2,256,128]{2,1,0:T(8,128)(2,1)S(1)}, u32[]{:S(2)}, u32[]{:S(2)}) collective-permute-start(bf16[2,256,128]{2,1,0:T(8,128)(2,1)S(1)} %get-tuple-element.36.own_ref), channel_id=1, source_target_pairs={{0,8},{2,10},{4,12},{6,14},{8,0},{10,2},{12,4},{14,6},{16,24},{18,... | collective-permute-start | bytes 393224 | tf_op jit(solution)/shard_map/ppermute | solution.py:37
  2.2 22.1 %collective-permute-start.11 = (bf16[2,256,128]{2,1,0:T(8,128)(2,1)S(1)}, bf16[2,256,128]{2,1,0:T(8,128)(2,1)S(1)}, u32[]{:S(2)}, u32[]{:S(2)}) collective-permute-start(bf16[2,256,128]{2,1,0:T(8,128)(2,1)S(1)} %get-tuple-element.36.own_ref), channel_id=1, source_target_pairs={{0,24},{2,26},{4,28},{6,30},{8,16},{10,18},{12,20},{14,22},{16,8},... | collective-permute-start | bytes 393224 | tf_op jit(solution)/shard_map/ppermute | solution.py:37
  7.0 8.1 %collective-permute-start = (bf16[8,4096]{1,0:T(8,128)(2,1)S(1)}, bf16[8,4096]{1,0:T(8,128)(2,1)S(1)}, u32[]{:S(2)}, u32[]{:S(2)}) collective-permute-start(bf16[8,4096]{1,0:T(8,128)(2,1)S(1)} %get-tuple-element.32), channel_id=1, source_target_pairs={{0,2},{2,4},{4,6},{6,8},{8,10},{10,12},{12,14},{14,16},{16,18},{18... | collective-permute-start | bytes 196616 | tf_op jit(solution)/shard_map/ppermute | solution.py:32
  8.9 6.4 %collective-permute-start.1 = (bf16[8,4096]{1,0:T(8,128)(2,1)S(1)}, bf16[8,4096]{1,0:T(8,128)(2,1)S(1)}, u32[]{:S(2)}, u32[]{:S(2)}) collective-permute-start(bf16[8,4096]{1,0:T(8,128)(2,1)S(1)} %get-tuple-element.33), channel_id=1, source_target_pairs={{2,0},{4,2},{6,4},{8,6},{10,8},{12,10},{14,12},{16,14},{18,16},{20... | collective-permute-start | bytes 196616 | tf_op jit(solution)/shard_map/ppermute | solution.py:32
  15.1 14.8 %collective-permute-start.6 = (bf16[2,256,128]{2,1,0:T(8,128)(2,1)S(1)}, bf16[2,256,128]{2,1,0:T(8,128)(2,1)S(1)}, u32[]{:S(2)}, u32[]{:S(2)}) collective-permute-start(bf16[2,256,128]{2,1,0:T(8,128)(2,1)S(1)} %get-tuple-element.37.own_ref), channel_id=1, source_target_pairs={{0,16},{2,18},{4,20},{6,22},{8,24},{10,26},{12,28},{14,30},{16,0},... | collective-permute-start | bytes 393224 | tf_op jit(solution)/shard_map/ppermute | solution.py:37
  15.4 16.7 %collective-permute-start.5 = (bf16[2,256,128]{2,1,0:T(8,128)(2,1)S(1)}, bf16[2,256,128]{2,1,0:T(8,128)(2,1)S(1)}, u32[]{:S(2)}, u32[]{:S(2)}) collective-permute-start(bf16[2,256,128]{2,1,0:T(8,128)(2,1)S(1)} %get-tuple-element.37.own_ref), channel_id=1, source_target_pairs={{0,8},{2,10},{4,12},{6,14},{8,0},{10,2},{12,4},{14,6},{16,24},{18,... | collective-permute-start | bytes 393224 | tf_op jit(solution)/shard_map/ppermute | solution.py:37
  21.8 8.1 %collective-permute-start.2 = (bf16[2,256,128]{2,1,0:T(8,128)(2,1)S(1)}, bf16[2,256,128]{2,1,0:T(8,128)(2,1)S(1)}, u32[]{:S(2)}, u32[]{:S(2)}) collective-permute-start(bf16[2,256,128]{2,1,0:T(8,128)(2,1)S(1)} %get-tuple-element.37.own_ref), channel_id=1, source_target_pairs={{0,24},{2,26},{4,28},{6,30},{8,16},{10,18},{12,20},{14,22},{16,8},... | collective-permute-start | bytes 393224 | tf_op jit(solution)/shard_map/ppermute | solution.py:37
  24.3 15.0 %collective-permute-start.9 = (bf16[2,2,256,128]{3,2,1,0:T(8,128)(2,1)S(1)}, bf16[2,2,256,128]{3,2,1,0:T(8,128)(2,1)S(1)}, u32[]{:S(2)}, u32[]{:S(2)}) collective-permute-start(bf16[2,2,256,128]{3,2,1,0:T(8,128)(2,1)S(1)} %get-tuple-element.41), channel_id=1, source_target_pairs={{0,4},{2,6},{4,0},{6,2},{8,12},{10,14},{12,8},{14,10},{16,20},{18,... | collective-permute-start | bytes 786440 | tf_op jit(solution)/shard_map/ppermute | solution.py:37
  24.4 15.5 %collective-permute-start.12 = (bf16[1,2,256,128]{3,2,1,0:T(8,128)(2,1)S(1)}, bf16[1,2,256,128]{3,2,1,0:T(8,128)(2,1)S(1)}, u32[]{:S(2)}, u32[]{:S(2)}) collective-permute-start(bf16[1,2,256,128]{3,2,1,0:T(8,128)(2,1)S(1)} %bitcast.38), channel_id=1, source_target_pairs={{0,4},{2,6},{4,0},{6,2},{8,12},{10,14},{12,8},{14,10},{16,20},{18,... | collective-permute-start | bytes 393224 | tf_op jit(solution)/shard_map/ppermute | solution.py:37
  29.9 9.2 %collective-permute-start.3 = (bf16[1,2,256,128]{3,2,1,0:T(8,128)(2,1)S(1)}, bf16[1,2,256,128]{3,2,1,0:T(8,128)(2,1)S(1)}, u32[]{:S(2)}, u32[]{:S(2)}) collective-permute-start(bf16[1,2,256,128]{3,2,1,0:T(8,128)(2,1)S(1)} %bitcast.40), channel_id=1, source_target_pairs={{0,4},{2,6},{4,0},{6,2},{8,12},{10,14},{12,8},{14,10},{16,20},{18,... | collective-permute-start | bytes 393224 | tf_op jit(solution)/shard_map/ppermute | solution.py:37
  30.0 16.3 %collective-permute-start.16 = (bf16[2,2,256,128]{3,2,1,0:T(8,128)(2,1)S(1)}, bf16[2,2,256,128]{3,2,1,0:T(8,128)(2,1)S(1)}, u32[]{:S(2)}, u32[]{:S(2)}) collective-permute-start(bf16[2,2,256,128]{3,2,1,0:T(8,128)(2,1)S(1)} %pad_maximum_fusion.7), channel_id=1, source_target_pairs={{0,4},{2,6},{4,0},{6,2},{8,12},{10,14},{12,8},{14,10},{16,20},{18,... | collective-permute-start | bytes 786440 | tf_op jit(solution)/shard_map/ppermute | solution.py:37
  32.0 14.8 %copy-start.4 = (bf16[256,2048]{1,0:T(8,128)(2,1)S(1)}, bf16[256,2048]{1,0:T(8,128)(2,1)}, u32[]{:S(2)}) copy-start(bf16[256,2048]{1,0:T(8,128)(2,1)} %query_ref.11) | copy-start | bytes 3145732
  32.1 14.0 %collective-permute-start.7 = (bf16[2,2,256,128]{3,2,1,0:T(8,128)(2,1)S(1)}, bf16[2,2,256,128]{3,2,1,0:T(8,128)(2,1)S(1)}, u32[]{:S(2)}, u32[]{:S(2)}) collective-permute-start(bf16[2,2,256,128]{3,2,1,0:T(8,128)(2,1)S(1)} %pad_maximum_fusion.4), channel_id=1, source_target_pairs={{0,4},{2,6},{4,0},{6,2},{8,12},{10,14},{12,8},{14,10},{16,20},{18,... | collective-permute-start | bytes 786440 | tf_op jit(solution)/shard_map/ppermute | solution.py:37
  39.2 20.2 %collective-permute-start.4 = (bf16[2,2,256,128]{3,2,1,0:T(8,128)(2,1)S(1)}, bf16[2,2,256,128]{3,2,1,0:T(8,128)(2,1)S(1)}, u32[]{:S(2)}, u32[]{:S(2)}) collective-permute-start(bf16[2,2,256,128]{3,2,1,0:T(8,128)(2,1)S(1)} %pad_maximum_fusion.3.near_ref), channel_id=1, source_target_pairs={{0,2},{2,0},{4,6},{6,4},{8,10},{10,8},{12,14},{14,12},{16,18},{18,... | collective-permute-start | bytes 786440 | tf_op jit(solution)/shard_map/ppermute | solution.py:37
  39.3 7.5 %collective-permute-start.10 = (bf16[2,2,2,256,128]{4,3,2,1,0:T(8,128)(2,1)S(1)}, bf16[2,2,2,256,128]{4,3,2,1,0:T(8,128)(2,1)S(1)}, u32[]{:S(2)}, u32[]{:S(2)}) collective-permute-start(bf16[2,2,2,256,128]{4,3,2,1,0:T(8,128)(2,1)S(1)} %pad_maximum_fusion.1), channel_id=1, source_target_pairs={{0,2},{2,0},{4,6},{6,4},{8,10},{10,8},{12,14},{14,12},{16,18},{18,... | collective-permute-start | bytes 1572872 | tf_op jit(solution)/shard_map/ppermute | solution.py:37
  39.9 31.8 %collective-permute-start.13 = (bf16[2,2,256,128]{3,2,1,0:T(8,128)(2,1)S(1)}, bf16[2,2,256,128]{3,2,1,0:T(8,128)(2,1)S(1)}, u32[]{:S(2)}, u32[]{:S(2)}) collective-permute-start(bf16[2,2,256,128]{3,2,1,0:T(8,128)(2,1)S(1)} %pad_maximum_fusion.6.near_ref), channel_id=1, source_target_pairs={{0,2},{2,0},{4,6},{6,4},{8,10},{10,8},{12,14},{14,12},{16,18},{18,... | collective-permute-start | bytes 786440 | tf_op jit(solution)/shard_map/ppermute | solution.py:37
  46.1 6.3 %collective-permute-start.8 = (bf16[4,2,256,128]{3,2,1,0:T(8,128)(2,1)S(1)}, bf16[4,2,256,128]{3,2,1,0:T(8,128)(2,1)S(1)}, u32[]{:S(2)}, u32[]{:S(2)}) collective-permute-start(bf16[4,2,256,128]{3,2,1,0:T(8,128)(2,1)S(1)} %pad_maximum_fusion.near_ref), channel_id=1, source_target_pairs={{0,2},{2,0},{4,6},{6,4},{8,10},{10,8},{12,14},{14,12},{16,18},{18,... | collective-permute-start | bytes 1572872 | tf_op jit(solution)/shard_map/ppermute | solution.py:37
  46.3 18.4 %collective-permute-start.17 = (bf16[4,2,256,128]{3,2,1,0:T(8,128)(2,1)S(1)}, bf16[4,2,256,128]{3,2,1,0:T(8,128)(2,1)S(1)}, u32[]{:S(2)}, u32[]{:S(2)}) collective-permute-start(bf16[4,2,256,128]{3,2,1,0:T(8,128)(2,1)S(1)} %pad_maximum_fusion.2.near_ref), channel_id=1, source_target_pairs={{0,2},{2,0},{4,6},{6,4},{8,10},{10,8},{12,14},{14,12},{16,18},{18,... | collective-permute-start | bytes 1572872 | tf_op jit(solution)/shard_map/ppermute | solution.py:37
  63.2 13.9 %collective-permute-start.18 = (bf16[256,1024]{1,0:T(8,128)(2,1)S(1)}, bf16[256,1024]{1,0:T(8,128)(2,1)S(1)}, u32[]{:S(2)}, u32[]{:S(2)}) collective-permute-start(bf16[256,1024]{1,0:T(8,128)(2,1)S(1)} %attend_last.2.refs_0_), channel_id=1, source_target_pairs={{0,1},{1,0},{2,3},{3,2},{4,5},{5,4},{6,7},{7,6},{8,9},{9,8},{10,11... | collective-permute-start | bytes 1572872 | tf_op jit(solution)/shard_map/ppermute | solution.py:428
  71.7 5.5 %copy-start = (bf16[384,4096]{1,0:T(8,128)(2,1)S(1)}, bf16[384,4096]{1,0:T(8,128)(2,1)}, u32[]{:S(2)}) copy-start(bf16[384,4096]{1,0:T(8,128)(2,1)} %teacher_ref.1) | copy-start | bytes 9437188
  75.6 13.7 %collective-permute-start.19 = (bf16[256,1024]{1,0:T(8,128)(2,1)S(1)}, bf16[256,1024]{1,0:T(8,128)(2,1)S(1)}, u32[]{:S(2)}, u32[]{:S(2)}) collective-permute-start(bf16[256,1024]{1,0:T(8,128)(2,1)S(1)} %attend_last.3.refs_1_), channel_id=1, source_target_pairs={{0,1},{1,0},{2,3},{3,2},{4,5},{5,4},{6,7},{7,6},{8,9},{9,8},{10,11... | collective-permute-start | bytes 1572872 | tf_op jit(solution)/shard_map/ppermute | solution.py:428
  94.8 4.3 %collective-permute-start.21 = (bf16[8,4096]{1,0:T(8,128)(2,1)S(1)}, bf16[8,4096]{1,0:T(8,128)(2,1)S(1)}, u32[]{:S(2)}, u32[]{:S(2)}) collective-permute-start(bf16[8,4096]{1,0:T(8,128)(2,1)S(1)} %get-tuple-element.42), channel_id=1, source_target_pairs={{2,0},{4,2},{6,4},{8,6},{10,8},{12,10},{14,12},{16,14},{18,16},{20... | collective-permute-start | bytes 196616 | tf_op jit(solution)/shard_map/ppermute | solution.py:32
  96.7 6.5 %collective-permute-start.20 = (bf16[8,4096]{1,0:T(8,128)(2,1)S(1)}, bf16[8,4096]{1,0:T(8,128)(2,1)S(1)}, u32[]{:S(2)}, u32[]{:S(2)}) collective-permute-start(bf16[8,4096]{1,0:T(8,128)(2,1)S(1)} %get-tuple-element.43), channel_id=1, source_target_pairs={{0,2},{2,4},{4,6},{6,8},{8,10},{10,12},{12,14},{14,16},{16,18},{18... | collective-permute-start | bytes 196616 | tf_op jit(solution)/shard_map/ppermute | solution.py:32
  (3 other events, 16.3 us)

commit v2 on v1

v2 whole, which is shorter than its diff:
```python
import functools
import math

import jax
import jax.numpy as jnp
from jax import lax
from jax.experimental import pallas as pl
from jax.experimental.pallas import tpu as pltpu
from jax.sharding import PartitionSpec as P


HEADS = 32
KVH = 4
HD = 128
HALO = 8
GROUP = 4

F32 = jnp.float32
BF16 = jnp.bfloat16
floor_score = -1e30
exp2_scale = math.log2(math.e) / math.sqrt(HD)

ATTN_VMEM = 9 * 1024 * 1024
PROJECT_VMEM = 20 * 1024 * 1024
FINISH_VMEM = 8 * 1024 * 1024


def odd_swapped(value, axis):
    count = lax.axis_size(axis)
    return lax.ppermute(
        value, axis, [(i, i + 1 if i % 2 else i - 1) for i in range(1, count - 1)]
    )


def swapped(value, axis, bit):
    count = lax.axis_size(axis)
    return lax.ppermute(value, axis, [(source, source ^ bit) for source in range(count)])


def attention_step(
    query_ref, heads, keys, values, state, hidden, diagonal, peak_ref, accum_ref
):
    rows = keys[0].shape[0]
    ones = jnp.ones((rows, HD), BF16)
    padded = [jnp.concatenate([block, ones], axis=1) for block in values]

    def product(head):
        query = query_ref[:, head * HD : (head + 1) * HD]
        return [
            lax.dot_general(query, block, (((1,), (1,)), ((), ())), preferred_element_type=F32)
            for block in keys
        ]

    scores = product(0)
    for head in range(heads):
        following = product(head + 1) if head + 1 < heads else None
        if diagonal is not None:
            scores[0] = jnp.where(diagonal, scores[0], floor_score)
        if hidden is None:
            top = functools.reduce(jnp.maximum, scores)
            top = jnp.max(top, axis=1, keepdims=True) * exp2_scale
        else:
            tops = [
                jnp.max(block, axis=1, keepdims=True) * exp2_scale - off
                for block, off in zip(scores, hidden)
            ]
            top = functools.reduce(jnp.maximum, tops)
        peak = top if state is None else jnp.maximum(state[head][0], top)
        accum = None if state is None else state[head][1][...] * jnp.exp2(state[head][0] - peak)
        for index, (block, value) in enumerate(zip(scores, padded)):
            shift = peak if hidden is None else peak + hidden[index]
            weights = jnp.exp2(block * exp2_scale - shift).astype(BF16)
            added = jnp.dot(weights, value, preferred_element_type=F32)
            accum = added if accum is None else accum + added
        peak_ref[:, head : head + 1] = peak
        accum_ref[head] = accum
        scores = following


def own_kernel(heads, query_ref, own_ref, side_ref, other_ref, peak_ref, accum_ref):
    rows = query_ref.shape[0]
    place = lax.rem(lax.axis_index("ctx"), GROUP)
    pieces = [own_ref, side_ref, other_ref.at[0], other_ref.at[1]]
    hidden = [0.0] + [
        jnp.where((place ^ flip) < place, 0.0, -floor_score).astype(F32) for flip in (2, 1, 3)
    ]
    diagonal = lax.broadcasted_iota(jnp.int32, (rows, rows), 1) <= lax.broadcasted_iota(
        jnp.int32, (rows, rows), 0
    )
    attention_step(
        query_ref,
        heads,
        [p[0] for p in pieces],
        [p[1] for p in pieces],
        None,
        hidden,
        diagonal,
        peak_ref,
        accum_ref,
    )


def weight_rows(step, start, depth, lane_rows, tp_count):
    lane = lax.rem(lax.axis_index("tp") + tp_count - step, tp_count)
    return pl.ds(pl.multiple_of(lane * lane_rows + start, HD), depth)


def more_kernel(heads, first, stages, fetch, query_ref, near_ref, far_ref, *refs):
    (peak_in, accum_in), refs = refs[:2], refs[2:]
    copy = None
    if fetch:
        weight_hbm, out_ref, weight_ref, peak_ref, accum_ref, sem = refs
        copy = pltpu.make_async_copy(weight_hbm.at[weight_rows(*fetch), :], weight_ref, sem)
        copy.start()
    else:
        out_ref, peak_ref, accum_ref = refs
    for head in range(heads):
        accum_ref[head] = accum_in[first + head]
        peak_ref[:, head : head + 1] = peak_in[:, first + head : first + head + 1]
    group = lax.div(lax.axis_index("ctx"), GROUP)
    count = len(stages)

    def step(index, carry):
        @pl.when((group ^ (index + stages[0])) < group)
        def _():
            pieces = [ref.at[at] for ref in (near_ref, far_ref) for at in (index, index + count)]
            state = [(peak_ref[:, head : head + 1], accum_ref.at[head]) for head in range(heads)]
            attention_step(
                query_ref,
                heads,
                [p[0] for p in pieces],
                [p[1] for p in pieces],
                state,
                None,
                None,
                peak_ref,
                accum_ref,
            )

        return carry

    lax.fori_loop(0, count, step, 0)
    for head in range(heads):
        accum = accum_ref[head]
        out_ref[:, head * HD : (head + 1) * HD] = (accum[:, :HD] / accum[:, HD:]).astype(BF16)
    if copy is not None:
        copy.wait()


VMEM_SPEC = pl.BlockSpec(memory_space=pltpu.VMEM)
HBM_SPEC = pl.BlockSpec(memory_space=pltpu.HBM)
MIB = 1024 * 1024


def attention_cost(rows, heads, keys):
    return pl.CostEstimate(
        flops=4 * rows * heads * keys * HD * 2,
        transcendentals=rows * heads * keys,
        bytes_accessed=2 * MIB,
    )


def state_shapes(rows, heads):
    return [((rows, HD), F32), ((heads, rows, 2 * HD), F32)]


def query_spec(rows, heads, kv):
    return pl.BlockSpec((rows, heads * HD), lambda i: (0, kv))


def attend_own(queries, kv, heads, own, side, other):
    rows = queries.shape[0]
    return pl.pallas_call(
        functools.partial(own_kernel, heads),
        grid=(1,),
        in_specs=[query_spec(rows, heads, kv)] + [VMEM_SPEC] * 3,
        out_specs=[VMEM_SPEC] * 2,
        out_shape=[jax.ShapeDtypeStruct(*shape) for shape in state_shapes(rows, heads)],
        compiler_params=pltpu.CompilerParams(vmem_limit_bytes=ATTN_VMEM),
        cost_estimate=attention_cost(rows, heads, GROUP * rows),
        name="attend_own",
    )(queries, own, side, other)


def attend_more(queries, kv, per_own, first, heads, stages, near, far, state, fetch, out_weight):
    rows = queries.shape[0]
    extra = [out_weight] if fetch else []
    return pl.pallas_call(
        functools.partial(more_kernel, heads, first, stages, fetch),
        grid=(1,),
        in_specs=[query_spec(rows, heads, (kv * per_own + first) // heads)]
        + [VMEM_SPEC] * 4
        + [HBM_SPEC] * len(extra),
        out_specs=[VMEM_SPEC] * (1 + len(extra)),
        out_shape=[jax.ShapeDtypeStruct((rows, heads * HD), BF16)]
        + [pltpu.VMEM((fetch[2], out_weight.shape[1]), BF16) for _ in extra],
        scratch_shapes=[pltpu.VMEM(*shape) for shape in state_shapes(rows, heads)]
        + [pltpu.SemaphoreType.DMA] * len(extra),
        compiler_params=pltpu.CompilerParams(vmem_limit_bytes=ATTN_VMEM),
        cost_estimate=attention_cost(rows, heads, 2 * near.shape[0] * rows),
        name="attend_more",
    )(queries, near, far, *state, *extra)


def upright(row):
    count = row.shape[1]
    same = iota((count, count), 0) == iota((count, count), 1)
    return jnp.sum(jnp.where(same, row, 0), axis=1, keepdims=True)


def member_of(starts, lens, columns):
    return ((columns >= starts) & (columns < starts + lens)).astype(F32).astype(BF16)


def iota(shape, axis):
    return lax.broadcasted_iota(jnp.int32, shape, axis)


def is_odd():
    return lax.rem(lax.axis_index("ctx"), 2) == 1


def rim_rows(index, teach):
    below = (index < HALO) == is_odd()
    index = jnp.where(index < HALO, index, index - HALO)
    return jnp.where(below, index - HALO, index + teach)


def streamed(pieces, piece_refs, weight_hbm, lane_rows, tp_count, cols, slots, buf, sems):
    steps = weight_hbm.shape[1] // cols

    def loads(step):
        copies, at = [], 0
        for index, (lane_step, start, depth) in enumerate(pieces):
            copies.append(
                pltpu.make_async_copy(
                    weight_hbm.at[
                        weight_rows(lane_step, start, depth, lane_rows, tp_count),
                        pl.ds(step * cols, cols),
                    ],
                    buf.at[step % slots, pl.ds(at, depth), :],
                    sems.at[step % slots, index],
                )
            )
            at += depth
        return copies

    def begin(step):
        for load in loads(step):
            load.start()

    def product(step, total):
        at = 0
        for load in loads(step):
            load.wait()
        for (_, _, depth), ref in zip(pieces, piece_refs):
            block = buf[step % slots, at : at + depth, :]
            total += jnp.dot(ref[...], block, preferred_element_type=F32)
            at += depth
        if step + slots < steps:
            begin(step + slots)
        return total

    for step in range(min(slots, steps)):
        begin(step)
    return product


def base_kernel(pieces, lane_rows, tp_count, cols, slots, start_ref, len_ref, *refs):
    student_ref, teacher_ref, near_ref, far_ref = refs[:4]
    piece_refs = refs[4 : 4 + len(pieces)]
    weight_hbm, base_ref, target_ref, buf, sems = refs[4 + len(pieces) :]
    product = streamed(
        pieces, piece_refs, weight_hbm, lane_rows, tp_count, cols, slots, buf, sems
    )
    rows, width = student_ref.shape
    teach = teacher_ref.shape[0]
    starts = upright(start_ref[...]) - lax.axis_index("ctx") * teach
    lens = upright(len_ref[...])
    inner = member_of(starts, lens, iota((rows, teach), 1))
    outer = member_of(starts, lens, rim_rows(iota((rows, 2 * HALO), 1), teach))
    counts = lens.astype(F32)
    for step in range(width // cols):
        span = slice(step * cols, (step + 1) * cols)
        target = jnp.dot(inner, teacher_ref[:, span], preferred_element_type=F32)
        halo = [ref[:, span].astype(F32) for ref in (near_ref, far_ref)]
        halo = jnp.concatenate(halo, axis=0).astype(BF16)
        target += jnp.dot(outer, halo, preferred_element_type=F32)
        target_ref[:, span] = target / counts
        base_ref[:, span] = product(step, student_ref[:, span].astype(F32))


def add_kernel(pieces, lane_rows, tp_count, cols, slots, base_ref, *refs):
    piece_refs = refs[: len(pieces)]
    weight_hbm, out_ref, buf, sems = refs[len(pieces) :]
    product = streamed(
        pieces, piece_refs, weight_hbm, lane_rows, tp_count, cols, slots, buf, sems
    )
    for step in range(base_ref.shape[1] // cols):
        span = slice(step * cols, (step + 1) * cols)
        out_ref[:, span] = product(step, base_ref[:, span])


def project(kernel, outputs, pieces, values, lane_rows, tp_count, inputs, out_weight):
    width = out_weight.shape[1]
    cols, slots = min(512, width), 4
    depth = sum(piece[2] for piece in pieces)
    rows = inputs[-1].shape[0] if len(inputs) == 1 else inputs[2].shape[0]
    return pl.pallas_call(
        functools.partial(kernel, pieces, lane_rows, tp_count, cols, slots),
        in_specs=[VMEM_SPEC] * (len(inputs) + len(values)) + [HBM_SPEC],
        out_specs=[VMEM_SPEC] * outputs,
        out_shape=[jax.ShapeDtypeStruct((rows, width), F32)] * outputs,
        scratch_shapes=[
            pltpu.VMEM((slots, max(depth, 16), cols), BF16),
            pltpu.SemaphoreType.DMA((slots, max(1, len(pieces)))),
        ],
        compiler_params=pltpu.CompilerParams(vmem_limit_bytes=PROJECT_VMEM),
        cost_estimate=pl.CostEstimate(
            flops=2 * rows * width * depth,
            transcendentals=0,
            bytes_accessed=2 * depth * width + 10 * rows * width,
        ),
    )(*inputs, *values, out_weight)


def final_kernel(count, cols, teach, start_ref, len_ref, base_ref, target_ref, *refs):
    piece_refs, weight_ref = refs[:count], refs[count]
    student_out, weighted_ref, near_ref, far_ref, student_buf, sems = refs[count + 1 :]
    rows, width = base_ref.shape
    starts, lens = start_ref[...] - lax.axis_index("ctx") * teach, len_ref[...]
    outer_t = member_of(starts, lens, rim_rows(iota((2 * HALO, rows), 0), teach))
    counts = upright(lens).astype(F32)
    copies = []
    for index, start in enumerate(range(0, width, cols)):
        span = slice(start, start + cols)
        total = base_ref[:, span]
        at = 0
        for ref in piece_refs:
            block = weight_ref[at : at + ref.shape[1], span]
            total += jnp.dot(ref[...], block, preferred_element_type=F32)
            at += ref.shape[1]
        student_buf[:, span] = total.astype(BF16)
        copy = pltpu.make_async_copy(
            student_buf.at[:, span], student_out.at[:, span], sems.at[index]
        )
        copy.start()
        copies.append(copy)
        weighted = ((total - target_ref[:, span]) / counts).astype(BF16)
        weighted_ref[:, span] = weighted
        edge = jnp.dot(outer_t, weighted, preferred_element_type=F32)
        near_ref[:, span] = edge[:HALO].astype(BF16)
        far_ref[:, span] = edge[HALO:].astype(BF16)
    for copy in copies:
        copy.wait()


def finish(starts, lens, base, target, teach, pieces, weight):
    rows, width = base.shape
    count, depth = len(pieces), weight.shape[0]
    cols = min(512, width)
    return pl.pallas_call(
        functools.partial(final_kernel, count, cols, teach),
        in_specs=[VMEM_SPEC] * (5 + count),
        out_specs=[HBM_SPEC] + [VMEM_SPEC] * 3,
        scratch_shapes=[pltpu.VMEM((rows, width), BF16), pltpu.SemaphoreType.DMA((width // cols,))],
        out_shape=[
            jax.ShapeDtypeStruct((rows, width), BF16),
            jax.ShapeDtypeStruct((rows, width), BF16),
            jax.ShapeDtypeStruct((HALO, width), BF16),
            jax.ShapeDtypeStruct((HALO, width), BF16),
        ],
        compiler_params=pltpu.CompilerParams(vmem_limit_bytes=FINISH_VMEM),
        cost_estimate=pl.CostEstimate(
            flops=2 * rows * width * depth,
            transcendentals=0,
            bytes_accessed=2 * depth * width + 10 * rows * width,
        ),
        name="finish",
    )(starts[None, :], lens[None, :], base, target, *pieces, weight)


def spread_kernel(cols, start_ref, len_ref, weighted_ref, core_out, rim_ref, core_buf, sems):
    rows, width = weighted_ref.shape
    teach = core_buf.shape[0]
    starts, lens = start_ref[...] - lax.axis_index("ctx") * teach, len_ref[...]
    inner_t = member_of(starts, lens, iota((teach, rows), 0))
    copies = []
    for index, start in enumerate(range(0, width, cols)):
        span = slice(start, start + cols)
        core = jnp.dot(inner_t, weighted_ref[:, span], preferred_element_type=F32)
        core_buf[:, span] = core.astype(BF16)
        rim_ref[: 2 * HALO, span] = core[: 2 * HALO]
        rim_ref[2 * HALO :, span] = core[teach - 2 * HALO :]
        copy = pltpu.make_async_copy(
            core_buf.at[:, span], core_out.at[:, span], sems.at[index]
        )
        copy.start()
        copies.append(copy)
    for copy in copies:
        copy.wait()


def spread_out(starts, lens, weighted, teach):
    rows, width = weighted.shape
    cols = min(1024, width)
    return pl.pallas_call(
        functools.partial(spread_kernel, cols),
        in_specs=[VMEM_SPEC] * 3,
        out_specs=[HBM_SPEC, VMEM_SPEC],
        scratch_shapes=[pltpu.VMEM((teach, width), BF16), pltpu.SemaphoreType.DMA((width // cols,))],
        out_shape=[
            jax.ShapeDtypeStruct((teach, width), BF16),
            jax.ShapeDtypeStruct((4 * HALO, width), F32),
        ],
        compiler_params=pltpu.CompilerParams(vmem_limit_bytes=FINISH_VMEM),
        cost_estimate=pl.CostEstimate(
            flops=2 * rows * width * teach, transcendentals=0, bytes_accessed=2 * teach * width
        ),
        name="spread_out",
    )(starts[None, :], lens[None, :], weighted)


def rim_kernel(core_in, rim_ref, near_ref, far_ref, core_out, block_ref, sems):
    del core_in
    near, far = near_ref[...].astype(F32), far_ref[...].astype(F32)
    rest = jnp.zeros_like(near)
    odd = is_odd()
    first = jnp.concatenate([jnp.where(odd, near, far), rest], axis=0)
    last = jnp.concatenate([rest, jnp.where(odd, far, near)], axis=0)
    height = 2 * HALO
    copies = []
    for slot, (part, row) in enumerate(((first, 0), (last, core_out.shape[0] - height))):
        block_ref[slot] = (rim_ref[slot * height : (slot + 1) * height] + part).astype(BF16)
        copy = pltpu.make_async_copy(
            block_ref.at[slot], core_out.at[pl.ds(row, height), :], sems.at[slot]
        )
        copy.start()
        copies.append(copy)
    for copy in copies:
        copy.wait()


def add_rim(core, rim, near, far):
    width = core.shape[1]
    return pl.pallas_call(
        rim_kernel,
        in_specs=[HBM_SPEC] + [VMEM_SPEC] * 3,
        out_specs=HBM_SPEC,
        out_shape=jax.ShapeDtypeStruct(core.shape, core.dtype),
        scratch_shapes=[pltpu.VMEM((2, 2 * HALO, width), BF16), pltpu.SemaphoreType.DMA((2,))],
        input_output_aliases={0: 0},
        compiler_params=pltpu.CompilerParams(vmem_limit_bytes=4 * MIB),
        name="add_rim",
    )(core, rim, near, far)


def body(student_rows, queries, keys_values, out_weight, teacher_rows, span_start, span_len):
    ctx_count = lax.axis_size("ctx")
    tp_lane = lax.axis_index("tp")
    tp_count = lax.axis_size("tp")
    teach_dev = teacher_rows.shape[0]
    heads_dev = queries.shape[1] // HD
    group_size = HEADS // KVH
    kv_dev = max(1, heads_dev // group_size)
    per_own = heads_dev // kv_dev
    groups = ctx_count // GROUP
    kv_first = tp_lane * heads_dev // group_size

    owns = [
        lax.dynamic_slice_in_dim(keys_values, (kv_first + kv) * HD, HD, 2) for kv in range(kv_dev)
    ]
    place = jnp.where(is_odd(), 0, teach_dev - HALO)
    edges = [
        lax.dynamic_slice_in_dim(teacher_rows, start, HALO, 0)
        for start in (place, teach_dev - HALO - place)
    ]
    owns, edges = lax.optimization_barrier((owns, edges))
    halos = [swapped(edges[0], "ctx", 1)]
    halos.append(odd_swapped(edges[1], "ctx"))
    both = jnp.stack(owns)
    side_all = swapped(both, "ctx", 2)
    other_all = swapped(jnp.stack([both, side_all], axis=1), "ctx", 1)
    stages = list(range(1, groups))
    lane_rows = heads_dev * HD
    out_weight = pltpu.with_memory_space_constraint(out_weight, pltpu.HBM)
    attended = []
    for kv in range(kv_dev):
        lifts = []
        for step in range(1, groups):
            lifts.append(swapped(owns[kv], "ctx", GROUP * step))
        state = attend_own(queries, kv, per_own, owns[kv], side_all[kv], other_all[kv])
        straight = jnp.stack(lifts)
        near = jnp.concatenate([straight, swapped(straight, "ctx", 2)])
        far = swapped(near, "ctx", 1)
        final = kv == kv_dev - 1
        parts = 2 if final and per_own % 2 == 0 else 1
        heads = per_own // parts
        for part in range(parts):
            first = part * heads
            fetch = None
            if final and part == 0:
                fetch = (tp_count - 1, kv * per_own * HD, per_own * HD, lane_rows, tp_count)
            result = attend_more(
                queries, kv, per_own, first, heads, stages, near, far, state, fetch, out_weight
            )
            if fetch:
                weight = result[1]
            attended.append((kv, part, (kv * per_own + first) * HD, result[0]))

    early, late, rest = [], [], []
    for kv, part, start, value in attended:
        (late if kv == kv_dev - 1 else early).append(((0, start, value.shape[1]), value))
    for step in range(1, tp_count):
        ring = [(i, (i + step) % tp_count) for i in range(tp_count)]
        for kv, part, start, value in attended:
            got = lax.ppermute(value, "tp", ring)
            if kv == kv_dev - 1 and step == tp_count - 1:
                rest.append(got)
            else:
                late.append(((step, start, value.shape[1]), got))
    spans = (span_start[None, :], span_len[None, :])
    base, target = project(
        base_kernel,
        2,
        [piece for piece, _ in early],
        [value for _, value in early],
        lane_rows,
        tp_count,
        [*spans, student_rows, teacher_rows, *halos],
        out_weight,
    )
    (base,) = project(
        add_kernel,
        1,
        [piece for piece, _ in late],
        [value for _, value in late],
        lane_rows,
        tp_count,
        [base],
        out_weight,
    )
    student_out, weighted, near, far = finish(
        span_start, span_len, base, target, teach_dev, rest, weight
    )
    near = swapped(near, "ctx", 1)
    far = odd_swapped(far, "ctx")
    core, rim = spread_out(span_start, span_len, weighted, teach_dev)
    return (student_out, add_rim(core, rim, near, far))


def solution(mesh):
    return jax.shard_map(
        body,
        mesh=mesh,
        in_specs=(
            P("ctx", "tp"),
            P("ctx", "tp"),
            P(None, "ctx", None),
            P(None, "tp"),
            P("ctx", "tp"),
            P("ctx"),
            P("ctx"),
        ),
        out_specs=(P("ctx", "tp"), P("ctx", "tp")),
        check_vma=False,
    )
```

time: 105 us -> 96.8 us (0.922)
  the two profiles are of different devices: /device:TPU:24 before, /device:TPU:25 now
where the time goes in v2:
time: 96.8 us; the launch traced here: 96.6 us
  Pallas kernels  48.7 us (50%)
  starting transfers between devices  24.6 us (25%)
  waiting for transfers between devices  19.8 us (20%)
  local copies, waits for them, and re-layouts  1.97 us (2%)
  between operations  1.1 us (1%)
    pallas_call x3, Pallas kernels, attend_more(): pl.pallas_call(functools.partial(more_kernel, heads, first, stages, fetch...  22 us
    ppermute x14, waiting for transfers between devices, swapped(): lax.ppermute(value, axis, [(source, source ^ bit) for source in range(cou...  18.7 us
    ppermute x14, starting transfers between devices, swapped(): lax.ppermute(value, axis, [(source, source ^ bit) for source in range(cou...  16.3 us
    pallas_call x2, Pallas kernels, project(): pl.pallas_call(functools.partial(kernel, pieces, lane_rows, tp_count, col...  14 us
    ppermute x2, starting transfers between devices, odd_swapped(): lax.ppermute(value, axis, [(i, i + 1 if i % 2 else i - 1) for i in range(...  5.48 us
    pallas_call x2, Pallas kernels, attend_own(): pl.pallas_call(functools.partial(own_kernel, heads), grid=(1,), in_specs=...  5.45 us
    pallas_call x1, Pallas kernels, finish(): pl.pallas_call(functools.partial(final_kernel, count, cols, teach), in_sp...  4.46 us
    ppermute x3, starting transfers between devices, body(): got = lax.ppermute(value, 'tp', ring)  2.88 us
  transfers between devices with their start and end apart: 19, of which 6 were waited for; matrix products, arithmetic and copies ran while one was open for 0% of the time, Pallas kernels for 45%

profile of v2, /device:TPU:25, one launch (start us, length us, event | category | flops | bytes accessed | tf_op | source)
XLA Modules:
  0.0 96.6 jit_solution(13345130148858575973)
XLA Ops:
  2.8 3.4 %collective-permute-start.4 = (bf16[2,256,128]{2,1,0:T(8,128)(2,1)S(1)}, bf16[2,256,128]{2,1,0:T(8,128)(2,1)S(1)}, u32[]{:S(2)}, u32[]{:S(2)}) collective-permute-start(bf16[2,256,128]{2,1,0:T(8,128)(2,1)S(1)} %get-tuple-element.22.own_ref), channel_id=1, source_target_pairs={{0,24},{2,26},{4,28},{6,30},{8,16},{10,18},{12,20},{14,22},{16,8},... | collective-permute-start | bytes 393224 | tf_op jit(solution)/shard_map/ppermute | solution.py:37
  6.5 2.1 %collective-permute-done.2 = bf16[2,256,128]{2,1,0:T(8,128)(2,1)S(1)} collective-permute-done((bf16[2,256,128]{2,1,0:T(8,128)(2,1)S(1)}, bf16[2,256,128]{2,1,0:T(8,128)(2,1)S(1)}, u32[]{:S(2)}, u32[]{:S(2)}) %collective-permute-start.2) | collective-permute-done | bytes 131104 | tf_op jit(solution)/shard_map/ppermute | solution.py:37
  8.6 1.2 %collective-permute-start.11 = (bf16[2,256,128]{2,1,0:T(8,128)(2,1)S(1)}, bf16[2,256,128]{2,1,0:T(8,128)(2,1)S(1)}, u32[]{:S(2)}, u32[]{:S(2)}) collective-permute-start(bf16[2,256,128]{2,1,0:T(8,128)(2,1)S(1)} %get-tuple-element.23.own_ref), channel_id=1, source_target_pairs={{0,24},{2,26},{4,28},{6,30},{8,16},{10,18},{12,20},{14,22},{16,8},... | collective-permute-start | bytes 393224 | tf_op jit(solution)/shard_map/ppermute | solution.py:37
  9.8 3.2 %collective-permute-done.3 = bf16[2,256,128]{2,1,0:T(8,128)(2,1)S(1)} collective-permute-done((bf16[2,256,128]{2,1,0:T(8,128)(2,1)S(1)}, bf16[2,256,128]{2,1,0:T(8,128)(2,1)S(1)}, u32[]{:S(2)}, u32[]{:S(2)}) %collective-permute-start.3) | collective-permute-done | bytes 131104 | tf_op jit(solution)/shard_map/ppermute | solution.py:37
  13.0 1.2 %collective-permute-start.7 = (bf16[2,2,256,128]{3,2,1,0:T(8,128)(2,1)S(1)}, bf16[2,2,256,128]{3,2,1,0:T(8,128)(2,1)S(1)}, u32[]{:S(2)}, u32[]{:S(2)}) collective-permute-start(bf16[2,2,256,128]{3,2,1,0:T(8,128)(2,1)S(1)} %get-tuple-element.47), channel_id=1, source_target_pairs={{0,4},{2,6},{4,0},{6,2},{8,12},{10,14},{12,8},{14,10},{16,20},{18,... | collective-permute-start | bytes 786440 | tf_op jit(solution)/shard_map/ppermute | solution.py:37
  15.4 9.6 %collective-permute-done.10 = bf16[2,256,128]{2,1,0:T(8,128)(2,1)S(1)} collective-permute-done((bf16[2,256,128]{2,1,0:T(8,128)(2,1)S(1)}, bf16[2,256,128]{2,1,0:T(8,128)(2,1)S(1)}, u32[]{:S(2)}, u32[]{:S(2)}) %collective-permute-start.10) | collective-permute-done | bytes 131104 | tf_op jit(solution)/shard_map/ppermute | solution.py:37
  25.0 1.3 %collective-permute-start.12 = (bf16[3,2,256,128]{3,2,1,0:T(8,128)(2,1)S(1)}, bf16[3,2,256,128]{3,2,1,0:T(8,128)(2,1)S(1)}, u32[]{:S(2)}, u32[]{:S(2)}) collective-permute-start(bf16[3,2,256,128]{3,2,1,0:T(8,128)(2,1)S(1)} %pad_maximum_fusion.4), channel_id=1, source_target_pairs={{0,4},{2,6},{4,0},{6,2},{8,12},{10,14},{12,8},{14,10},{16,20},{18,... | collective-permute-start | bytes 1179656 | tf_op jit(solution)/shard_map/ppermute | solution.py:37
  26.4 3.1 %collective-permute-start.8 = (bf16[2,2,2,256,128]{4,3,2,0,1:T(8,128)(2,1)S(1)}, bf16[2,2,2,256,128]{4,3,2,0,1:T(8,128)(2,1)S(1)}, u32[]{:S(2)}, u32[]{:S(2)}) collective-permute-start(bf16[2,2,2,256,128]{4,3,2,0,1:T(8,128)(2,1)S(1)} %pad_maximum_fusion.2), channel_id=1, source_target_pairs={{0,2},{2,0},{4,6},{6,4},{8,10},{10,8},{12,14},{14,12},{16,18},{18,... | collective-permute-start | bytes 1572872 | tf_op jit(solution)/shard_map/ppermute | solution.py:37
  29.5 2.4 %collective-permute-start.1 = (bf16[8,4096]{1,0:T(8,128)(2,1)S(1)}, bf16[8,4096]{1,0:T(8,128)(2,1)S(1)}, u32[]{:S(2)}, u32[]{:S(2)}) collective-permute-start(bf16[8,4096]{1,0:T(8,128)(2,1)S(1)} %get-tuple-element.21), channel_id=1, source_target_pairs={{2,4},{4,2},{6,8},{8,6},{10,12},{12,10},{14,16},{16,14},{18,20},{2... | collective-permute-start | bytes 196616 | tf_op jit(solution)/shard_map/ppermute | solution.py:30
  32.1 1.8 %collective-permute-start.6 = (bf16[6,2,256,128]{3,2,1,0:T(8,128)(2,1)S(1)}, bf16[6,2,256,128]{3,2,1,0:T(8,128)(2,1)S(1)}, u32[]{:S(2)}, u32[]{:S(2)}) collective-permute-start(bf16[6,2,256,128]{3,2,1,0:T(8,128)(2,1)S(1)} %pad_maximum_fusion.near_ref), channel_id=1, source_target_pairs={{0,2},{2,0},{4,6},{6,4},{8,10},{10,8},{12,14},{14,12},{16,18},{18,... | collective-permute-start | bytes 2359304 | tf_op jit(solution)/shard_map/ppermute | solution.py:37
  33.9 3.0 %collective-permute-done.12 = bf16[3,2,256,128]{3,2,1,0:T(8,128)(2,1)S(1)} collective-permute-done((bf16[3,2,256,128]{3,2,1,0:T(8,128)(2,1)S(1)}, bf16[3,2,256,128]{3,2,1,0:T(8,128)(2,1)S(1)}, u32[]{:S(2)}, u32[]{:S(2)}) %collective-permute-start.12) | collective-permute-done | bytes 393248 | tf_op jit(solution)/shard_map/ppermute | solution.py:37
  37.0 2.4 %collective-permute-start.13 = (bf16[6,2,256,128]{3,2,1,0:T(8,128)(2,1)S(1)}, bf16[6,2,256,128]{3,2,1,0:T(8,128)(2,1)S(1)}, u32[]{:S(2)}, u32[]{:S(2)}) collective-permute-start(bf16[6,2,256,128]{3,2,1,0:T(8,128)(2,1)S(1)} %pad_maximum_fusion.1.near_ref), channel_id=1, source_target_pairs={{0,2},{2,0},{4,6},{6,4},{8,10},{10,8},{12,14},{14,12},{16,18},{18,... | collective-permute-start | bytes 2359304 | tf_op jit(solution)/shard_map/ppermute | solution.py:37
  39.5 2.8 %attend_own.3 = (f32[256,128]{1,0:T(8,128)S(1)}, f32[8,256,256]{2,1,0:T(8,128)S(1)}) custom-call(bf16[256,2048]{1,0:T(8,128)(2,1)S(1)} %copy-done.2, bf16[2,256,128]{2,1,0:T(8,128)(2,1)S(1)} %get-tuple-element.23.own_ref, bf16[2,256,128]{2,1,0:T(8,128)(2,1)S(1)} %get-tuple-element.44.side_ref, bf16[2,2,256,128]{3,2,1,0:T(8,128)(2,1)S(1)} %get-tuple-element.40.other_ref), custom_call_target="tpu_custom_call" | custom-call | flops 2147483648 | bytes 2097152 | tf_op jit(solution)/shard_map/attend_own/pallas_call | solution.py:173
  42.2 2.7 %attend_own.2 = (f32[256,128]{1,0:T(8,128)S(1)}, f32[8,256,256]{2,1,0:T(8,128)S(1)}) custom-call(bf16[256,2048]{1,0:T(8,128)(2,1)S(1)} %copy-done.2, bf16[2,256,128]{2,1,0:T(8,128)(2,1)S(1)} %get-tuple-element.22.own_ref, bf16[2,256,128]{2,1,0:T(8,128)(2,1)S(1)} %get-tuple-element.45.side_ref, bf16[2,2,256,128]{3,2,1,0:T(8,128)(2,1)S(1)} %get-tuple-element.41.other_ref), custom_call_target="tpu_custom_call" | custom-call | flops 2147483648 | bytes 2097152 | tf_op jit(solution)/shard_map/attend_own/pallas_call | solution.py:173
  45.0 10.5 %attend_more.3.refs_4_ = bf16[256,1024]{1,0:T(8,128)(2,1)S(1)} custom-call(bf16[256,2048]{1,0:T(8,128)(2,1)S(1)} %copy-done.2, bf16[6,2,256,128]{3,2,1,0:T(8,128)(2,1)S(1)} %pad_maximum_fusion.near_ref, bf16[6,2,256,128]{3,2,1,0:T(8,128)(2,1)S(1)} %collective-permute-done.6.far_ref, f32[256,128]{1,0:T(8,128)S(1)} %get-tuple-element.24.refs_0_, ...), custom_call_target="tpu_custom_call" | custom-call | flops 6442450944 | bytes 2097152 | tf_op jit(solution)/shard_map/attend_more/pallas_call | solution.py:188
  55.5 1.3 %collective-permute-start.14 = (bf16[256,1024]{1,0:T(8,128)(2,1)S(1)}, bf16[256,1024]{1,0:T(8,128)(2,1)S(1)}, u32[]{:S(2)}, u32[]{:S(2)}) collective-permute-start(bf16[256,1024]{1,0:T(8,128)(2,1)S(1)} %attend_more.3.refs_4_), channel_id=1, source_target_pairs={{0,1},{1,0},{2,3},{3,2},{4,5},{5,4},{6,7},{7,6},{8,9},{9,8},{10,11... | collective-permute-start | bytes 1572872 | tf_op jit(solution)/shard_map/ppermute | solution.py:517
  56.8 5.6 %attend_more.4 = (bf16[256,512]{1,0:T(8,128)(2,1)S(1)}, bf16[1024,4096]{1,0:T(8,128)(2,1)S(1)}) custom-call(bf16[256,2048]{1,0:T(8,128)(2,1)S(1)} %copy-done.2, bf16[6,2,256,128]{3,2,1,0:T(8,128)(2,1)S(1)} %pad_maximum_fusion.1.near_ref, bf16[6,2,256,128]{3,2,1,0:T(8,128)(2,1)S(1)} %collective-permute-done.13.far_ref, ...), custom_call_target="tpu_custom_call" | custom-call | flops 3221225472 | bytes 2097152 | tf_op jit(solution)/shard_map/attend_more/pallas_call | solution.py:188
  62.8 5.9 %attend_more.5.refs_1_ = bf16[256,512]{1,0:T(8,128)(2,1)S(1)} custom-call(bf16[256,2048]{1,0:T(8,128)(2,1)S(1)} %copy-done.2, bf16[6,2,256,128]{3,2,1,0:T(8,128)(2,1)S(1)} %pad_maximum_fusion.1.near_ref, bf16[6,2,256,128]{3,2,1,0:T(8,128)(2,1)S(1)} %collective-permute-done.13.far_ref, f32[256,128]{1,0:T(8,128)S(1)} %get-tuple-element.27.refs_0_, ...), custom_call_target="tpu_custom_call" | custom-call | flops 3221225472 | bytes 2097152 | tf_op jit(solution)/shard_map/attend_more/pallas_call | solution.py:188
  68.7 1.3 %collective-permute-start.16 = (bf16[256,512]{1,0:T(8,128)(2,1)S(1)}, bf16[256,512]{1,0:T(8,128)(2,1)S(1)}, u32[]{:S(2)}, u32[]{:S(2)}) collective-permute-start(bf16[256,512]{1,0:T(8,128)(2,1)S(1)} %attend_more.5.refs_1_), channel_id=1, source_target_pairs={{0,1},{1,0},{2,3},{3,2},{4,5},{5,4},{6,7},{7,6},{8,9},{9,8},{10,11... | collective-permute-start | bytes 786440 | tf_op jit(solution)/shard_map/ppermute | solution.py:517
  70.0 6.4 %shard_map.86 = (f32[256,4096]{1,0:T(8,128)S(1)}, f32[256,4096]{1,0:T(8,128)S(1)}) custom-call(s32[1,256]{1,0:T(1,128)S(1)} %bitcast.23, s32[1,256]{1,0:T(1,128)S(1)} %bitcast.26, bf16[256,4096]{1,0:T(8,128)(2,1)S(1)} %copy-done.1, bf16[384,4096]{1,0:T(8,128)(2,1)S(1)} %copy-done, bf16[8,4096]{1,0:T(8,128)(2,1)S(1)} %collective-permute-done.refs_2_, ...), custom_call_target="tpu_custom_call" | custom-call | flops 2147483648 | bytes 18874368 | tf_op jit(solution)/shard_map/pallas_call | solution.py:309
  76.4 7.6 %shard_map.87.base_ref = f32[256,4096]{1,0:T(8,128)S(1)} custom-call(f32[256,4096]{1,0:T(8,128)S(1)} %get-tuple-element.26.base_ref, bf16[256,512]{1,0:T(8,128)(2,1)S(1)} %get-tuple-element.29.refs_0_, bf16[256,512]{1,0:T(8,128)(2,1)S(1)} %attend_more.5.refs_1_, bf16[256,1024]{1,0:T(8,128)(2,1)S(1)} %collective-permute-done.14.refs_2_, ...), custom_call_target="tpu_custom_call" | custom-call | flops 4294967296 | bytes 27262976 | tf_op jit(solution)/shard_map/pallas_call | solution.py:309
  84.0 4.5 %finish.1 = (bf16[256,4096]{1,0:T(8,128)(2,1)}, bf16[256,4096]{1,0:T(8,128)(2,1)S(1)}, bf16[8,4096]{1,0:T(8,128)(2,1)S(1)}, bf16[8,4096]{1,0:T(8,128)(2,1)S(1)}) custom-call(s32[1,256]{1,0:T(1,128)S(1)} %bitcast.24, s32[1,256]{1,0:T(1,128)S(1)} %bitcast.27, f32[256,4096]{1,0:T(8,128)S(1)} %shard_map.87.base_ref, ...), custom_call_target="tpu_custom_call" | custom-call | flops 2147483648 | bytes 18874368 | tf_op jit(solution)/shard_map/finish/pallas_call | solution.py:362
  89.4 3.0 %collective-permute-start.18 = (bf16[8,4096]{1,0:T(8,128)(2,1)S(1)}, bf16[8,4096]{1,0:T(8,128)(2,1)S(1)}, u32[]{:S(2)}, u32[]{:S(2)}) collective-permute-start(bf16[8,4096]{1,0:T(8,128)(2,1)S(1)} %get-tuple-element.37), channel_id=1, source_target_pairs={{2,4},{4,2},{6,8},{8,6},{10,12},{12,10},{14,16},{16,14},{18,20},{2... | collective-permute-start | bytes 196616 | tf_op jit(solution)/shard_map/ppermute | solution.py:30
  92.5 2.1 %spread_out.1 = (bf16[384,4096]{1,0:T(8,128)(2,1)}, f32[32,4096]{1,0:T(8,128)S(1)}) custom-call(s32[1,256]{1,0:T(1,128)S(1)} %bitcast.25, s32[1,256]{1,0:T(1,128)S(1)} %bitcast.28, bf16[256,4096]{1,0:T(8,128)(2,1)S(1)} %get-tuple-element.33.weighted_ref), custom_call_target="tpu_custom_call" | custom-call | flops 805306368 | bytes 3145728 | tf_op jit(solution)/shard_map/spread_out/pallas_call | solution.py:407
  (44 shorter events, 7.2 us)
Async XLA Ops:
  2.5 6.0 %collective-permute-start.2 = (bf16[2,256,128]{2,1,0:T(8,128)(2,1)S(1)}, bf16[2,256,128]{2,1,0:T(8,128)(2,1)S(1)}, u32[]{:S(2)}, u32[]{:S(2)}) collective-permute-start(bf16[2,256,128]{2,1,0:T(8,128)(2,1)S(1)} %get-tuple-element.22.own_ref), channel_id=1, source_target_pairs={{0,8},{2,10},{4,12},{6,14},{8,0},{10,2},{12,4},{14,6},{16,24},{18,... | collective-permute-start | bytes 393224 | tf_op jit(solution)/shard_map/ppermute | solution.py:37
  2.8 10.2 %collective-permute-start.3 = (bf16[2,256,128]{2,1,0:T(8,128)(2,1)S(1)}, bf16[2,256,128]{2,1,0:T(8,128)(2,1)S(1)}, u32[]{:S(2)}, u32[]{:S(2)}) collective-permute-start(bf16[2,256,128]{2,1,0:T(8,128)(2,1)S(1)} %get-tuple-element.22.own_ref), channel_id=1, source_target_pairs={{0,16},{2,18},{4,20},{6,22},{8,24},{10,26},{12,28},{14,30},{16,0},... | collective-permute-start | bytes 393224 | tf_op jit(solution)/shard_map/ppermute | solution.py:37
  2.8 11.4 %collective-permute-start.4 = (bf16[2,256,128]{2,1,0:T(8,128)(2,1)S(1)}, bf16[2,256,128]{2,1,0:T(8,128)(2,1)S(1)}, u32[]{:S(2)}, u32[]{:S(2)}) collective-permute-start(bf16[2,256,128]{2,1,0:T(8,128)(2,1)S(1)} %get-tuple-element.22.own_ref), channel_id=1, source_target_pairs={{0,24},{2,26},{4,28},{6,30},{8,16},{10,18},{12,20},{14,22},{16,8},... | collective-permute-start | bytes 393224 | tf_op jit(solution)/shard_map/ppermute | solution.py:37
  6.2 9.2 %collective-permute-start.9 = (bf16[2,256,128]{2,1,0:T(8,128)(2,1)S(1)}, bf16[2,256,128]{2,1,0:T(8,128)(2,1)S(1)}, u32[]{:S(2)}, u32[]{:S(2)}) collective-permute-start(bf16[2,256,128]{2,1,0:T(8,128)(2,1)S(1)} %get-tuple-element.23.own_ref), channel_id=1, source_target_pairs={{0,8},{2,10},{4,12},{6,14},{8,0},{10,2},{12,4},{14,6},{16,24},{18,... | collective-permute-start | bytes 393224 | tf_op jit(solution)/shard_map/ppermute | solution.py:37
  6.2 18.8 %collective-permute-start.10 = (bf16[2,256,128]{2,1,0:T(8,128)(2,1)S(1)}, bf16[2,256,128]{2,1,0:T(8,128)(2,1)S(1)}, u32[]{:S(2)}, u32[]{:S(2)}) collective-permute-start(bf16[2,256,128]{2,1,0:T(8,128)(2,1)S(1)} %get-tuple-element.23.own_ref), channel_id=1, source_target_pairs={{0,16},{2,18},{4,20},{6,22},{8,24},{10,26},{12,28},{14,30},{16,0},... | collective-permute-start | bytes 393224 | tf_op jit(solution)/shard_map/ppermute | solution.py:37
  8.6 16.4 %collective-permute-start.11 = (bf16[2,256,128]{2,1,0:T(8,128)(2,1)S(1)}, bf16[2,256,128]{2,1,0:T(8,128)(2,1)S(1)}, u32[]{:S(2)}, u32[]{:S(2)}) collective-permute-start(bf16[2,256,128]{2,1,0:T(8,128)(2,1)S(1)} %get-tuple-element.23.own_ref), channel_id=1, source_target_pairs={{0,24},{2,26},{4,28},{6,30},{8,16},{10,18},{12,20},{14,22},{16,8},... | collective-permute-start | bytes 393224 | tf_op jit(solution)/shard_map/ppermute | solution.py:37
  13.0 13.3 %collective-permute-start.7 = (bf16[2,2,256,128]{3,2,1,0:T(8,128)(2,1)S(1)}, bf16[2,2,256,128]{3,2,1,0:T(8,128)(2,1)S(1)}, u32[]{:S(2)}, u32[]{:S(2)}) collective-permute-start(bf16[2,2,256,128]{3,2,1,0:T(8,128)(2,1)S(1)} %get-tuple-element.47), channel_id=1, source_target_pairs={{0,4},{2,6},{4,0},{6,2},{8,12},{10,14},{12,8},{14,10},{16,20},{18,... | collective-permute-start | bytes 786440 | tf_op jit(solution)/shard_map/ppermute | solution.py:37
  14.3 17.7 %collective-permute-start.5 = (bf16[3,2,256,128]{3,2,1,0:T(8,128)(2,1)S(1)}, bf16[3,2,256,128]{3,2,1,0:T(8,128)(2,1)S(1)}, u32[]{:S(2)}, u32[]{:S(2)}) collective-permute-start(bf16[3,2,256,128]{3,2,1,0:T(8,128)(2,1)S(1)} %pad_maximum_fusion.3), channel_id=1, source_target_pairs={{0,4},{2,6},{4,0},{6,2},{8,12},{10,14},{12,8},{14,10},{16,20},{18,... | collective-permute-start | bytes 1179656 | tf_op jit(solution)/shard_map/ppermute | solution.py:37
  25.0 14.5 %copy-start.2 = (bf16[256,2048]{1,0:T(8,128)(2,1)S(1)}, bf16[256,2048]{1,0:T(8,128)(2,1)}, u32[]{:S(2)}) copy-start(bf16[256,2048]{1,0:T(8,128)(2,1)} %query_ref.9) | copy-start | bytes 3145732
  25.0 11.9 %collective-permute-start.12 = (bf16[3,2,256,128]{3,2,1,0:T(8,128)(2,1)S(1)}, bf16[3,2,256,128]{3,2,1,0:T(8,128)(2,1)S(1)}, u32[]{:S(2)}, u32[]{:S(2)}) collective-permute-start(bf16[3,2,256,128]{3,2,1,0:T(8,128)(2,1)S(1)} %pad_maximum_fusion.4), channel_id=1, source_target_pairs={{0,4},{2,6},{4,0},{6,2},{8,12},{10,14},{12,8},{14,10},{16,20},{18,... | collective-permute-start | bytes 1179656 | tf_op jit(solution)/shard_map/ppermute | solution.py:37
  26.4 13.0 %collective-permute-start.8 = (bf16[2,2,2,256,128]{4,3,2,0,1:T(8,128)(2,1)S(1)}, bf16[2,2,2,256,128]{4,3,2,0,1:T(8,128)(2,1)S(1)}, u32[]{:S(2)}, u32[]{:S(2)}) collective-permute-start(bf16[2,2,2,256,128]{4,3,2,0,1:T(8,128)(2,1)S(1)} %pad_maximum_fusion.2), channel_id=1, source_target_pairs={{0,2},{2,0},{4,6},{6,4},{8,10},{10,8},{12,14},{14,12},{16,18},{18,... | collective-permute-start | bytes 1572872 | tf_op jit(solution)/shard_map/ppermute | solution.py:37
  29.5 40.5 %collective-permute-start = (bf16[8,4096]{1,0:T(8,128)(2,1)S(1)}, bf16[8,4096]{1,0:T(8,128)(2,1)S(1)}, u32[]{:S(2)}, u32[]{:S(2)}) collective-permute-start(bf16[8,4096]{1,0:T(8,128)(2,1)S(1)} %get-tuple-element.20), channel_id=1, source_target_pairs={{0,2},{2,0},{4,6},{6,4},{8,10},{10,8},{12,14},{14,12},{16,18},{18,... | collective-permute-start | bytes 196616 | tf_op jit(solution)/shard_map/ppermute | solution.py:37
  29.5 40.4 %collective-permute-start.1 = (bf16[8,4096]{1,0:T(8,128)(2,1)S(1)}, bf16[8,4096]{1,0:T(8,128)(2,1)S(1)}, u32[]{:S(2)}, u32[]{:S(2)}) collective-permute-start(bf16[8,4096]{1,0:T(8,128)(2,1)S(1)} %get-tuple-element.21), channel_id=1, source_target_pairs={{2,4},{4,2},{6,8},{8,6},{10,12},{12,10},{14,16},{16,14},{18,20},{2... | collective-permute-start | bytes 196616 | tf_op jit(solution)/shard_map/ppermute | solution.py:30
  32.1 12.9 %collective-permute-start.6 = (bf16[6,2,256,128]{3,2,1,0:T(8,128)(2,1)S(1)}, bf16[6,2,256,128]{3,2,1,0:T(8,128)(2,1)S(1)}, u32[]{:S(2)}, u32[]{:S(2)}) collective-permute-start(bf16[6,2,256,128]{3,2,1,0:T(8,128)(2,1)S(1)} %pad_maximum_fusion.near_ref), channel_id=1, source_target_pairs={{0,2},{2,0},{4,6},{6,4},{8,10},{10,8},{12,14},{14,12},{16,18},{18,... | collective-permute-start | bytes 2359304 | tf_op jit(solution)/shard_map/ppermute | solution.py:37
  37.0 19.8 %collective-permute-start.13 = (bf16[6,2,256,128]{3,2,1,0:T(8,128)(2,1)S(1)}, bf16[6,2,256,128]{3,2,1,0:T(8,128)(2,1)S(1)}, u32[]{:S(2)}, u32[]{:S(2)}) collective-permute-start(bf16[6,2,256,128]{3,2,1,0:T(8,128)(2,1)S(1)} %pad_maximum_fusion.1.near_ref), channel_id=1, source_target_pairs={{0,2},{2,0},{4,6},{6,4},{8,10},{10,8},{12,14},{14,12},{16,18},{18,... | collective-permute-start | bytes 2359304 | tf_op jit(solution)/shard_map/ppermute | solution.py:37
  55.5 20.9 %collective-permute-start.14 = (bf16[256,1024]{1,0:T(8,128)(2,1)S(1)}, bf16[256,1024]{1,0:T(8,128)(2,1)S(1)}, u32[]{:S(2)}, u32[]{:S(2)}) collective-permute-start(bf16[256,1024]{1,0:T(8,128)(2,1)S(1)} %attend_more.3.refs_4_), channel_id=1, source_target_pairs={{0,1},{1,0},{2,3},{3,2},{4,5},{5,4},{6,7},{7,6},{8,9},{9,8},{10,11... | collective-permute-start | bytes 1572872 | tf_op jit(solution)/shard_map/ppermute | solution.py:517
  62.4 7.6 %copy-start = (bf16[384,4096]{1,0:T(8,128)(2,1)S(1)}, bf16[384,4096]{1,0:T(8,128)(2,1)}, u32[]{:S(2)}) copy-start(bf16[384,4096]{1,0:T(8,128)(2,1)} %refs_1_.1) | copy-start | bytes 9437188
  62.4 7.6 %copy-start.1 = (bf16[256,4096]{1,0:T(8,128)(2,1)S(1)}, bf16[256,4096]{1,0:T(8,128)(2,1)}, u32[]{:S(2)}) copy-start(bf16[256,4096]{1,0:T(8,128)(2,1)} %refs_0_.1) | copy-start | bytes 6291460
  62.4 7.6 %copy-start.3 = (s32[256]{0:T(256)S(1)}, s32[256]{0:T(256)}, u32[]{:S(2)}) copy-start(s32[256]{0:T(256)} %param.12) | copy-start | bytes 3076
  62.4 7.5 %copy-start.4 = (s32[256]{0:T(256)S(1)}, s32[256]{0:T(256)}, u32[]{:S(2)}) copy-start(s32[256]{0:T(256)} %param.13) | copy-start | bytes 3076
  62.4 21.5 %collective-permute-start.15 = (bf16[256,512]{1,0:T(8,128)(2,1)S(1)}, bf16[256,512]{1,0:T(8,128)(2,1)S(1)}, u32[]{:S(2)}, u32[]{:S(2)}) collective-permute-start(bf16[256,512]{1,0:T(8,128)(2,1)S(1)} %get-tuple-element.29.refs_0_), channel_id=1, source_target_pairs={{0,1},{1,0},{2,3},{3,2},{4,5},{5,4},{6,7},{7,6},{8,9},{9,8},{10,11... | collective-permute-start | bytes 786440 | tf_op jit(solution)/shard_map/ppermute | solution.py:517
  68.7 15.3 %collective-permute-start.16 = (bf16[256,512]{1,0:T(8,128)(2,1)S(1)}, bf16[256,512]{1,0:T(8,128)(2,1)S(1)}, u32[]{:S(2)}, u32[]{:S(2)}) collective-permute-start(bf16[256,512]{1,0:T(8,128)(2,1)S(1)} %attend_more.5.refs_1_), channel_id=1, source_target_pairs={{0,1},{1,0},{2,3},{3,2},{4,5},{5,4},{6,7},{7,6},{8,9},{9,8},{10,11... | collective-permute-start | bytes 786440 | tf_op jit(solution)/shard_map/ppermute | solution.py:517
  88.5 6.1 %collective-permute-start.17 = (bf16[8,4096]{1,0:T(8,128)(2,1)S(1)}, bf16[8,4096]{1,0:T(8,128)(2,1)S(1)}, u32[]{:S(2)}, u32[]{:S(2)}) collective-permute-start(bf16[8,4096]{1,0:T(8,128)(2,1)S(1)} %get-tuple-element.36), channel_id=1, source_target_pairs={{0,2},{2,0},{4,6},{6,4},{8,10},{10,8},{12,14},{14,12},{16,18},{18,... | collective-permute-start | bytes 196616 | tf_op jit(solution)/shard_map/ppermute | solution.py:37
  89.4 6.3 %collective-permute-start.18 = (bf16[8,4096]{1,0:T(8,128)(2,1)S(1)}, bf16[8,4096]{1,0:T(8,128)(2,1)S(1)}, u32[]{:S(2)}, u32[]{:S(2)}) collective-permute-start(bf16[8,4096]{1,0:T(8,128)(2,1)S(1)} %get-tuple-element.37), channel_id=1, source_target_pairs={{2,4},{4,2},{6,8},{8,6},{10,12},{12,10},{14,16},{16,14},{18,20},{2... | collective-permute-start | bytes 196616 | tf_op jit(solution)/shard_map/ppermute | solution.py:30

commit v3 on v2

--- a/solution.py
+++ b/solution.py
@@ -21,7 +21,7 @@
 exp2_scale = math.log2(math.e) / math.sqrt(HD)
 
 ATTN_VMEM = 9 * 1024 * 1024
-PROJECT_VMEM = 20 * 1024 * 1024
+PROJECT_VMEM = 6 * 1024 * 1024
 FINISH_VMEM = 8 * 1024 * 1024
 
 
@@ -105,45 +105,53 @@
     return pl.ds(pl.multiple_of(lane * lane_rows + start, HD), depth)
 
 
-def more_kernel(heads, first, stages, fetch, query_ref, near_ref, far_ref, *refs):
-    (peak_in, accum_in), refs = refs[:2], refs[2:]
-    copy = None
-    if fetch:
-        weight_hbm, out_ref, weight_ref, peak_ref, accum_ref, sem = refs
-        copy = pltpu.make_async_copy(weight_hbm.at[weight_rows(*fetch), :], weight_ref, sem)
+def fetches(blocks, lanes, weight_hbm, refs, sems):
+    return [
+        pltpu.make_async_copy(weight_hbm.at[weight_rows(*block, *lanes), :], ref, sems.at[index])
+        for index, (block, ref) in enumerate(zip(blocks, refs))
+    ]
+
+
+def more_kernel(heads, first, turns, fetch, lanes, query_ref, *refs):
+    parts = [(stages, refs[4 * k : 4 * k + 4]) for k, stages in enumerate(turns)]
+    refs = refs[4 * len(turns) :]
+    (peak_in, accum_in, weight_hbm, out_ref), refs = refs[:4], refs[4:]
+    peak_ref, accum_ref, sems = refs[-3:]
+    copies = fetches(fetch, lanes, weight_hbm, refs[:-3], sems)
+    for copy in copies:
         copy.start()
-    else:
-        out_ref, peak_ref, accum_ref = refs
     for head in range(heads):
         accum_ref[head] = accum_in[first + head]
         peak_ref[:, head : head + 1] = peak_in[:, first + head : first + head + 1]
     group = lax.div(lax.axis_index("ctx"), GROUP)
-    count = len(stages)
-
-    def step(index, carry):
-        @pl.when((group ^ (index + stages[0])) < group)
-        def _():
-            pieces = [ref.at[at] for ref in (near_ref, far_ref) for at in (index, index + count)]
-            state = [(peak_ref[:, head : head + 1], accum_ref.at[head]) for head in range(heads)]
-            attention_step(
-                query_ref,
-                heads,
-                [p[0] for p in pieces],
-                [p[1] for p in pieces],
-                state,
-                None,
-                None,
-                peak_ref,
-                accum_ref,
-            )
-
-        return carry
-
-    lax.fori_loop(0, count, step, 0)
+    for stages, blocks in parts:
+
+        def step(index, carry, stages=stages, blocks=blocks):
+            @pl.when((group ^ (index + stages[0])) < group)
+            def _():
+                pieces = [ref.at[index] for ref in blocks]
+                state = [
+                    (peak_ref[:, head : head + 1], accum_ref.at[head]) for head in range(heads)
+                ]
+                attention_step(
+                    query_ref,
+                    heads,
+                    [p[0] for p in pieces],
+                    [p[1] for p in pieces],
+                    state,
+                    None,
+                    None,
+                    peak_ref,
+                    accum_ref,
+                )
+
+            return carry
+
+        lax.fori_loop(0, len(stages), step, 0)
     for head in range(heads):
         accum = accum_ref[head]
         out_ref[:, head * HD : (head + 1) * HD] = (accum[:, :HD] / accum[:, HD:]).astype(BF16)
-    if copy is not None:
+    for copy in copies:
         copy.wait()
 
 
@@ -182,24 +190,28 @@
     )(queries, own, side, other)
 
 
-def attend_more(queries, kv, per_own, first, heads, stages, near, far, state, fetch, out_weight):
+def fetched(fetch, out_weight):
+    return [pltpu.VMEM((depth, out_weight.shape[1]), BF16) for _, _, depth in fetch]
+
+
+def attend_more(
+    queries, kv, per_own, first, heads, turns, blocks, state, fetch, lanes, out_weight
+):
     rows = queries.shape[0]
-    extra = [out_weight] if fetch else []
-    return pl.pallas_call(
-        functools.partial(more_kernel, heads, first, stages, fetch),
+    return pl.pallas_call(
+        functools.partial(more_kernel, heads, first, turns, fetch, lanes),
         grid=(1,),
         in_specs=[query_spec(rows, heads, (kv * per_own + first) // heads)]
-        + [VMEM_SPEC] * 4
-        + [HBM_SPEC] * len(extra),
-        out_specs=[VMEM_SPEC] * (1 + len(extra)),
-        out_shape=[jax.ShapeDtypeStruct((rows, heads * HD), BF16)]
-        + [pltpu.VMEM((fetch[2], out_weight.shape[1]), BF16) for _ in extra],
+        + [VMEM_SPEC] * (len(blocks) + 2)
+        + [HBM_SPEC],
+        out_specs=[VMEM_SPEC] * (1 + len(fetch)),
+        out_shape=[jax.ShapeDtypeStruct((rows, heads * HD), BF16)] + fetched(fetch, out_weight),
         scratch_shapes=[pltpu.VMEM(*shape) for shape in state_shapes(rows, heads)]
-        + [pltpu.SemaphoreType.DMA] * len(extra),
+        + [pltpu.SemaphoreType.DMA((max(1, len(fetch)),))],
         compiler_params=pltpu.CompilerParams(vmem_limit_bytes=ATTN_VMEM),
-        cost_estimate=attention_cost(rows, heads, 2 * near.shape[0] * rows),
+        cost_estimate=attention_cost(rows, heads, GROUP * len(sum(turns, [])) * rows),
         name="attend_more",
-    )(queries, near, far, *state, *extra)
+    )(queries, *blocks, *state, out_weight)
 
 
 def upright(row):
@@ -226,102 +238,98 @@
     return jnp.where(below, index - HALO, index + teach)
 
 
-def streamed(pieces, piece_refs, weight_hbm, lane_rows, tp_count, cols, slots, buf, sems):
-    steps = weight_hbm.shape[1] // cols
-
-    def loads(step):
-        copies, at = [], 0
-        for index, (lane_step, start, depth) in enumerate(pieces):
-            copies.append(
-                pltpu.make_async_copy(
-                    weight_hbm.at[
-                        weight_rows(lane_step, start, depth, lane_rows, tp_count),
-                        pl.ds(step * cols, cols),
-                    ],
-                    buf.at[step % slots, pl.ds(at, depth), :],
-                    sems.at[step % slots, index],
-                )
-            )
-            at += depth
-        return copies
-
-    def begin(step):
-        for load in loads(step):
-            load.start()
-
-    def product(step, total):
-        at = 0
-        for load in loads(step):
-            load.wait()
-        for (_, _, depth), ref in zip(pieces, piece_refs):
-            block = buf[step % slots, at : at + depth, :]
-            total += jnp.dot(ref[...], block, preferred_element_type=F32)
-            at += depth
-        if step + slots < steps:
-            begin(step + slots)
-        return total
-
-    for step in range(min(slots, steps)):
-        begin(step)
-    return product
-
-
-def base_kernel(pieces, lane_rows, tp_count, cols, slots, start_ref, len_ref, *refs):
+def joined(pieces, piece_refs):
+    runs = []
+    for (block, start, depth), ref in zip(pieces, piece_refs):
+        if runs and runs[-1][0] == block and runs[-1][1] + runs[-1][2] == start:
+            runs[-1][2] += depth
+            runs[-1][3].append(ref)
+        else:
+            runs.append([block, start, depth, [ref]])
+    return [
+        (block, start, depth, jnp.concatenate([ref[...] for ref in refs], axis=1))
+        for block, start, depth, refs in runs
+    ]
+
+
+def product(runs, weight_refs, span, total):
+    for block, start, depth, value in runs:
+        rows = weight_refs[block][start : start + depth, span]
+        total += jnp.dot(value, rows, preferred_element_type=F32)
+    return total
+
+
+def base_kernel(pieces, cols, start_ref, len_ref, *refs):
     student_ref, teacher_ref, near_ref, far_ref = refs[:4]
-    piece_refs = refs[4 : 4 + len(pieces)]
-    weight_hbm, base_ref, target_ref, buf, sems = refs[4 + len(pieces) :]
-    product = streamed(
-        pieces, piece_refs, weight_hbm, lane_rows, tp_count, cols, slots, buf, sems
-    )
+    piece_refs, weight_refs = refs[4 : 4 + len(pieces)], refs[4 + len(pieces) : -2]
+    base_ref, target_ref = refs[-2:]
     rows, width = student_ref.shape
     teach = teacher_ref.shape[0]
     starts = upright(start_ref[...]) - lax.axis_index("ctx") * teach
     lens = upright(len_ref[...])
     inner = member_of(starts, lens, iota((rows, teach), 1))
     outer = member_of(starts, lens, rim_rows(iota((rows, 2 * HALO), 1), teach))
-    counts = lens.astype(F32)
+    share = 1.0 / lens.astype(F32)
+    runs = joined(pieces, piece_refs)
     for step in range(width // cols):
         span = slice(step * cols, (step + 1) * cols)
         target = jnp.dot(inner, teacher_ref[:, span], preferred_element_type=F32)
         halo = [ref[:, span].astype(F32) for ref in (near_ref, far_ref)]
         halo = jnp.concatenate(halo, axis=0).astype(BF16)
         target += jnp.dot(outer, halo, preferred_element_type=F32)
-        target_ref[:, span] = target / counts
-        base_ref[:, span] = product(step, student_ref[:, span].astype(F32))
-
-
-def add_kernel(pieces, lane_rows, tp_count, cols, slots, base_ref, *refs):
-    piece_refs = refs[: len(pieces)]
-    weight_hbm, out_ref, buf, sems = refs[len(pieces) :]
-    product = streamed(
-        pieces, piece_refs, weight_hbm, lane_rows, tp_count, cols, slots, buf, sems
-    )
-    for step in range(base_ref.shape[1] // cols):
-        span = slice(step * cols, (step + 1) * cols)
-        out_ref[:, span] = product(step, base_ref[:, span])
-
-
-def project(kernel, outputs, pieces, values, lane_rows, tp_count, inputs, out_weight):
-    width = out_weight.shape[1]
-    cols, slots = min(512, width), 4
+        target_ref[:, span] = target * share
+        total = student_ref[:, span].astype(F32)
+        base_ref[:, span] = product(runs, weight_refs, span, total)
+
+
+def late_kernel(pieces, count, fetch, lanes, cols, base_ref, *refs):
+    piece_refs, weight_refs = refs[: len(pieces)], refs[len(pieces) : len(pieces) + count]
+    weight_hbm, out_ref, last_ref, sems = refs[len(pieces) + count :]
+    copies = fetches(fetch, lanes, weight_hbm, [last_ref], sems)
+    for copy in copies:
+        copy.start()
+    runs = joined(pieces, piece_refs)
+    for start in range(0, base_ref.shape[1], cols):
+        span = slice(start, start + cols)
+        out_ref[:, span] = product(runs, weight_refs, span, base_ref[:, span])
+    for copy in copies:
+        copy.wait()
+
+
+def product_cost(rows, width, pieces):
     depth = sum(piece[2] for piece in pieces)
-    rows = inputs[-1].shape[0] if len(inputs) == 1 else inputs[2].shape[0]
-    return pl.pallas_call(
-        functools.partial(kernel, pieces, lane_rows, tp_count, cols, slots),
-        in_specs=[VMEM_SPEC] * (len(inputs) + len(values)) + [HBM_SPEC],
-        out_specs=[VMEM_SPEC] * outputs,
-        out_shape=[jax.ShapeDtypeStruct((rows, width), F32)] * outputs,
-        scratch_shapes=[
-            pltpu.VMEM((slots, max(depth, 16), cols), BF16),
-            pltpu.SemaphoreType.DMA((slots, max(1, len(pieces)))),
-        ],
+    return pl.CostEstimate(
+        flops=2 * rows * width * depth,
+        transcendentals=0,
+        bytes_accessed=2 * depth * width + 10 * rows * width,
+    )
+
+
+def project_base(pieces, values, weights, starts, lens, student, teacher, halos):
+    rows, width = student.shape
+    return pl.pallas_call(
+        functools.partial(base_kernel, pieces, min(512, width)),
+        in_specs=[VMEM_SPEC] * (6 + len(values) + len(weights)),
+        out_specs=[VMEM_SPEC] * 2,
+        out_shape=[jax.ShapeDtypeStruct((rows, width), F32)] * 2,
         compiler_params=pltpu.CompilerParams(vmem_limit_bytes=PROJECT_VMEM),
-        cost_estimate=pl.CostEstimate(
-            flops=2 * rows * width * depth,
-            transcendentals=0,
-            bytes_accessed=2 * depth * width + 10 * rows * width,
-        ),
-    )(*inputs, *values, out_weight)
+        cost_estimate=product_cost(rows, width, pieces),
+        name="project_base",
+    )(starts[None, :], lens[None, :], student, teacher, *halos, *values, *weights)
+
+
+def project_late(pieces, values, weights, base, fetch, lanes, out_weight):
+    rows, width = base.shape
+    return pl.pallas_call(
+        functools.partial(late_kernel, pieces, len(weights), fetch, lanes, min(512, width)),
+        in_specs=[VMEM_SPEC] * (1 + len(values) + len(weights)) + [HBM_SPEC],
+        out_specs=[VMEM_SPEC] * 2,
+        out_shape=[jax.ShapeDtypeStruct((rows, width), F32)] + fetched(fetch, out_weight),
+        scratch_shapes=[pltpu.SemaphoreType.DMA((1,))],
+        compiler_params=pltpu.CompilerParams(vmem_limit_bytes=PROJECT_VMEM),
+        cost_estimate=product_cost(rows, width, pieces),
+        name="project_late",
+    )(base, *values, *weights, out_weight)
 
 
 def final_kernel(count, cols, teach, start_ref, len_ref, base_ref, target_ref, *refs):
@@ -330,23 +338,20 @@
     rows, width = base_ref.shape
     starts, lens = start_ref[...] - lax.axis_index("ctx") * teach, len_ref[...]
     outer_t = member_of(starts, lens, rim_rows(iota((2 * HALO, rows), 0), teach))
-    counts = upright(lens).astype(F32)
+    share = 1.0 / upright(lens).astype(F32)
+    value = jnp.concatenate([ref[...] for ref in piece_refs], axis=1)
     copies = []
     for index, start in enumerate(range(0, width, cols)):
         span = slice(start, start + cols)
         total = base_ref[:, span]
-        at = 0
-        for ref in piece_refs:
-            block = weight_ref[at : at + ref.shape[1], span]
-            total += jnp.dot(ref[...], block, preferred_element_type=F32)
-            at += ref.shape[1]
+        total += jnp.dot(value, weight_ref[:, span], preferred_element_type=F32)
         student_buf[:, span] = total.astype(BF16)
         copy = pltpu.make_async_copy(
             student_buf.at[:, span], student_out.at[:, span], sems.at[index]
         )
         copy.start()
         copies.append(copy)
-        weighted = ((total - target_ref[:, span]) / counts).astype(BF16)
+        weighted = ((total - target_ref[:, span]) * share).astype(BF16)
         weighted_ref[:, span] = weighted
         edge = jnp.dot(outer_t, weighted, preferred_element_type=F32)
         near_ref[:, span] = edge[:HALO].astype(BF16)
@@ -475,14 +480,15 @@
         lax.dynamic_slice_in_dim(teacher_rows, start, HALO, 0)
         for start in (place, teach_dev - HALO - place)
     ]
-    owns, edges = lax.optimization_barrier((owns, edges))
     halos = [swapped(edges[0], "ctx", 1)]
     halos.append(odd_swapped(edges[1], "ctx"))
     both = jnp.stack(owns)
     side_all = swapped(both, "ctx", 2)
     other_all = swapped(jnp.stack([both, side_all], axis=1), "ctx", 1)
     stages = list(range(1, groups))
-    lane_rows = heads_dev * HD
+    lanes = (heads_dev * HD, tp_count)
+    depth = per_own * HD
+    weights = {}
     out_weight = pltpu.with_memory_space_constraint(out_weight, pltpu.HBM)
     attended = []
     for kv in range(kv_dev):
@@ -490,27 +496,43 @@
         for step in range(1, groups):
             lifts.append(swapped(owns[kv], "ctx", GROUP * step))
         state = attend_own(queries, kv, per_own, owns[kv], side_all[kv], other_all[kv])
-        straight = jnp.stack(lifts)
-        near = jnp.concatenate([straight, swapped(straight, "ctx", 2)])
-        far = swapped(near, "ctx", 1)
+        turns = [stages] if kv or len(stages) < 2 else [stages[:1], stages[1:]]
+        blocks = []
+        for turn, chosen in enumerate(turns):
+            straight = jnp.stack([lifts[step - 1] for step in chosen])
+            crossed = swapped(straight, "ctx", 2)
+            if turn < len(turns) - 1:
+                pair = swapped(jnp.concatenate([straight, crossed]), "ctx", 1)
+                blocks += [straight, crossed, pair[: len(chosen)], pair[len(chosen) :]]
+                continue
+            blocks += [straight, crossed, swapped(straight, "ctx", 1)]
+            blocks.append(swapped(crossed, "ctx", 1))
         final = kv == kv_dev - 1
         parts = 2 if final and per_own % 2 == 0 else 1
         heads = per_own // parts
         for part in range(parts):
             first = part * heads
-            fetch = None
-            if final and part == 0:
-                fetch = (tp_count - 1, kv * per_own * HD, per_own * HD, lane_rows, tp_count)
+            if not final:
+                wanted = [(0, kv)]
+            else:
+                wanted = [(0, kv)] + [
+                    (step, other)
+                    for step in range(1, tp_count)
+                    for other in range(kv_dev)
+                    if (step, other) != (tp_count - 1, kv)
+                ]
+                share = -(-len(wanted) // parts)
+                wanted = wanted[part * share : (part + 1) * share]
+            fetch = [(step, other * depth, depth) for step, other in wanted]
             result = attend_more(
-                queries, kv, per_own, first, heads, stages, near, far, state, fetch, out_weight
+                queries, kv, per_own, first, heads, turns, blocks, state, fetch, lanes, out_weight
             )
-            if fetch:
-                weight = result[1]
-            attended.append((kv, part, (kv * per_own + first) * HD, result[0]))
+            weights.update(zip(wanted, result[1:]))
+            attended.append((kv, part, first * HD, result[0]))
 
     early, late, rest = [], [], []
     for kv, part, start, value in attended:
-        (late if kv == kv_dev - 1 else early).append(((0, start, value.shape[1]), value))
+        (late if kv == kv_dev - 1 else early).append(((0, kv), start, value))
     for step in range(1, tp_count):
         ring = [(i, (i + step) % tp_count) for i in range(tp_count)]
         for kv, part, start, value in attended:
@@ -518,28 +540,18 @@
             if kv == kv_dev - 1 and step == tp_count - 1:
                 rest.append(got)
             else:
-                late.append(((step, start, value.shape[1]), got))
-    spans = (span_start[None, :], span_len[None, :])
-    base, target = project(
-        base_kernel,
-        2,
-        [piece for piece, _ in early],
-        [value for _, value in early],
-        lane_rows,
-        tp_count,
-        [*spans, student_rows, teacher_rows, *halos],
-        out_weight,
-    )
-    (base,) = project(
-        add_kernel,
-        1,
-        [piece for piece, _ in late],
-        [value for _, value in late],
-        lane_rows,
-        tp_count,
-        [base],
-        out_weight,
-    )
+                late.append(((step, kv), start, got))
+
+    def products(entries):
+        blocks = list(dict.fromkeys(block for block, _, _ in entries))
+        pieces = [(blocks.index(block), at, value.shape[1]) for block, at, value in entries]
+        return pieces, [value for _, _, value in entries], [weights[block] for block in blocks]
+
+    base, target = project_base(
+        *products(early), span_start, span_len, student_rows, teacher_rows, halos
+    )
+    fetch = [(tp_count - 1, (kv_dev - 1) * depth, depth)]
+    base, weight = project_late(*products(late), base, fetch, lanes, out_weight)
     student_out, weighted, near, far = finish(
         span_start, span_len, base, target, teach_dev, rest, weight
     )

time: 96.8 us -> 96.6 us (level)
  starting transfers between devices: 24.6 us -> 34.2 us
  waiting for transfers between devices: 19.8 us -> 11.4 us
  Pallas kernels: 48.7 us -> 47.5 us
    ppermute x14 -> x18, starting transfers between devices: 16.3 us -> 25.5 us  [swapped(): lax.ppermute(value, axis, [(source, source ^ bit) for source in range(cou...]
    ppermute x14 -> x18, waiting for transfers between devices: 18.7 us -> 9.88 us  [swapped(): lax.ppermute(value, axis, [(source, source ^ bit) for source in range(cou...]
    pallas_call x5, Pallas kernels: 36 us -> 34.5 us  [the longest x3 22.7 us: attend_more(): pl.pallas_call(functools.partial(more_kernel, heads, first, turns, fetch,...]
  transfers between devices with their start and end apart: 19 -> 23, of which waited for: 6 -> 7; matrix products, arithmetic and copies ran while one was open for 0% -> 1% of each run, Pallas kernels for 45% -> 44%
where the time goes in v3:
time: 96.6 us; the launch traced here: 96.3 us
  Pallas kernels  47.5 us (49%)
  starting transfers between devices  34.2 us (35%)
  waiting for transfers between devices  11.4 us (12%)
  local copies, waits for them, and re-layouts  1.97 us (2%)
  between operations  1.13 us (1%)
    ppermute x18, starting transfers between devices, swapped(): lax.ppermute(value, axis, [(source, source ^ bit) for source in range(cou...  25.5 us
    pallas_call x3, Pallas kernels, attend_more(): pl.pallas_call(functools.partial(more_kernel, heads, first, turns, fetch,...  22.7 us
    ppermute x18, waiting for transfers between devices, swapped(): lax.ppermute(value, axis, [(source, source ^ bit) for source in range(cou...  9.88 us
    pallas_call x1, Pallas kernels, project_late(): pl.pallas_call(functools.partial(late_kernel, pieces, len(weights), fetch...  7.69 us
    ppermute x2, starting transfers between devices, odd_swapped(): lax.ppermute(value, axis, [(i, i + 1 if i % 2 else i - 1) for i in range(...  5.73 us
    pallas_call x2, Pallas kernels, attend_own(): pl.pallas_call(functools.partial(own_kernel, heads), grid=(1,), in_specs=...  5.57 us
    pallas_call x1, Pallas kernels, finish(): pl.pallas_call(functools.partial(final_kernel, count, cols, teach), in_sp...  4.56 us
    pallas_call x1, Pallas kernels, project_base(): pl.pallas_call(functools.partial(base_kernel, pieces, min(512, width)), i...  4.16 us
  transfers between devices with their start and end apart: 23, of which 7 were waited for; matrix products, arithmetic and copies ran while one was open for 1% of the time, Pallas kernels for 44%

profile of v3, /device:TPU:25, one launch (start us, length us, event | category | flops | bytes accessed | tf_op | source)
XLA Modules:
  0.0 96.3 jit_solution(15387004835786561991)
XLA Ops:
  1.9 3.4 %collective-permute-start.6 = (bf16[2,256,128]{2,1,0:T(8,128)(2,1)S(1)}, bf16[2,256,128]{2,1,0:T(8,128)(2,1)S(1)}, u32[]{:S(2)}, u32[]{:S(2)}) collective-permute-start(bf16[2,256,128]{2,1,0:T(8,128)(2,1)S(1)} %get-tuple-element.47.own_ref), channel_id=1, source_target_pairs={{0,24},{2,26},{4,28},{6,30},{8,16},{10,18},{12,20},{14,22},{16,8},... | collective-permute-start | bytes 393224 | tf_op jit(solution)/shard_map/ppermute | solution.py:37
  5.3 1.3 %collective-permute-start.10 = (bf16[2,2,256,128]{3,2,1,0:T(8,128)(2,1)S(1)}, bf16[2,2,256,128]{3,2,1,0:T(8,128)(2,1)S(1)}, u32[]{:S(2)}, u32[]{:S(2)}) collective-permute-start(bf16[2,2,256,128]{3,2,1,0:T(8,128)(2,1)S(1)} %get-tuple-element.51), channel_id=1, source_target_pairs={{0,4},{2,6},{4,0},{6,2},{8,12},{10,14},{12,8},{14,10},{16,20},{18,... | collective-permute-start | bytes 786440 | tf_op jit(solution)/shard_map/ppermute | solution.py:37
  9.8 2.3 %collective-permute-done.5 = bf16[2,256,128]{2,1,0:T(8,128)(2,1)S(1)} collective-permute-done((bf16[2,256,128]{2,1,0:T(8,128)(2,1)S(1)}, bf16[2,256,128]{2,1,0:T(8,128)(2,1)S(1)}, u32[]{:S(2)}, u32[]{:S(2)}) %collective-permute-start.5) | collective-permute-done | bytes 131104 | tf_op jit(solution)/shard_map/ppermute | solution.py:37
  12.1 1.6 %collective-permute-start.14 = (bf16[2,256,128]{2,1,0:T(8,128)(2,1)S(1)}, bf16[2,256,128]{2,1,0:T(8,128)(2,1)S(1)}, u32[]{:S(2)}, u32[]{:S(2)}) collective-permute-start(bf16[2,256,128]{2,1,0:T(8,128)(2,1)S(1)} %get-tuple-element.46.own_ref), channel_id=1, source_target_pairs={{0,24},{2,26},{4,28},{6,30},{8,16},{10,18},{12,20},{14,22},{16,8},... | collective-permute-start | bytes 393224 | tf_op jit(solution)/shard_map/ppermute | solution.py:37
  14.5 2.7 %collective-permute-start = (bf16[8,4096]{1,0:T(8,128)(2,1)S(1)}, bf16[8,4096]{1,0:T(8,128)(2,1)S(1)}, u32[]{:S(2)}, u32[]{:S(2)}) collective-permute-start(bf16[8,4096]{1,0:T(8,128)(2,1)S(1)} %get-tuple-element.43), channel_id=1, source_target_pairs={{0,2},{2,0},{4,6},{6,4},{8,10},{10,8},{12,14},{14,12},{16,18},{18,... | collective-permute-start | bytes 196616 | tf_op jit(solution)/shard_map/ppermute | solution.py:37
  17.2 3.1 %collective-permute-start.1 = (bf16[8,4096]{1,0:T(8,128)(2,1)S(1)}, bf16[8,4096]{1,0:T(8,128)(2,1)S(1)}, u32[]{:S(2)}, u32[]{:S(2)}) collective-permute-start(bf16[8,4096]{1,0:T(8,128)(2,1)S(1)} %get-tuple-element.42), channel_id=1, source_target_pairs={{2,4},{4,2},{6,8},{8,6},{10,12},{12,10},{14,16},{16,14},{18,20},{2... | collective-permute-start | bytes 196616 | tf_op jit(solution)/shard_map/ppermute | solution.py:30
  20.5 3.6 %collective-permute-done.13 = bf16[2,256,128]{2,1,0:T(8,128)(2,1)S(1)} collective-permute-done((bf16[2,256,128]{2,1,0:T(8,128)(2,1)S(1)}, bf16[2,256,128]{2,1,0:T(8,128)(2,1)S(1)}, u32[]{:S(2)}, u32[]{:S(2)}) %collective-permute-start.13) | collective-permute-done | bytes 131104 | tf_op jit(solution)/shard_map/ppermute | solution.py:37
  24.1 4.5 %collective-permute-start.11 = (bf16[2,2,2,256,128]{4,3,2,1,0:T(8,128)(2,1)S(1)}, bf16[2,2,2,256,128]{4,3,2,1,0:T(8,128)(2,1)S(1)}, u32[]{:S(2)}, u32[]{:S(2)}) collective-permute-start(bf16[2,2,2,256,128]{4,3,2,1,0:T(8,128)(2,1)S(1)} %pad_maximum_fusion), channel_id=1, source_target_pairs={{0,2},{2,0},{4,6},{6,4},{8,10},{10,8},{12,14},{14,12},{16,18},{18,... | collective-permute-start | bytes 1572872 | tf_op jit(solution)/shard_map/ppermute | solution.py:37
  28.7 1.7 %collective-permute-done.4 = bf16[2,2,256,128]{3,2,1,0:T(8,128)(2,1)S(1)} collective-permute-done((bf16[2,2,256,128]{3,2,1,0:T(8,128)(2,1)S(1)}, bf16[2,2,256,128]{3,2,1,0:T(8,128)(2,1)S(1)}, u32[]{:S(2)}, u32[]{:S(2)}) %collective-permute-start.4) | collective-permute-done | bytes 262176 | tf_op jit(solution)/shard_map/ppermute | solution.py:37
  30.9 1.7 %collective-permute-start.15 = (bf16[3,2,256,128]{3,2,1,0:T(8,128)(2,1)S(1)}, bf16[3,2,256,128]{3,2,1,0:T(8,128)(2,1)S(1)}, u32[]{:S(2)}, u32[]{:S(2)}) collective-permute-start(bf16[3,2,256,128]{3,2,1,0:T(8,128)(2,1)S(1)} %pad_maximum_fusion.1.refs_0_), channel_id=1, source_target_pairs={{0,4},{2,6},{4,0},{6,2},{8,12},{10,14},{12,8},{14,10},{16,20},{18,... | collective-permute-start | bytes 1179656 | tf_op jit(solution)/shard_map/ppermute | solution.py:37
  32.6 2.8 %collective-permute-start.9 = (bf16[2,2,256,128]{3,2,1,0:T(8,128)(2,1)S(1)}, bf16[2,2,256,128]{3,2,1,0:T(8,128)(2,1)S(1)}, u32[]{:S(2)}, u32[]{:S(2)}) collective-permute-start(bf16[2,2,256,128]{3,2,1,0:T(8,128)(2,1)S(1)} %collective-permute-done.7.refs_5_), channel_id=1, source_target_pairs={{0,2},{2,0},{4,6},{6,4},{8,10},{10,8},{12,14},{14,12},{16,18},{18,... | collective-permute-start | bytes 786440 | tf_op jit(solution)/shard_map/ppermute | solution.py:37
  35.5 2.8 %attend_own.2 = (f32[256,128]{1,0:T(8,128)S(1)}, f32[8,256,256]{2,1,0:T(8,128)S(1)}) custom-call(bf16[256,2048]{1,0:T(8,128)(2,1)S(1)} %copy-done, bf16[2,256,128]{2,1,0:T(8,128)(2,1)S(1)} %get-tuple-element.47.own_ref, bf16[2,256,128]{2,1,0:T(8,128)(2,1)S(1)} %get-tuple-element.49.side_ref, bf16[2,2,256,128]{3,2,1,0:T(8,128)(2,1)S(1)} %get-tuple-element.45.other_ref), custom_call_target="tpu_custom_call" | custom-call | flops 2147483648 | bytes 2097152 | tf_op jit(solution)/shard_map/attend_own/pallas_call | solution.py:181
  38.7 4.6 %collective-permute-start.17 = (bf16[3,2,256,128]{3,2,1,0:T(8,128)(2,1)S(1)}, bf16[3,2,256,128]{3,2,1,0:T(8,128)(2,1)S(1)}, u32[]{:S(2)}, u32[]{:S(2)}) collective-permute-start(bf16[3,2,256,128]{3,2,1,0:T(8,128)(2,1)S(1)} %collective-permute-done.15.refs_1_), channel_id=1, source_target_pairs={{0,2},{2,0},{4,6},{6,4},{8,10},{10,8},{12,14},{14,12},{16,18},{18,... | collective-permute-start | bytes 1179656 | tf_op jit(solution)/shard_map/ppermute | solution.py:37
  43.3 10.8 %attend_more.3 = (bf16[256,1024]{1,0:T(8,128)(2,1)S(1)}, bf16[1024,4096]{1,0:T(8,128)(2,1)S(1)}) custom-call(bf16[256,2048]{1,0:T(8,128)(2,1)S(1)} %copy-done, bf16[1,2,256,128]{3,2,1,0:T(8,128)(2,1)S(1)} %bitcast.25, bf16[1,2,256,128]{3,2,1,0:T(8,128)(2,1)S(1)} %collective-permute-done.3.refs_1_, bf16[1,2,256,128]{3,2,1,0:T(8,128)(2,1)S(1)} %get-tuple-element.53.refs_2_, ...), custom_call_target="tpu_custom_call" | custom-call | flops 6442450944 | bytes 2097152 | tf_op jit(solution)/shard_map/attend_more/pallas_call | solution.py:201
  54.0 1.3 %collective-permute-start.18 = (bf16[256,1024]{1,0:T(8,128)(2,1)S(1)}, bf16[256,1024]{1,0:T(8,128)(2,1)S(1)}, u32[]{:S(2)}, u32[]{:S(2)}) collective-permute-start(bf16[256,1024]{1,0:T(8,128)(2,1)S(1)} %get-tuple-element.24.refs_4_), channel_id=1, source_target_pairs={{0,1},{1,0},{2,3},{3,2},{4,5},{5,4},{6,7},{7,6},{8,9},{9,8},{10,11... | collective-permute-start | bytes 1572872 | tf_op jit(solution)/shard_map/ppermute | solution.py:539
  55.3 2.8 %attend_own.3 = (f32[256,128]{1,0:T(8,128)S(1)}, f32[8,256,256]{2,1,0:T(8,128)S(1)}) custom-call(bf16[256,2048]{1,0:T(8,128)(2,1)S(1)} %copy-done, bf16[2,256,128]{2,1,0:T(8,128)(2,1)S(1)} %get-tuple-element.46.own_ref, bf16[2,256,128]{2,1,0:T(8,128)(2,1)S(1)} %get-tuple-element.48.side_ref, bf16[2,2,256,128]{3,2,1,0:T(8,128)(2,1)S(1)} %get-tuple-element.44.other_ref), custom_call_target="tpu_custom_call" | custom-call | flops 2147483648 | bytes 2097152 | tf_op jit(solution)/shard_map/attend_own/pallas_call | solution.py:181
  58.2 4.2 %project_base.1 = (f32[256,4096]{1,0:T(8,128)S(1)}, f32[256,4096]{1,0:T(8,128)S(1)}) custom-call(s32[1,256]{1,0:T(1,128)S(1)} %bitcast.28, s32[1,256]{1,0:T(1,128)S(1)} %bitcast.31, bf16[256,4096]{1,0:T(8,128)(2,1)S(1)} %copy-done.2, bf16[384,4096]{1,0:T(8,128)(2,1)S(1)} %copy-done.1, bf16[8,4096]{1,0:T(8,128)(2,1)S(1)} %collective-permute-done.refs_2_, ...), custom_call_target="tpu_custom_call" | custom-call | flops 2147483648 | bytes 18874368 | tf_op jit(solution)/shard_map/project_base/pallas_call | solution.py:310
  62.4 5.9 %attend_more.5 = (bf16[256,512]{1,0:T(8,128)(2,1)S(1)}, bf16[1024,4096]{1,0:T(8,128)(2,1)S(1)}) custom-call(bf16[256,2048]{1,0:T(8,128)(2,1)S(1)} %copy-done, bf16[3,2,256,128]{3,2,1,0:T(8,128)(2,1)S(1)} %pad_maximum_fusion.1.refs_0_, bf16[3,2,256,128]{3,2,1,0:T(8,128)(2,1)S(1)} %collective-permute-done.15.refs_1_, ...), custom_call_target="tpu_custom_call" | custom-call | flops 3221225472 | bytes 2097152 | tf_op jit(solution)/shard_map/attend_more/pallas_call | solution.py:201
  68.6 6.0 %attend_more.4 = (bf16[256,512]{1,0:T(8,128)(2,1)S(1)}, bf16[1024,4096]{1,0:T(8,128)(2,1)S(1)}) custom-call(bf16[256,2048]{1,0:T(8,128)(2,1)S(1)} %copy-done, bf16[3,2,256,128]{3,2,1,0:T(8,128)(2,1)S(1)} %pad_maximum_fusion.1.refs_0_, bf16[3,2,256,128]{3,2,1,0:T(8,128)(2,1)S(1)} %collective-permute-done.15.refs_1_, ...), custom_call_target="tpu_custom_call" | custom-call | flops 3221225472 | bytes 2097152 | tf_op jit(solution)/shard_map/attend_more/pallas_call | solution.py:201
  75.9 7.7 %project_late.1 = (f32[256,4096]{1,0:T(8,128)S(1)}, bf16[1024,4096]{1,0:T(8,128)(2,1)S(1)}) custom-call(f32[256,4096]{1,0:T(8,128)S(1)} %get-tuple-element.26.base_ref, bf16[256,512]{1,0:T(8,128)(2,1)S(1)} %get-tuple-element.29.refs_0_, bf16[256,512]{1,0:T(8,128)(2,1)S(1)} %get-tuple-element.30.refs_1_, ...), custom_call_target="tpu_custom_call" | custom-call | flops 4294967296 | bytes 27262976 | tf_op jit(solution)/shard_map/project_late/pallas_call | solution.py:323
  83.6 4.6 %finish.1 = (bf16[256,4096]{1,0:T(8,128)(2,1)}, bf16[256,4096]{1,0:T(8,128)(2,1)S(1)}, bf16[8,4096]{1,0:T(8,128)(2,1)S(1)}, bf16[8,4096]{1,0:T(8,128)(2,1)S(1)}) custom-call(s32[1,256]{1,0:T(1,128)S(1)} %bitcast.29, s32[1,256]{1,0:T(1,128)S(1)} %bitcast.32, f32[256,4096]{1,0:T(8,128)S(1)} %get-tuple-element.33.base_ref, ...), custom_call_target="tpu_custom_call" | custom-call | flops 2147483648 | bytes 18874368 | tf_op jit(solution)/shard_map/finish/pallas_call | solution.py:367
  89.1 2.7 %collective-permute-start.22 = (bf16[8,4096]{1,0:T(8,128)(2,1)S(1)}, bf16[8,4096]{1,0:T(8,128)(2,1)S(1)}, u32[]{:S(2)}, u32[]{:S(2)}) collective-permute-start(bf16[8,4096]{1,0:T(8,128)(2,1)S(1)} %get-tuple-element.41), channel_id=1, source_target_pairs={{2,4},{4,2},{6,8},{8,6},{10,12},{12,10},{14,16},{16,14},{18,20},{2... | collective-permute-start | bytes 196616 | tf_op jit(solution)/shard_map/ppermute | solution.py:30
  91.8 2.1 %spread_out.1 = (bf16[384,4096]{1,0:T(8,128)(2,1)}, f32[32,4096]{1,0:T(8,128)S(1)}) custom-call(s32[1,256]{1,0:T(1,128)S(1)} %bitcast.30, s32[1,256]{1,0:T(1,128)S(1)} %bitcast.33, bf16[256,4096]{1,0:T(8,128)(2,1)S(1)} %get-tuple-element.37.weighted_ref), custom_call_target="tpu_custom_call" | custom-call | flops 805306368 | bytes 3145728 | tf_op jit(solution)/shard_map/spread_out/pallas_call | solution.py:412
  93.9 1.5 %collective-permute-done.22.far_ref = bf16[8,4096]{1,0:T(8,128)(2,1)S(1)} collective-permute-done((bf16[8,4096]{1,0:T(8,128)(2,1)S(1)}, bf16[8,4096]{1,0:T(8,128)(2,1)S(1)}, u32[]{:S(2)}, u32[]{:S(2)}) %collective-permute-start.22) | collective-permute-done | bytes 65568 | tf_op jit(solution)/shard_map/ppermute | solution.py:30
  (52 shorter events, 9.7 us)
Async XLA Ops:
  1.7 33.8 %copy-start = (bf16[256,2048]{1,0:T(8,128)(2,1)S(1)}, bf16[256,2048]{1,0:T(8,128)(2,1)}, u32[]{:S(2)}) copy-start(bf16[256,2048]{1,0:T(8,128)(2,1)} %query_ref.9) | copy-start | bytes 3145732
  1.7 6.0 %collective-permute-start.2 = (bf16[2,256,128]{2,1,0:T(8,128)(2,1)S(1)}, bf16[2,256,128]{2,1,0:T(8,128)(2,1)S(1)}, u32[]{:S(2)}, u32[]{:S(2)}) collective-permute-start(bf16[2,256,128]{2,1,0:T(8,128)(2,1)S(1)} %get-tuple-element.47.own_ref), channel_id=1, source_target_pairs={{0,8},{2,10},{4,12},{6,14},{8,0},{10,2},{12,4},{14,6},{16,24},{18,... | collective-permute-start | bytes 393224 | tf_op jit(solution)/shard_map/ppermute | solution.py:37
  1.9 10.2 %collective-permute-start.5 = (bf16[2,256,128]{2,1,0:T(8,128)(2,1)S(1)}, bf16[2,256,128]{2,1,0:T(8,128)(2,1)S(1)}, u32[]{:S(2)}, u32[]{:S(2)}) collective-permute-start(bf16[2,256,128]{2,1,0:T(8,128)(2,1)S(1)} %get-tuple-element.47.own_ref), channel_id=1, source_target_pairs={{0,16},{2,18},{4,20},{6,22},{8,24},{10,26},{12,28},{14,30},{16,0},... | collective-permute-start | bytes 393224 | tf_op jit(solution)/shard_map/ppermute | solution.py:37
  1.9 10.2 %collective-permute-start.6 = (bf16[2,256,128]{2,1,0:T(8,128)(2,1)S(1)}, bf16[2,256,128]{2,1,0:T(8,128)(2,1)S(1)}, u32[]{:S(2)}, u32[]{:S(2)}) collective-permute-start(bf16[2,256,128]{2,1,0:T(8,128)(2,1)S(1)} %get-tuple-element.47.own_ref), channel_id=1, source_target_pairs={{0,24},{2,26},{4,28},{6,30},{8,16},{10,18},{12,20},{14,22},{16,8},... | collective-permute-start | bytes 393224 | tf_op jit(solution)/shard_map/ppermute | solution.py:37
  5.3 15.1 %collective-permute-start.12 = (bf16[2,256,128]{2,1,0:T(8,128)(2,1)S(1)}, bf16[2,256,128]{2,1,0:T(8,128)(2,1)S(1)}, u32[]{:S(2)}, u32[]{:S(2)}) collective-permute-start(bf16[2,256,128]{2,1,0:T(8,128)(2,1)S(1)} %get-tuple-element.46.own_ref), channel_id=1, source_target_pairs={{0,8},{2,10},{4,12},{6,14},{8,0},{10,2},{12,4},{14,6},{16,24},{18,... | collective-permute-start | bytes 393224 | tf_op jit(solution)/shard_map/ppermute | solution.py:37
  5.3 11.9 %collective-permute-start.10 = (bf16[2,2,256,128]{3,2,1,0:T(8,128)(2,1)S(1)}, bf16[2,2,256,128]{3,2,1,0:T(8,128)(2,1)S(1)}, u32[]{:S(2)}, u32[]{:S(2)}) collective-permute-start(bf16[2,2,256,128]{3,2,1,0:T(8,128)(2,1)S(1)} %get-tuple-element.51), channel_id=1, source_target_pairs={{0,4},{2,6},{4,0},{6,2},{8,12},{10,14},{12,8},{14,10},{16,20},{18,... | collective-permute-start | bytes 786440 | tf_op jit(solution)/shard_map/ppermute | solution.py:37
  7.7 6.8 %collective-permute-start.3 = (bf16[1,2,256,128]{3,2,1,0:T(8,128)(2,1)S(1)}, bf16[1,2,256,128]{3,2,1,0:T(8,128)(2,1)S(1)}, u32[]{:S(2)}, u32[]{:S(2)}) collective-permute-start(bf16[1,2,256,128]{3,2,1,0:T(8,128)(2,1)S(1)} %bitcast.23), channel_id=1, source_target_pairs={{0,4},{2,6},{4,0},{6,2},{8,12},{10,14},{12,8},{14,10},{16,20},{18,... | collective-permute-start | bytes 393224 | tf_op jit(solution)/shard_map/ppermute | solution.py:37
  12.1 12.0 %collective-permute-start.13 = (bf16[2,256,128]{2,1,0:T(8,128)(2,1)S(1)}, bf16[2,256,128]{2,1,0:T(8,128)(2,1)S(1)}, u32[]{:S(2)}, u32[]{:S(2)}) collective-permute-start(bf16[2,256,128]{2,1,0:T(8,128)(2,1)S(1)} %get-tuple-element.46.own_ref), channel_id=1, source_target_pairs={{0,16},{2,18},{4,20},{6,22},{8,24},{10,26},{12,28},{14,30},{16,0},... | collective-permute-start | bytes 393224 | tf_op jit(solution)/shard_map/ppermute | solution.py:37
  12.1 16.4 %collective-permute-start.14 = (bf16[2,256,128]{2,1,0:T(8,128)(2,1)S(1)}, bf16[2,256,128]{2,1,0:T(8,128)(2,1)S(1)}, u32[]{:S(2)}, u32[]{:S(2)}) collective-permute-start(bf16[2,256,128]{2,1,0:T(8,128)(2,1)S(1)} %get-tuple-element.46.own_ref), channel_id=1, source_target_pairs={{0,24},{2,26},{4,28},{6,30},{8,16},{10,18},{12,20},{14,22},{16,8},... | collective-permute-start | bytes 393224 | tf_op jit(solution)/shard_map/ppermute | solution.py:37
  14.5 43.6 %collective-permute-start = (bf16[8,4096]{1,0:T(8,128)(2,1)S(1)}, bf16[8,4096]{1,0:T(8,128)(2,1)S(1)}, u32[]{:S(2)}, u32[]{:S(2)}) collective-permute-start(bf16[8,4096]{1,0:T(8,128)(2,1)S(1)} %get-tuple-element.43), channel_id=1, source_target_pairs={{0,2},{2,0},{4,6},{6,4},{8,10},{10,8},{12,14},{14,12},{16,18},{18,... | collective-permute-start | bytes 196616 | tf_op jit(solution)/shard_map/ppermute | solution.py:37
  17.2 40.9 %collective-permute-start.1 = (bf16[8,4096]{1,0:T(8,128)(2,1)S(1)}, bf16[8,4096]{1,0:T(8,128)(2,1)S(1)}, u32[]{:S(2)}, u32[]{:S(2)}) collective-permute-start(bf16[8,4096]{1,0:T(8,128)(2,1)S(1)} %get-tuple-element.42), channel_id=1, source_target_pairs={{2,4},{4,2},{6,8},{8,6},{10,12},{12,10},{14,16},{16,14},{18,20},{2... | collective-permute-start | bytes 196616 | tf_op jit(solution)/shard_map/ppermute | solution.py:30
  20.4 10.5 %collective-permute-start.7 = (bf16[2,2,256,128]{3,2,1,0:T(8,128)(2,1)S(1)}, bf16[2,2,256,128]{3,2,1,0:T(8,128)(2,1)S(1)}, u32[]{:S(2)}, u32[]{:S(2)}) collective-permute-start(bf16[2,2,256,128]{3,2,1,0:T(8,128)(2,1)S(1)} %pad_maximum_fusion.3.refs_4_), channel_id=1, source_target_pairs={{0,4},{2,6},{4,0},{6,2},{8,12},{10,14},{12,8},{14,10},{16,20},{18,... | collective-permute-start | bytes 786440 | tf_op jit(solution)/shard_map/ppermute | solution.py:37
  24.1 8.5 %collective-permute-start.11 = (bf16[2,2,2,256,128]{4,3,2,1,0:T(8,128)(2,1)S(1)}, bf16[2,2,2,256,128]{4,3,2,1,0:T(8,128)(2,1)S(1)}, u32[]{:S(2)}, u32[]{:S(2)}) collective-permute-start(bf16[2,2,2,256,128]{4,3,2,1,0:T(8,128)(2,1)S(1)} %pad_maximum_fusion), channel_id=1, source_target_pairs={{0,2},{2,0},{4,6},{6,4},{8,10},{10,8},{12,14},{14,12},{16,18},{18,... | collective-permute-start | bytes 1572872 | tf_op jit(solution)/shard_map/ppermute | solution.py:37
  28.5 1.9 %collective-permute-start.4 = (bf16[2,2,256,128]{3,2,1,0:T(8,128)(2,1)S(1)}, bf16[2,2,256,128]{3,2,1,0:T(8,128)(2,1)S(1)}, u32[]{:S(2)}, u32[]{:S(2)}) collective-permute-start(bf16[2,2,256,128]{3,2,1,0:T(8,128)(2,1)S(1)} %pad_maximum_fusion.2), channel_id=1, source_target_pairs={{0,2},{2,0},{4,6},{6,4},{8,10},{10,8},{12,14},{14,12},{16,18},{18,... | collective-permute-start | bytes 786440 | tf_op jit(solution)/shard_map/ppermute | solution.py:37
  30.5 7.8 %collective-permute-start.8 = (bf16[2,2,256,128]{3,2,1,0:T(8,128)(2,1)S(1)}, bf16[2,2,256,128]{3,2,1,0:T(8,128)(2,1)S(1)}, u32[]{:S(2)}, u32[]{:S(2)}) collective-permute-start(bf16[2,2,256,128]{3,2,1,0:T(8,128)(2,1)S(1)} %pad_maximum_fusion.3.refs_4_), channel_id=1, source_target_pairs={{0,2},{2,0},{4,6},{6,4},{8,10},{10,8},{12,14},{14,12},{16,18},{18,... | collective-permute-start | bytes 786440 | tf_op jit(solution)/shard_map/ppermute | solution.py:37
  30.9 7.8 %collective-permute-start.15 = (bf16[3,2,256,128]{3,2,1,0:T(8,128)(2,1)S(1)}, bf16[3,2,256,128]{3,2,1,0:T(8,128)(2,1)S(1)}, u32[]{:S(2)}, u32[]{:S(2)}) collective-permute-start(bf16[3,2,256,128]{3,2,1,0:T(8,128)(2,1)S(1)} %pad_maximum_fusion.1.refs_0_), channel_id=1, source_target_pairs={{0,4},{2,6},{4,0},{6,2},{8,12},{10,14},{12,8},{14,10},{16,20},{18,... | collective-permute-start | bytes 1179656 | tf_op jit(solution)/shard_map/ppermute | solution.py:37
  32.6 10.7 %collective-permute-start.9 = (bf16[2,2,256,128]{3,2,1,0:T(8,128)(2,1)S(1)}, bf16[2,2,256,128]{3,2,1,0:T(8,128)(2,1)S(1)}, u32[]{:S(2)}, u32[]{:S(2)}) collective-permute-start(bf16[2,2,256,128]{3,2,1,0:T(8,128)(2,1)S(1)} %collective-permute-done.7.refs_5_), channel_id=1, source_target_pairs={{0,2},{2,0},{4,6},{6,4},{8,10},{10,8},{12,14},{14,12},{16,18},{18,... | collective-permute-start | bytes 786440 | tf_op jit(solution)/shard_map/ppermute | solution.py:37
  38.3 24.1 %collective-permute-start.16 = (bf16[3,2,256,128]{3,2,1,0:T(8,128)(2,1)S(1)}, bf16[3,2,256,128]{3,2,1,0:T(8,128)(2,1)S(1)}, u32[]{:S(2)}, u32[]{:S(2)}) collective-permute-start(bf16[3,2,256,128]{3,2,1,0:T(8,128)(2,1)S(1)} %pad_maximum_fusion.1.refs_0_), channel_id=1, source_target_pairs={{0,2},{2,0},{4,6},{6,4},{8,10},{10,8},{12,14},{14,12},{16,18},{18,... | collective-permute-start | bytes 1179656 | tf_op jit(solution)/shard_map/ppermute | solution.py:37
  38.7 23.7 %collective-permute-start.17 = (bf16[3,2,256,128]{3,2,1,0:T(8,128)(2,1)S(1)}, bf16[3,2,256,128]{3,2,1,0:T(8,128)(2,1)S(1)}, u32[]{:S(2)}, u32[]{:S(2)}) collective-permute-start(bf16[3,2,256,128]{3,2,1,0:T(8,128)(2,1)S(1)} %collective-permute-done.15.refs_1_), channel_id=1, source_target_pairs={{0,2},{2,0},{4,6},{6,4},{8,10},{10,8},{12,14},{14,12},{16,18},{18,... | collective-permute-start | bytes 1179656 | tf_op jit(solution)/shard_map/ppermute | solution.py:37
  54.0 21.8 %collective-permute-start.18 = (bf16[256,1024]{1,0:T(8,128)(2,1)S(1)}, bf16[256,1024]{1,0:T(8,128)(2,1)S(1)}, u32[]{:S(2)}, u32[]{:S(2)}) collective-permute-start(bf16[256,1024]{1,0:T(8,128)(2,1)S(1)} %get-tuple-element.24.refs_4_), channel_id=1, source_target_pairs={{0,1},{1,0},{2,3},{3,2},{4,5},{5,4},{6,7},{7,6},{8,9},{9,8},{10,11... | collective-permute-start | bytes 1572872 | tf_op jit(solution)/shard_map/ppermute | solution.py:539
  68.3 15.3 %collective-permute-start.20 = (bf16[256,512]{1,0:T(8,128)(2,1)S(1)}, bf16[256,512]{1,0:T(8,128)(2,1)S(1)}, u32[]{:S(2)}, u32[]{:S(2)}) collective-permute-start(bf16[256,512]{1,0:T(8,128)(2,1)S(1)} %get-tuple-element.30.refs_1_), channel_id=1, source_target_pairs={{0,1},{1,0},{2,3},{3,2},{4,5},{5,4},{6,7},{7,6},{8,9},{9,8},{10,11... | collective-permute-start | bytes 786440 | tf_op jit(solution)/shard_map/ppermute | solution.py:539
  74.6 9.0 %collective-permute-start.19 = (bf16[256,512]{1,0:T(8,128)(2,1)S(1)}, bf16[256,512]{1,0:T(8,128)(2,1)S(1)}, u32[]{:S(2)}, u32[]{:S(2)}) collective-permute-start(bf16[256,512]{1,0:T(8,128)(2,1)S(1)} %get-tuple-element.29.refs_0_), channel_id=1, source_target_pairs={{0,1},{1,0},{2,3},{3,2},{4,5},{5,4},{6,7},{7,6},{8,9},{9,8},{10,11... | collective-permute-start | bytes 786440 | tf_op jit(solution)/shard_map/ppermute | solution.py:539
  88.2 5.7 %collective-permute-start.21 = (bf16[8,4096]{1,0:T(8,128)(2,1)S(1)}, bf16[8,4096]{1,0:T(8,128)(2,1)S(1)}, u32[]{:S(2)}, u32[]{:S(2)}) collective-permute-start(bf16[8,4096]{1,0:T(8,128)(2,1)S(1)} %get-tuple-element.40), channel_id=1, source_target_pairs={{0,2},{2,0},{4,6},{6,4},{8,10},{10,8},{12,14},{14,12},{16,18},{18,... | collective-permute-start | bytes 196616 | tf_op jit(solution)/shard_map/ppermute | solution.py:37
  89.1 6.3 %collective-permute-start.22 = (bf16[8,4096]{1,0:T(8,128)(2,1)S(1)}, bf16[8,4096]{1,0:T(8,128)(2,1)S(1)}, u32[]{:S(2)}, u32[]{:S(2)}) collective-permute-start(bf16[8,4096]{1,0:T(8,128)(2,1)S(1)} %get-tuple-element.41), channel_id=1, source_target_pairs={{2,4},{4,2},{6,8},{8,6},{10,12},{12,10},{14,16},{16,14},{18,20},{2... | collective-permute-start | bytes 196616 | tf_op jit(solution)/shard_map/ppermute | solution.py:30
  (4 other events, 11.4 us)

commit v4 on v3

--- a/solution.py
+++ b/solution.py
@@ -21,8 +21,8 @@
 exp2_scale = math.log2(math.e) / math.sqrt(HD)
 
 ATTN_VMEM = 9 * 1024 * 1024
-PROJECT_VMEM = 6 * 1024 * 1024
-FINISH_VMEM = 8 * 1024 * 1024
+PROJECT_VMEM = 10 * 1024 * 1024
+FINISH_VMEM = 10 * 1024 * 1024
 
 
 def odd_swapped(value, axis):
@@ -308,7 +308,7 @@
 def project_base(pieces, values, weights, starts, lens, student, teacher, halos):
     rows, width = student.shape
     return pl.pallas_call(
-        functools.partial(base_kernel, pieces, min(512, width)),
+        functools.partial(base_kernel, pieces, min(1024, width)),
         in_specs=[VMEM_SPEC] * (6 + len(values) + len(weights)),
         out_specs=[VMEM_SPEC] * 2,
         out_shape=[jax.ShapeDtypeStruct((rows, width), F32)] * 2,
@@ -321,7 +321,7 @@
 def project_late(pieces, values, weights, base, fetch, lanes, out_weight):
     rows, width = base.shape
     return pl.pallas_call(
-        functools.partial(late_kernel, pieces, len(weights), fetch, lanes, min(512, width)),
+        functools.partial(late_kernel, pieces, len(weights), fetch, lanes, min(1024, width)),
         in_specs=[VMEM_SPEC] * (1 + len(values) + len(weights)) + [HBM_SPEC],
         out_specs=[VMEM_SPEC] * 2,
         out_shape=[jax.ShapeDtypeStruct((rows, width), F32)] + fetched(fetch, out_weight),
@@ -363,7 +363,7 @@
 def finish(starts, lens, base, target, teach, pieces, weight):
     rows, width = base.shape
     count, depth = len(pieces), weight.shape[0]
-    cols = min(512, width)
+    cols = min(1024, width)
     return pl.pallas_call(
         functools.partial(final_kernel, count, cols, teach),
         in_specs=[VMEM_SPEC] * (5 + count),

time: 96.6 us -> 96 us (level)
  no operation moved by 1% of the time
where the time goes in v4:
time: 96 us; the launch traced here: 95.7 us
  Pallas kernels  46.9 us (49%)
  starting transfers between devices  34.1 us (36%)
  waiting for transfers between devices  11.4 us (12%)
  local copies, waits for them, and re-layouts  1.97 us (2%)
  between operations  1.13 us (1%)
    ppermute x18, starting transfers between devices, swapped(): lax.ppermute(value, axis, [(source, source ^ bit) for source in range(cou...  25.5 us
    pallas_call x3, Pallas kernels, attend_more(): pl.pallas_call(functools.partial(more_kernel, heads, first, turns, fetch,...  22.7 us
    ppermute x18, waiting for transfers between devices, swapped(): lax.ppermute(value, axis, [(source, source ^ bit) for source in range(cou...  9.88 us
    pallas_call x1, Pallas kernels, project_late(): pl.pallas_call(functools.partial(late_kernel, pieces, len(weights), fetch...  7.71 us
    ppermute x2, starting transfers between devices, odd_swapped(): lax.ppermute(value, axis, [(i, i + 1 if i % 2 else i - 1) for i in range(...  5.73 us
    pallas_call x2, Pallas kernels, attend_own(): pl.pallas_call(functools.partial(own_kernel, heads), grid=(1,), in_specs=...  5.57 us
    pallas_call x1, Pallas kernels, project_base(): pl.pallas_call(functools.partial(base_kernel, pieces, min(1024, width)),...  4.15 us
    pallas_call x1, Pallas kernels, finish(): pl.pallas_call(functools.partial(final_kernel, count, cols, teach), in_sp...  3.92 us
  transfers between devices with their start and end apart: 23, of which 7 were waited for; matrix products, arithmetic and copies ran while one was open for 1% of the time, Pallas kernels for 44%

profile of v4, /device:TPU:25, one launch (start us, length us, event | category | flops | bytes accessed | tf_op | source)
XLA Modules:
  0.0 95.7 jit_solution(16084607263381502986)
XLA Ops:
  1.9 3.4 %collective-permute-start.6 = (bf16[2,256,128]{2,1,0:T(8,128)(2,1)S(1)}, bf16[2,256,128]{2,1,0:T(8,128)(2,1)S(1)}, u32[]{:S(2)}, u32[]{:S(2)}) collective-permute-start(bf16[2,256,128]{2,1,0:T(8,128)(2,1)S(1)} %get-tuple-element.47.own_ref), channel_id=1, source_target_pairs={{0,24},{2,26},{4,28},{6,30},{8,16},{10,18},{12,20},{14,22},{16,8},... | collective-permute-start | bytes 393224 | tf_op jit(solution)/shard_map/ppermute | solution.py:37
  5.3 1.3 %collective-permute-start.10 = (bf16[2,2,256,128]{3,2,1,0:T(8,128)(2,1)S(1)}, bf16[2,2,256,128]{3,2,1,0:T(8,128)(2,1)S(1)}, u32[]{:S(2)}, u32[]{:S(2)}) collective-permute-start(bf16[2,2,256,128]{3,2,1,0:T(8,128)(2,1)S(1)} %get-tuple-element.51), channel_id=1, source_target_pairs={{0,4},{2,6},{4,0},{6,2},{8,12},{10,14},{12,8},{14,10},{16,20},{18,... | collective-permute-start | bytes 786440 | tf_op jit(solution)/shard_map/ppermute | solution.py:37
  9.8 2.3 %collective-permute-done.5 = bf16[2,256,128]{2,1,0:T(8,128)(2,1)S(1)} collective-permute-done((bf16[2,256,128]{2,1,0:T(8,128)(2,1)S(1)}, bf16[2,256,128]{2,1,0:T(8,128)(2,1)S(1)}, u32[]{:S(2)}, u32[]{:S(2)}) %collective-permute-start.5) | collective-permute-done | bytes 131104 | tf_op jit(solution)/shard_map/ppermute | solution.py:37
  12.1 1.6 %collective-permute-start.14 = (bf16[2,256,128]{2,1,0:T(8,128)(2,1)S(1)}, bf16[2,256,128]{2,1,0:T(8,128)(2,1)S(1)}, u32[]{:S(2)}, u32[]{:S(2)}) collective-permute-start(bf16[2,256,128]{2,1,0:T(8,128)(2,1)S(1)} %get-tuple-element.46.own_ref), channel_id=1, source_target_pairs={{0,24},{2,26},{4,28},{6,30},{8,16},{10,18},{12,20},{14,22},{16,8},... | collective-permute-start | bytes 393224 | tf_op jit(solution)/shard_map/ppermute | solution.py:37
  14.5 2.7 %collective-permute-start = (bf16[8,4096]{1,0:T(8,128)(2,1)S(1)}, bf16[8,4096]{1,0:T(8,128)(2,1)S(1)}, u32[]{:S(2)}, u32[]{:S(2)}) collective-permute-start(bf16[8,4096]{1,0:T(8,128)(2,1)S(1)} %get-tuple-element.43), channel_id=1, source_target_pairs={{0,2},{2,0},{4,6},{6,4},{8,10},{10,8},{12,14},{14,12},{16,18},{18,... | collective-permute-start | bytes 196616 | tf_op jit(solution)/shard_map/ppermute | solution.py:37
  17.2 3.1 %collective-permute-start.1 = (bf16[8,4096]{1,0:T(8,128)(2,1)S(1)}, bf16[8,4096]{1,0:T(8,128)(2,1)S(1)}, u32[]{:S(2)}, u32[]{:S(2)}) collective-permute-start(bf16[8,4096]{1,0:T(8,128)(2,1)S(1)} %get-tuple-element.42), channel_id=1, source_target_pairs={{2,4},{4,2},{6,8},{8,6},{10,12},{12,10},{14,16},{16,14},{18,20},{2... | collective-permute-start | bytes 196616 | tf_op jit(solution)/shard_map/ppermute | solution.py:30
  20.5 3.6 %collective-permute-done.13 = bf16[2,256,128]{2,1,0:T(8,128)(2,1)S(1)} collective-permute-done((bf16[2,256,128]{2,1,0:T(8,128)(2,1)S(1)}, bf16[2,256,128]{2,1,0:T(8,128)(2,1)S(1)}, u32[]{:S(2)}, u32[]{:S(2)}) %collective-permute-start.13) | collective-permute-done | bytes 131104 | tf_op jit(solution)/shard_map/ppermute | solution.py:37
  24.1 4.5 %collective-permute-start.11 = (bf16[2,2,2,256,128]{4,3,2,1,0:T(8,128)(2,1)S(1)}, bf16[2,2,2,256,128]{4,3,2,1,0:T(8,128)(2,1)S(1)}, u32[]{:S(2)}, u32[]{:S(2)}) collective-permute-start(bf16[2,2,2,256,128]{4,3,2,1,0:T(8,128)(2,1)S(1)} %pad_maximum_fusion), channel_id=1, source_target_pairs={{0,2},{2,0},{4,6},{6,4},{8,10},{10,8},{12,14},{14,12},{16,18},{18,... | collective-permute-start | bytes 1572872 | tf_op jit(solution)/shard_map/ppermute | solution.py:37
  28.7 1.7 %collective-permute-done.4 = bf16[2,2,256,128]{3,2,1,0:T(8,128)(2,1)S(1)} collective-permute-done((bf16[2,2,256,128]{3,2,1,0:T(8,128)(2,1)S(1)}, bf16[2,2,256,128]{3,2,1,0:T(8,128)(2,1)S(1)}, u32[]{:S(2)}, u32[]{:S(2)}) %collective-permute-start.4) | collective-permute-done | bytes 262176 | tf_op jit(solution)/shard_map/ppermute | solution.py:37
  30.9 1.7 %collective-permute-start.15 = (bf16[3,2,256,128]{3,2,1,0:T(8,128)(2,1)S(1)}, bf16[3,2,256,128]{3,2,1,0:T(8,128)(2,1)S(1)}, u32[]{:S(2)}, u32[]{:S(2)}) collective-permute-start(bf16[3,2,256,128]{3,2,1,0:T(8,128)(2,1)S(1)} %pad_maximum_fusion.1.refs_0_), channel_id=1, source_target_pairs={{0,4},{2,6},{4,0},{6,2},{8,12},{10,14},{12,8},{14,10},{16,20},{18,... | collective-permute-start | bytes 1179656 | tf_op jit(solution)/shard_map/ppermute | solution.py:37
  32.6 2.8 %collective-permute-start.9 = (bf16[2,2,256,128]{3,2,1,0:T(8,128)(2,1)S(1)}, bf16[2,2,256,128]{3,2,1,0:T(8,128)(2,1)S(1)}, u32[]{:S(2)}, u32[]{:S(2)}) collective-permute-start(bf16[2,2,256,128]{3,2,1,0:T(8,128)(2,1)S(1)} %collective-permute-done.7.refs_5_), channel_id=1, source_target_pairs={{0,2},{2,0},{4,6},{6,4},{8,10},{10,8},{12,14},{14,12},{16,18},{18,... | collective-permute-start | bytes 786440 | tf_op jit(solution)/shard_map/ppermute | solution.py:37
  35.5 2.8 %attend_own.2 = (f32[256,128]{1,0:T(8,128)S(1)}, f32[8,256,256]{2,1,0:T(8,128)S(1)}) custom-call(bf16[256,2048]{1,0:T(8,128)(2,1)S(1)} %copy-done, bf16[2,256,128]{2,1,0:T(8,128)(2,1)S(1)} %get-tuple-element.47.own_ref, bf16[2,256,128]{2,1,0:T(8,128)(2,1)S(1)} %get-tuple-element.49.side_ref, bf16[2,2,256,128]{3,2,1,0:T(8,128)(2,1)S(1)} %get-tuple-element.45.other_ref), custom_call_target="tpu_custom_call" | custom-call | flops 2147483648 | bytes 2097152 | tf_op jit(solution)/shard_map/attend_own/pallas_call | solution.py:181
  38.7 4.6 %collective-permute-start.17 = (bf16[3,2,256,128]{3,2,1,0:T(8,128)(2,1)S(1)}, bf16[3,2,256,128]{3,2,1,0:T(8,128)(2,1)S(1)}, u32[]{:S(2)}, u32[]{:S(2)}) collective-permute-start(bf16[3,2,256,128]{3,2,1,0:T(8,128)(2,1)S(1)} %collective-permute-done.15.refs_1_), channel_id=1, source_target_pairs={{0,2},{2,0},{4,6},{6,4},{8,10},{10,8},{12,14},{14,12},{16,18},{18,... | collective-permute-start | bytes 1179656 | tf_op jit(solution)/shard_map/ppermute | solution.py:37
  43.3 10.8 %attend_more.3 = (bf16[256,1024]{1,0:T(8,128)(2,1)S(1)}, bf16[1024,4096]{1,0:T(8,128)(2,1)S(1)}) custom-call(bf16[256,2048]{1,0:T(8,128)(2,1)S(1)} %copy-done, bf16[1,2,256,128]{3,2,1,0:T(8,128)(2,1)S(1)} %bitcast.25, bf16[1,2,256,128]{3,2,1,0:T(8,128)(2,1)S(1)} %collective-permute-done.3.refs_1_, bf16[1,2,256,128]{3,2,1,0:T(8,128)(2,1)S(1)} %get-tuple-element.53.refs_2_, ...), custom_call_target="tpu_custom_call" | custom-call | flops 6442450944 | bytes 2097152 | tf_op jit(solution)/shard_map/attend_more/pallas_call | solution.py:201
  55.3 2.8 %attend_own.3 = (f32[256,128]{1,0:T(8,128)S(1)}, f32[8,256,256]{2,1,0:T(8,128)S(1)}) custom-call(bf16[256,2048]{1,0:T(8,128)(2,1)S(1)} %copy-done, bf16[2,256,128]{2,1,0:T(8,128)(2,1)S(1)} %get-tuple-element.46.own_ref, bf16[2,256,128]{2,1,0:T(8,128)(2,1)S(1)} %get-tuple-element.48.side_ref, bf16[2,2,256,128]{3,2,1,0:T(8,128)(2,1)S(1)} %get-tuple-element.44.other_ref), custom_call_target="tpu_custom_call" | custom-call | flops 2147483648 | bytes 2097152 | tf_op jit(solution)/shard_map/attend_own/pallas_call | solution.py:181
  58.2 4.2 %project_base.1 = (f32[256,4096]{1,0:T(8,128)S(1)}, f32[256,4096]{1,0:T(8,128)S(1)}) custom-call(s32[1,256]{1,0:T(1,128)S(1)} %bitcast.28, s32[1,256]{1,0:T(1,128)S(1)} %bitcast.31, bf16[256,4096]{1,0:T(8,128)(2,1)S(1)} %copy-done.2, bf16[384,4096]{1,0:T(8,128)(2,1)S(1)} %copy-done.1, bf16[8,4096]{1,0:T(8,128)(2,1)S(1)} %collective-permute-done.refs_2_, ...), custom_call_target="tpu_custom_call" | custom-call | flops 2147483648 | bytes 18874368 | tf_op jit(solution)/shard_map/project_base/pallas_call | solution.py:310
  62.4 5.9 %attend_more.5 = (bf16[256,512]{1,0:T(8,128)(2,1)S(1)}, bf16[1024,4096]{1,0:T(8,128)(2,1)S(1)}) custom-call(bf16[256,2048]{1,0:T(8,128)(2,1)S(1)} %copy-done, bf16[3,2,256,128]{3,2,1,0:T(8,128)(2,1)S(1)} %pad_maximum_fusion.1.refs_0_, bf16[3,2,256,128]{3,2,1,0:T(8,128)(2,1)S(1)} %collective-permute-done.15.refs_1_, ...), custom_call_target="tpu_custom_call" | custom-call | flops 3221225472 | bytes 2097152 | tf_op jit(solution)/shard_map/attend_more/pallas_call | solution.py:201
  68.6 6.0 %attend_more.4 = (bf16[256,512]{1,0:T(8,128)(2,1)S(1)}, bf16[1024,4096]{1,0:T(8,128)(2,1)S(1)}) custom-call(bf16[256,2048]{1,0:T(8,128)(2,1)S(1)} %copy-done, bf16[3,2,256,128]{3,2,1,0:T(8,128)(2,1)S(1)} %pad_maximum_fusion.1.refs_0_, bf16[3,2,256,128]{3,2,1,0:T(8,128)(2,1)S(1)} %collective-permute-done.15.refs_1_, ...), custom_call_target="tpu_custom_call" | custom-call | flops 3221225472 | bytes 2097152 | tf_op jit(solution)/shard_map/attend_more/pallas_call | solution.py:201
  74.6 1.3 %collective-permute-start.19 = (bf16[256,512]{1,0:T(8,128)(2,1)S(1)}, bf16[256,512]{1,0:T(8,128)(2,1)S(1)}, u32[]{:S(2)}, u32[]{:S(2)}) collective-permute-start(bf16[256,512]{1,0:T(8,128)(2,1)S(1)} %get-tuple-element.29.refs_0_), channel_id=1, source_target_pairs={{0,1},{1,0},{2,3},{3,2},{4,5},{5,4},{6,7},{7,6},{8,9},{9,8},{10,11... | collective-permute-start | bytes 786440 | tf_op jit(solution)/shard_map/ppermute | solution.py:539
  75.9 7.7 %project_late.1 = (f32[256,4096]{1,0:T(8,128)S(1)}, bf16[1024,4096]{1,0:T(8,128)(2,1)S(1)}) custom-call(f32[256,4096]{1,0:T(8,128)S(1)} %get-tuple-element.26.base_ref, bf16[256,512]{1,0:T(8,128)(2,1)S(1)} %get-tuple-element.29.refs_0_, bf16[256,512]{1,0:T(8,128)(2,1)S(1)} %get-tuple-element.30.refs_1_, ...), custom_call_target="tpu_custom_call" | custom-call | flops 4294967296 | bytes 27262976 | tf_op jit(solution)/shard_map/project_late/pallas_call | solution.py:323
  83.6 3.9 %finish.1 = (bf16[256,4096]{1,0:T(8,128)(2,1)}, bf16[256,4096]{1,0:T(8,128)(2,1)S(1)}, bf16[8,4096]{1,0:T(8,128)(2,1)S(1)}, bf16[8,4096]{1,0:T(8,128)(2,1)S(1)}) custom-call(s32[1,256]{1,0:T(1,128)S(1)} %bitcast.29, s32[1,256]{1,0:T(1,128)S(1)} %bitcast.32, f32[256,4096]{1,0:T(8,128)S(1)} %get-tuple-element.33.base_ref, ...), custom_call_target="tpu_custom_call" | custom-call | flops 2147483648 | bytes 18874368 | tf_op jit(solution)/shard_map/finish/pallas_call | solution.py:367
  88.4 2.7 %collective-permute-start.22 = (bf16[8,4096]{1,0:T(8,128)(2,1)S(1)}, bf16[8,4096]{1,0:T(8,128)(2,1)S(1)}, u32[]{:S(2)}, u32[]{:S(2)}) collective-permute-start(bf16[8,4096]{1,0:T(8,128)(2,1)S(1)} %get-tuple-element.41), channel_id=1, source_target_pairs={{2,4},{4,2},{6,8},{8,6},{10,12},{12,10},{14,16},{16,14},{18,20},{2... | collective-permute-start | bytes 196616 | tf_op jit(solution)/shard_map/ppermute | solution.py:30
  91.1 2.1 %spread_out.1 = (bf16[384,4096]{1,0:T(8,128)(2,1)}, f32[32,4096]{1,0:T(8,128)S(1)}) custom-call(s32[1,256]{1,0:T(1,128)S(1)} %bitcast.30, s32[1,256]{1,0:T(1,128)S(1)} %bitcast.33, bf16[256,4096]{1,0:T(8,128)(2,1)S(1)} %get-tuple-element.37.weighted_ref), custom_call_target="tpu_custom_call" | custom-call | flops 805306368 | bytes 3145728 | tf_op jit(solution)/shard_map/spread_out/pallas_call | solution.py:412
  93.2 1.5 %collective-permute-done.22.far_ref = bf16[8,4096]{1,0:T(8,128)(2,1)S(1)} collective-permute-done((bf16[8,4096]{1,0:T(8,128)(2,1)S(1)}, bf16[8,4096]{1,0:T(8,128)(2,1)S(1)}, u32[]{:S(2)}, u32[]{:S(2)}) %collective-permute-start.22) | collective-permute-done | bytes 65568 | tf_op jit(solution)/shard_map/ppermute | solution.py:30
  (52 shorter events, 9.7 us)
Async XLA Ops:
  1.7 33.8 %copy-start = (bf16[256,2048]{1,0:T(8,128)(2,1)S(1)}, bf16[256,2048]{1,0:T(8,128)(2,1)}, u32[]{:S(2)}) copy-start(bf16[256,2048]{1,0:T(8,128)(2,1)} %query_ref.9) | copy-start | bytes 3145732
  1.7 6.0 %collective-permute-start.2 = (bf16[2,256,128]{2,1,0:T(8,128)(2,1)S(1)}, bf16[2,256,128]{2,1,0:T(8,128)(2,1)S(1)}, u32[]{:S(2)}, u32[]{:S(2)}) collective-permute-start(bf16[2,256,128]{2,1,0:T(8,128)(2,1)S(1)} %get-tuple-element.47.own_ref), channel_id=1, source_target_pairs={{0,8},{2,10},{4,12},{6,14},{8,0},{10,2},{12,4},{14,6},{16,24},{18,... | collective-permute-start | bytes 393224 | tf_op jit(solution)/shard_map/ppermute | solution.py:37
  1.9 10.2 %collective-permute-start.5 = (bf16[2,256,128]{2,1,0:T(8,128)(2,1)S(1)}, bf16[2,256,128]{2,1,0:T(8,128)(2,1)S(1)}, u32[]{:S(2)}, u32[]{:S(2)}) collective-permute-start(bf16[2,256,128]{2,1,0:T(8,128)(2,1)S(1)} %get-tuple-element.47.own_ref), channel_id=1, source_target_pairs={{0,16},{2,18},{4,20},{6,22},{8,24},{10,26},{12,28},{14,30},{16,0},... | collective-permute-start | bytes 393224 | tf_op jit(solution)/shard_map/ppermute | solution.py:37
  1.9 10.2 %collective-permute-start.6 = (bf16[2,256,128]{2,1,0:T(8,128)(2,1)S(1)}, bf16[2,256,128]{2,1,0:T(8,128)(2,1)S(1)}, u32[]{:S(2)}, u32[]{:S(2)}) collective-permute-start(bf16[2,256,128]{2,1,0:T(8,128)(2,1)S(1)} %get-tuple-element.47.own_ref), channel_id=1, source_target_pairs={{0,24},{2,26},{4,28},{6,30},{8,16},{10,18},{12,20},{14,22},{16,8},... | collective-permute-start | bytes 393224 | tf_op jit(solution)/shard_map/ppermute | solution.py:37
  5.3 15.1 %collective-permute-start.12 = (bf16[2,256,128]{2,1,0:T(8,128)(2,1)S(1)}, bf16[2,256,128]{2,1,0:T(8,128)(2,1)S(1)}, u32[]{:S(2)}, u32[]{:S(2)}) collective-permute-start(bf16[2,256,128]{2,1,0:T(8,128)(2,1)S(1)} %get-tuple-element.46.own_ref), channel_id=1, source_target_pairs={{0,8},{2,10},{4,12},{6,14},{8,0},{10,2},{12,4},{14,6},{16,24},{18,... | collective-permute-start | bytes 393224 | tf_op jit(solution)/shard_map/ppermute | solution.py:37
  5.3 11.9 %collective-permute-start.10 = (bf16[2,2,256,128]{3,2,1,0:T(8,128)(2,1)S(1)}, bf16[2,2,256,128]{3,2,1,0:T(8,128)(2,1)S(1)}, u32[]{:S(2)}, u32[]{:S(2)}) collective-permute-start(bf16[2,2,256,128]{3,2,1,0:T(8,128)(2,1)S(1)} %get-tuple-element.51), channel_id=1, source_target_pairs={{0,4},{2,6},{4,0},{6,2},{8,12},{10,14},{12,8},{14,10},{16,20},{18,... | collective-permute-start | bytes 786440 | tf_op jit(solution)/shard_map/ppermute | solution.py:37
  7.7 6.8 %collective-permute-start.3 = (bf16[1,2,256,128]{3,2,1,0:T(8,128)(2,1)S(1)}, bf16[1,2,256,128]{3,2,1,0:T(8,128)(2,1)S(1)}, u32[]{:S(2)}, u32[]{:S(2)}) collective-permute-start(bf16[1,2,256,128]{3,2,1,0:T(8,128)(2,1)S(1)} %bitcast.23), channel_id=1, source_target_pairs={{0,4},{2,6},{4,0},{6,2},{8,12},{10,14},{12,8},{14,10},{16,20},{18,... | collective-permute-start | bytes 393224 | tf_op jit(solution)/shard_map/ppermute | solution.py:37
  12.1 12.0 %collective-permute-start.13 = (bf16[2,256,128]{2,1,0:T(8,128)(2,1)S(1)}, bf16[2,256,128]{2,1,0:T(8,128)(2,1)S(1)}, u32[]{:S(2)}, u32[]{:S(2)}) collective-permute-start(bf16[2,256,128]{2,1,0:T(8,128)(2,1)S(1)} %get-tuple-element.46.own_ref), channel_id=1, source_target_pairs={{0,16},{2,18},{4,20},{6,22},{8,24},{10,26},{12,28},{14,30},{16,0},... | collective-permute-start | bytes 393224 | tf_op jit(solution)/shard_map/ppermute | solution.py:37
  12.1 16.4 %collective-permute-start.14 = (bf16[2,256,128]{2,1,0:T(8,128)(2,1)S(1)}, bf16[2,256,128]{2,1,0:T(8,128)(2,1)S(1)}, u32[]{:S(2)}, u32[]{:S(2)}) collective-permute-start(bf16[2,256,128]{2,1,0:T(8,128)(2,1)S(1)} %get-tuple-element.46.own_ref), channel_id=1, source_target_pairs={{0,24},{2,26},{4,28},{6,30},{8,16},{10,18},{12,20},{14,22},{16,8},... | collective-permute-start | bytes 393224 | tf_op jit(solution)/shard_map/ppermute | solution.py:37
  14.5 43.6 %collective-permute-start = (bf16[8,4096]{1,0:T(8,128)(2,1)S(1)}, bf16[8,4096]{1,0:T(8,128)(2,1)S(1)}, u32[]{:S(2)}, u32[]{:S(2)}) collective-permute-start(bf16[8,4096]{1,0:T(8,128)(2,1)S(1)} %get-tuple-element.43), channel_id=1, source_target_pairs={{0,2},{2,0},{4,6},{6,4},{8,10},{10,8},{12,14},{14,12},{16,18},{18,... | collective-permute-start | bytes 196616 | tf_op jit(solution)/shard_map/ppermute | solution.py:37
  17.2 40.9 %collective-permute-start.1 = (bf16[8,4096]{1,0:T(8,128)(2,1)S(1)}, bf16[8,4096]{1,0:T(8,128)(2,1)S(1)}, u32[]{:S(2)}, u32[]{:S(2)}) collective-permute-start(bf16[8,4096]{1,0:T(8,128)(2,1)S(1)} %get-tuple-element.42), channel_id=1, source_target_pairs={{2,4},{4,2},{6,8},{8,6},{10,12},{12,10},{14,16},{16,14},{18,20},{2... | collective-permute-start | bytes 196616 | tf_op jit(solution)/shard_map/ppermute | solution.py:30
  20.4 10.5 %collective-permute-start.7 = (bf16[2,2,256,128]{3,2,1,0:T(8,128)(2,1)S(1)}, bf16[2,2,256,128]{3,2,1,0:T(8,128)(2,1)S(1)}, u32[]{:S(2)}, u32[]{:S(2)}) collective-permute-start(bf16[2,2,256,128]{3,2,1,0:T(8,128)(2,1)S(1)} %pad_maximum_fusion.3.refs_4_), channel_id=1, source_target_pairs={{0,4},{2,6},{4,0},{6,2},{8,12},{10,14},{12,8},{14,10},{16,20},{18,... | collective-permute-start | bytes 786440 | tf_op jit(solution)/shard_map/ppermute | solution.py:37
  24.1 8.5 %collective-permute-start.11 = (bf16[2,2,2,256,128]{4,3,2,1,0:T(8,128)(2,1)S(1)}, bf16[2,2,2,256,128]{4,3,2,1,0:T(8,128)(2,1)S(1)}, u32[]{:S(2)}, u32[]{:S(2)}) collective-permute-start(bf16[2,2,2,256,128]{4,3,2,1,0:T(8,128)(2,1)S(1)} %pad_maximum_fusion), channel_id=1, source_target_pairs={{0,2},{2,0},{4,6},{6,4},{8,10},{10,8},{12,14},{14,12},{16,18},{18,... | collective-permute-start | bytes 1572872 | tf_op jit(solution)/shard_map/ppermute | solution.py:37
  28.5 1.9 %collective-permute-start.4 = (bf16[2,2,256,128]{3,2,1,0:T(8,128)(2,1)S(1)}, bf16[2,2,256,128]{3,2,1,0:T(8,128)(2,1)S(1)}, u32[]{:S(2)}, u32[]{:S(2)}) collective-permute-start(bf16[2,2,256,128]{3,2,1,0:T(8,128)(2,1)S(1)} %pad_maximum_fusion.2), channel_id=1, source_target_pairs={{0,2},{2,0},{4,6},{6,4},{8,10},{10,8},{12,14},{14,12},{16,18},{18,... | collective-permute-start | bytes 786440 | tf_op jit(solution)/shard_map/ppermute | solution.py:37
  30.5 7.8 %collective-permute-start.8 = (bf16[2,2,256,128]{3,2,1,0:T(8,128)(2,1)S(1)}, bf16[2,2,256,128]{3,2,1,0:T(8,128)(2,1)S(1)}, u32[]{:S(2)}, u32[]{:S(2)}) collective-permute-start(bf16[2,2,256,128]{3,2,1,0:T(8,128)(2,1)S(1)} %pad_maximum_fusion.3.refs_4_), channel_id=1, source_target_pairs={{0,2},{2,0},{4,6},{6,4},{8,10},{10,8},{12,14},{14,12},{16,18},{18,... | collective-permute-start | bytes 786440 | tf_op jit(solution)/shard_map/ppermute | solution.py:37
  30.9 7.8 %collective-permute-start.15 = (bf16[3,2,256,128]{3,2,1,0:T(8,128)(2,1)S(1)}, bf16[3,2,256,128]{3,2,1,0:T(8,128)(2,1)S(1)}, u32[]{:S(2)}, u32[]{:S(2)}) collective-permute-start(bf16[3,2,256,128]{3,2,1,0:T(8,128)(2,1)S(1)} %pad_maximum_fusion.1.refs_0_), channel_id=1, source_target_pairs={{0,4},{2,6},{4,0},{6,2},{8,12},{10,14},{12,8},{14,10},{16,20},{18,... | collective-permute-start | bytes 1179656 | tf_op jit(solution)/shard_map/ppermute | solution.py:37
  32.6 10.7 %collective-permute-start.9 = (bf16[2,2,256,128]{3,2,1,0:T(8,128)(2,1)S(1)}, bf16[2,2,256,128]{3,2,1,0:T(8,128)(2,1)S(1)}, u32[]{:S(2)}, u32[]{:S(2)}) collective-permute-start(bf16[2,2,256,128]{3,2,1,0:T(8,128)(2,1)S(1)} %collective-permute-done.7.refs_5_), channel_id=1, source_target_pairs={{0,2},{2,0},{4,6},{6,4},{8,10},{10,8},{12,14},{14,12},{16,18},{18,... | collective-permute-start | bytes 786440 | tf_op jit(solution)/shard_map/ppermute | solution.py:37
  38.3 24.1 %collective-permute-start.16 = (bf16[3,2,256,128]{3,2,1,0:T(8,128)(2,1)S(1)}, bf16[3,2,256,128]{3,2,1,0:T(8,128)(2,1)S(1)}, u32[]{:S(2)}, u32[]{:S(2)}) collective-permute-start(bf16[3,2,256,128]{3,2,1,0:T(8,128)(2,1)S(1)} %pad_maximum_fusion.1.refs_0_), channel_id=1, source_target_pairs={{0,2},{2,0},{4,6},{6,4},{8,10},{10,8},{12,14},{14,12},{16,18},{18,... | collective-permute-start | bytes 1179656 | tf_op jit(solution)/shard_map/ppermute | solution.py:37
  38.7 23.7 %collective-permute-start.17 = (bf16[3,2,256,128]{3,2,1,0:T(8,128)(2,1)S(1)}, bf16[3,2,256,128]{3,2,1,0:T(8,128)(2,1)S(1)}, u32[]{:S(2)}, u32[]{:S(2)}) collective-permute-start(bf16[3,2,256,128]{3,2,1,0:T(8,128)(2,1)S(1)} %collective-permute-done.15.refs_1_), channel_id=1, source_target_pairs={{0,2},{2,0},{4,6},{6,4},{8,10},{10,8},{12,14},{14,12},{16,18},{18,... | collective-permute-start | bytes 1179656 | tf_op jit(solution)/shard_map/ppermute | solution.py:37
  54.0 21.9 %collective-permute-start.18 = (bf16[256,1024]{1,0:T(8,128)(2,1)S(1)}, bf16[256,1024]{1,0:T(8,128)(2,1)S(1)}, u32[]{:S(2)}, u32[]{:S(2)}) collective-permute-start(bf16[256,1024]{1,0:T(8,128)(2,1)S(1)} %get-tuple-element.24.refs_4_), channel_id=1, source_target_pairs={{0,1},{1,0},{2,3},{3,2},{4,5},{5,4},{6,7},{7,6},{8,9},{9,8},{10,11... | collective-permute-start | bytes 1572872 | tf_op jit(solution)/shard_map/ppermute | solution.py:539
  68.3 15.4 %collective-permute-start.20 = (bf16[256,512]{1,0:T(8,128)(2,1)S(1)}, bf16[256,512]{1,0:T(8,128)(2,1)S(1)}, u32[]{:S(2)}, u32[]{:S(2)}) collective-permute-start(bf16[256,512]{1,0:T(8,128)(2,1)S(1)} %get-tuple-element.30.refs_1_), channel_id=1, source_target_pairs={{0,1},{1,0},{2,3},{3,2},{4,5},{5,4},{6,7},{7,6},{8,9},{9,8},{10,11... | collective-permute-start | bytes 786440 | tf_op jit(solution)/shard_map/ppermute | solution.py:539
  74.6 9.0 %collective-permute-start.19 = (bf16[256,512]{1,0:T(8,128)(2,1)S(1)}, bf16[256,512]{1,0:T(8,128)(2,1)S(1)}, u32[]{:S(2)}, u32[]{:S(2)}) collective-permute-start(bf16[256,512]{1,0:T(8,128)(2,1)S(1)} %get-tuple-element.29.refs_0_), channel_id=1, source_target_pairs={{0,1},{1,0},{2,3},{3,2},{4,5},{5,4},{6,7},{7,6},{8,9},{9,8},{10,11... | collective-permute-start | bytes 786440 | tf_op jit(solution)/shard_map/ppermute | solution.py:539
  87.6 5.7 %collective-permute-start.21 = (bf16[8,4096]{1,0:T(8,128)(2,1)S(1)}, bf16[8,4096]{1,0:T(8,128)(2,1)S(1)}, u32[]{:S(2)}, u32[]{:S(2)}) collective-permute-start(bf16[8,4096]{1,0:T(8,128)(2,1)S(1)} %get-tuple-element.40), channel_id=1, source_target_pairs={{0,2},{2,0},{4,6},{6,4},{8,10},{10,8},{12,14},{14,12},{16,18},{18,... | collective-permute-start | bytes 196616 | tf_op jit(solution)/shard_map/ppermute | solution.py:37
  88.4 6.3 %collective-permute-start.22 = (bf16[8,4096]{1,0:T(8,128)(2,1)S(1)}, bf16[8,4096]{1,0:T(8,128)(2,1)S(1)}, u32[]{:S(2)}, u32[]{:S(2)}) collective-permute-start(bf16[8,4096]{1,0:T(8,128)(2,1)S(1)} %get-tuple-element.41), channel_id=1, source_target_pairs={{2,4},{4,2},{6,8},{8,6},{10,12},{12,10},{14,16},{16,14},{18,20},{2... | collective-permute-start | bytes 196616 | tf_op jit(solution)/shard_map/ppermute | solution.py:30
  (4 other events, 11.4 us)
